TPU v7x, 32 devices: a whole 2x2x4 slice. The times are simulated.
32 devices in a mesh: seq: 8 (over z, y), tp: 4 (over x, core).
Axes of the slice: x: 2, y: 2, z: 4, core: 2. Of those that a mesh axis runs over, the one named last changes fastest.
Arguments:
- tokens: bfloat16 [8, 2048, 1024], P(None, 'seq'), may hold values from -6 to 6
- seg_ids: int32 [8, 2048], replicated, may hold values from 0 to 3, never falling along the last dimension, each value on 1 to 1024 neighbouring positions
- routed_index: int32 [8, 256], replicated, may hold values from 0 to 2047, as said below
- gain_attn: bfloat16 [1024], replicated, may hold values from 0.099609375 to 1.8984375
- w_qkv: bfloat16 [1024, 3, 1024], P(None, None, 'tp'), may hold values from -0.1875 to 0.1875
- w_out: bfloat16 [1024, 1024], P('tp'), may hold values from -0.375 to 0.375
- gain_mlp: bfloat16 [1024], replicated, may hold values from 0.099609375 to 1.8984375
- w_up: bfloat16 [1024, 4096], P(None, 'tp'), may hold values from -0.1875 to 0.1875
- w_down: bfloat16 [4096, 1024], P('tp'), may hold values from -0.09375 to 0.09375
- w_router: bfloat16 [1024], replicated, may hold values from -0.1875 to 0.1875
- out_grad: bfloat16 [8, 2048, 1024], P(None, 'seq'), may hold values from -6 to 6
Outputs:
- block_out: bfloat16 [8, 2048, 1024], P(None, 'seq')
- grad_tokens: float32 [8, 2048, 1024], P(None, 'seq')
- grad_gain_attn: float32 [1024], P('seq')
- grad_qkv: float32 [1024, 3, 1024], P('seq', None, 'tp')
- grad_out: float32 [1024, 1024], P('tp', 'seq')
- grad_gain_mlp: float32 [1024], P('seq')
- grad_up: float32 [1024, 4096], P('seq', 'tp')
- grad_down: float32 [4096, 1024], P('tp', 'seq')
- grad_router: float32 [1024], P('seq')
Inputs may be any that keep to these rules, and one draw needn't show every extreme that they name: `routed_index`: each row lists the 256 routed positions of one sequence, all different, in rising order. Cutting a sequence into blocks of 256 positions, the position of rank r lies in block r // 32 or in the block before it; some block holds 64 routed positions.
All inputs are finite; a program needn't handle non-finite values.
Results may differ from a plain program's by a relative error of at most 0.018.
Values may be sent and summed in bfloat16 or wider, within the bound.
No kernel may reach another device: no remote copies, remote signals or barrier semaphores. Data moves between devices by JAX's collectives and lax.ppermute only.
A program may use at most 384 MiB of HBM per device.

v0:
```python
import jax
import jax.numpy as jnp
from jax import lax
from jax.sharding import PartitionSpec as P

HEAD_DIM = 64


precise = lax.Precision.HIGHEST


def normed(values, gain):
    factor = lax.rsqrt(jnp.mean(values * values, axis=-1, keepdims=True) + 1e-05)
    return values * factor * gain


def gelu_tanh(values):
    return jax.nn.gelu(values, approximate=True)


def match_table(positions, usable, anchor, extent):
    offsets = jnp.arange(extent, dtype=jnp.int32)
    hits = (positions - anchor)[:, :, None] == offsets[None, None, :]
    return jnp.logical_and(hits, usable[:, :, None]).astype(jnp.bfloat16)


def compact(table, source):
    return jnp.einsum("sqc,scd->sqd", table, source, preferred_element_type=jnp.float32)


def spread(table, routed_rows):
    return jnp.einsum("sqc,sqd->scd", table, routed_rows, preferred_element_type=jnp.float32)


def on_device(
    tokens,
    seg_ids,
    routed_index,
    gain_attn,
    w_qkv,
    w_out,
    gain_mlp,
    w_up,
    w_down,
    w_router,
    out_grad,
):
    seq_count, group_len, model_width = tokens.shape
    routed_len = routed_index.shape[1]
    dev_count = lax.axis_size("seq")
    dev_index = lax.axis_index("seq")
    per_dev = routed_len // dev_count
    group_base = dev_index * group_len
    seg_routed = jnp.take_along_axis(seg_ids, routed_index, axis=1)
    capacity = 2 * per_dev
    slot_ids = jnp.arange(capacity, dtype=jnp.int32)
    first_rank = jnp.sum((routed_index < group_base).astype(jnp.int32), axis=1)
    group_count = (
        jnp.sum((routed_index < group_base + group_len).astype(jnp.int32), axis=1) - first_rank
    )
    query_rank = first_rank[:, None] + slot_ids[None, :]
    query_valid = slot_ids[None, :] < group_count[:, None]
    clipped = jnp.minimum(query_rank, routed_len - 1)
    query_pos = jnp.take_along_axis(routed_index, clipped, axis=1)
    own_table = match_table(query_pos, query_valid, group_base, group_len)
    routed_rows = compact(own_table, tokens).astype(jnp.bfloat16)
    routed_grads = compact(own_table, out_grad).astype(jnp.bfloat16)
    query_seg = jnp.take_along_axis(seg_routed, clipped, axis=1)
    bounds = jnp.arange(dev_count, dtype=jnp.int32) * group_len
    firsts = jnp.sum((routed_index[:, :, None] < bounds[None, None, :]).astype(jnp.int32), axis=1)
    next_firsts = jnp.concatenate(
        [firsts[:, 1:], jnp.full((seq_count, 1), routed_len, jnp.int32)], axis=1
    )
    key_rank = (firsts[:, :, None] + slot_ids[None, None, :]).reshape(seq_count, -1)
    key_valid = (slot_ids[None, None, :] < (next_firsts - firsts)[:, :, None]).reshape(
        seq_count, -1
    )
    key_seg = jnp.take_along_axis(seg_routed, jnp.minimum(key_rank, routed_len - 1), axis=1)
    allowed = jnp.logical_and(
        key_rank[:, None, :] <= query_rank[:, :, None], key_seg[:, None, :] == query_seg[:, :, None]
    )
    allowed = jnp.logical_and(allowed, key_valid[:, None, :])[:, None]
    rows_float = routed_rows.astype(jnp.float32)
    gain_first = gain_attn.astype(jnp.float32)
    gain_second = gain_mlp.astype(jnp.float32)
    router_score = jnp.einsum(
        "sqd,d->sq", routed_rows, w_router, preferred_element_type=jnp.float32
    )
    gating = jax.nn.sigmoid(router_score)
    attn_input = normed(rows_float, gain_first).astype(jnp.bfloat16)
    qkv_rows = jnp.einsum(
        "sqd,dch->sqch", attn_input, w_qkv, preferred_element_type=jnp.float32
    ).astype(jnp.bfloat16)
    query_count = qkv_rows.shape[1]
    head_count = qkv_rows.shape[3] // HEAD_DIM
    query_flat = qkv_rows[:, :, 0]
    queries = query_flat.reshape(seq_count, query_count, head_count, HEAD_DIM)
    key_pair = (qkv_rows[:, :, 1], qkv_rows[:, :, 2])
    all_keys = lax.all_gather(key_pair[0], "seq", axis=1, tiled=True)
    all_values = lax.all_gather(key_pair[1], "seq", axis=1, tiled=True)
    key_count = all_keys.shape[1]
    all_keys = all_keys.reshape(seq_count, key_count, head_count, HEAD_DIM)
    all_values = all_values.reshape(seq_count, key_count, head_count, HEAD_DIM)
    scaling = HEAD_DIM ** (-0.5)

    def masked_logits():
        raw_scores = jnp.einsum(
            "sqhe,skhe->shqk", queries, all_keys, preferred_element_type=jnp.float32
        )
        return jnp.where(allowed, raw_scores * scaling, -1e30)

    logits = masked_logits()
    row_peak = jnp.max(logits, axis=-1, keepdims=True)
    powered = jnp.exp(logits - row_peak)
    row_total = jnp.sum(powered, axis=-1, keepdims=True)
    log_total = row_peak + jnp.log(row_total)
    probs_low = (powered / row_total).astype(jnp.bfloat16)
    mixed = jnp.einsum("shqk,skhe->sqhe", probs_low, all_values, preferred_element_type=jnp.float32)
    mixed = mixed.reshape(seq_count, query_count, -1).astype(jnp.bfloat16)
    attn_out = lax.psum(
        jnp.einsum("sqh,hd->sqd", mixed, w_out, preferred_element_type=jnp.float32).astype(
            jnp.bfloat16
        ),
        "tp",
    ).astype(jnp.float32)
    residual = rows_float + attn_out
    mlp_input = normed(residual, gain_second).astype(jnp.bfloat16)
    pre_act = jnp.einsum("sqd,df->sqf", mlp_input, w_up, preferred_element_type=jnp.float32)
    hidden = gelu_tanh(pre_act).astype(jnp.bfloat16)
    mlp_out = lax.psum(
        jnp.einsum("sqf,fd->sqd", hidden, w_down, preferred_element_type=jnp.float32).astype(
            jnp.bfloat16
        ),
        "tp",
    ).astype(jnp.float32)
    branch = attn_out + mlp_out
    update_rows = (gating[:, :, None] * branch).astype(jnp.bfloat16)
    block_out = (tokens.astype(jnp.float32) + spread(own_table, update_rows)).astype(jnp.bfloat16)
    grad_rows = routed_grads.astype(jnp.float32)
    scaled_grad = gating[:, :, None] * grad_rows
    grad_score = jnp.sum(grad_rows * branch, axis=-1) * gating * (1.0 - gating)
    grad_mlp = scaled_grad.astype(jnp.bfloat16)
    grad_down = jnp.einsum("sqf,sqd->fd", hidden, grad_mlp, preferred_element_type=jnp.float32)
    grad_hidden = jnp.einsum("sqd,fd->sqf", grad_mlp, w_down, preferred_element_type=jnp.float32)
    gelu_pull = jax.vjp(gelu_tanh, pre_act)[1]
    grad_pre = gelu_pull(grad_hidden)[0].astype(jnp.bfloat16)
    grad_up = jnp.einsum("sqd,sqf->df", mlp_input, grad_pre, preferred_element_type=jnp.float32)
    grad_mlp_input = lax.psum(
        jnp.einsum("sqf,df->sqd", grad_pre, w_up, preferred_element_type=jnp.float32).astype(
            jnp.bfloat16
        ),
        "tp",
    ).astype(jnp.float32)
    second_pull = jax.vjp(normed, residual, gain_second)[1]
    grad_residual, grad_gain_mlp = second_pull(grad_mlp_input)
    grad_attn = (grad_residual + scaled_grad).astype(jnp.bfloat16)
    grad_out = jnp.einsum("sqh,sqd->hd", mixed, grad_attn, preferred_element_type=jnp.float32)
    grad_mixed_flat = jnp.einsum(
        "sqd,hd->sqh", grad_attn, w_out, preferred_element_type=jnp.float32
    ).astype(jnp.bfloat16)
    grad_mixed = grad_mixed_flat.reshape(seq_count, query_count, head_count, HEAD_DIM)
    probs_again = jnp.where(allowed, jnp.exp(masked_logits() - log_total), 0.0)
    grad_probs = jnp.einsum(
        "sqhe,skhe->shqk", grad_mixed, all_values, preferred_element_type=jnp.float32
    )
    inner_sum = jnp.sum(probs_again * grad_probs, axis=-1, keepdims=True)
    grad_raw = (probs_again * (grad_probs - inner_sum) * scaling).astype(jnp.bfloat16)
    grad_query = jnp.einsum(
        "shqk,skhe->sqhe", grad_raw, all_keys, preferred_element_type=jnp.float32
    )
    grad_query = grad_query.reshape(seq_count, query_count, -1).astype(jnp.bfloat16)
    probs_again_low = probs_again.astype(jnp.bfloat16)
    key_part = jnp.einsum(
        "shqk,sqhe->skhe", grad_raw, queries, preferred_element_type=jnp.float32
    ).reshape(seq_count, key_count, -1)
    value_part = jnp.einsum(
        "shqk,sqhe->skhe", probs_again_low, grad_mixed, preferred_element_type=jnp.float32
    ).reshape(seq_count, key_count, -1)
    key_pair = (key_part, value_part)
    grad_keys = lax.psum_scatter(key_pair[0], "seq", scatter_dimension=1, tiled=True)
    grad_values = lax.psum_scatter(key_pair[1], "seq", scatter_dimension=1, tiled=True)
    grad_qkv_rows = jnp.stack(
        [grad_query, grad_keys.astype(jnp.bfloat16), grad_values.astype(jnp.bfloat16)], axis=2
    )
    grad_qkv = jnp.einsum(
        "sqd,sqch->dch", attn_input, grad_qkv_rows, preferred_element_type=jnp.float32
    )
    grad_attn_input = lax.psum(
        jnp.einsum(
            "sqch,dch->sqd", grad_qkv_rows, w_qkv, preferred_element_type=jnp.float32
        ).astype(jnp.bfloat16),
        "tp",
    ).astype(jnp.float32)
    first_pull = jax.vjp(normed, rows_float, gain_first)[1]
    grad_norm, grad_gain_attn = first_pull(grad_attn_input)
    grad_router = jnp.einsum("sq,sqd->d", grad_score, rows_float, precision=precise)
    grad_routed_in = (
        grad_residual + grad_norm + grad_score[:, :, None] * w_router.astype(jnp.float32)
    ).astype(jnp.bfloat16)
    grad_tokens = out_grad.astype(jnp.float32) + spread(own_table, grad_routed_in)
    reduced = (
        lax.psum_scatter(grad_gain_attn, "seq", scatter_dimension=0, tiled=True),
        lax.psum_scatter(grad_qkv, "seq", scatter_dimension=0, tiled=True),
        lax.psum_scatter(grad_out, "seq", scatter_dimension=1, tiled=True),
        lax.psum_scatter(grad_gain_mlp, "seq", scatter_dimension=0, tiled=True),
        lax.psum_scatter(grad_up, "seq", scatter_dimension=0, tiled=True),
        lax.psum_scatter(grad_down, "seq", scatter_dimension=1, tiled=True),
        lax.psum_scatter(grad_router, "seq", scatter_dimension=0, tiled=True),
    )
    return (block_out, grad_tokens) + tuple(reduced)


def solution(mesh):
    return jax.shard_map(
        on_device,
        mesh=mesh,
        in_specs=(
            P(None, "seq", None),
            P(),
            P(),
            P(),
            P(None, None, "tp"),
            P("tp", None),
            P(),
            P(None, "tp"),
            P("tp", None),
            P(),
            P(None, "seq", None),
        ),
        out_specs=(
            P(None, "seq", None),
            P(None, "seq", None),
            P("seq"),
            P("seq", None, "tp"),
            P("tp", "seq"),
            P("seq"),
            P("seq", "tp"),
            P("tp", "seq"),
            P("seq"),
        ),
        check_vma=False,
    )
```

profile of v0, /device:TPU:0, one launch (start us, length us, event | category | flops | bytes accessed | tf_op | source)
XLA Modules:
  0.0 843.0 jit_solution(11866250530468293948)
XLA Ops:
  8.8 14.0 %gather_fusion = s32[2048]{0:T(1024)S(1)} fusion(s32[8,2048]{1,0:T(8,128)} %param.14, s32[2048]{0:T(1024)S(1)} %bitcast.118), kind=kCustom, calls=%fused_computation.2 | custom fusion | bytes 32768 | tf_op jit(solution)/shard_map/jit(take_along_axis)/gather | solution.py:54
  23.2 3.6 gather_fusion.2
  26.8 3.6 gather_fusion.3
  30.6 3.3 fusion.34
  37.4 25.5 %gather_fusion.1 = s32[4096]{0:T(1024)S(1)} fusion(s32[8,256]{1,0:T(8,128)S(1)} %get-tuple-element.27, s32[4096]{0:T(1024)S(1)} %bitcast.117), kind=kCustom, calls=%fused_computation.3 | custom fusion | bytes 65536 | tf_op jit(solution)/shard_map/jit(take_along_axis)/gather | solution.py:78
  64.9 22.9 %all-gather.7.cloned.1.call-done = bf16[8,512,1,256]{3,1,2,0:T(8,128)(2,1)} async-done(((bf16[8,64,1,256]{3,1,2,0:T(8,128)(2,1)}), bf16[8,512,1,256]{3,1,2,0:T(8,128)(2,1)}) %all-gather.7.cloned.1.call-update) | async-done | bytes 2097168 | tf_op jit(solution)/shard_map/all_gather | solution.py:99
  87.8 3.9 copy.59
  91.7 2.7 fusion.5
  94.5 2.0 copy-done.3
  96.5 1.4 fusion.2
  97.9 40.3 %all-gather.5.cloned.1.call-done = bf16[8,512,1,256]{3,1,2,0:T(8,128)(2,1)} async-done(((bf16[8,64,1,256]{3,1,2,0:T(8,128)(2,1)}), bf16[8,512,1,256]{3,1,2,0:T(8,128)(2,1)}) %all-gather.5.cloned.1.call-update) | async-done | bytes 2097168 | tf_op jit(solution)/shard_map/all_gather | solution.py:100
  138.2 3.9 copy.58
  142.1 4.5 fusion.63
  147.4 1.5 convolution_convert_fusion.2
  149.5 4.1 convolution_convert_fusion
  153.6 30.3 %all-reduce.10.cloned.1.call-done = bf16[8,64,1024]{2,1,0:T(8,128)(2,1)} async-done(((bf16[8,64,1024]{2,1,0:T(8,128)(2,1)}), bf16[8,64,1024]{2,1,0:T(8,128)(2,1)}) %all-reduce.10.cloned.1.call-update) | async-done | bytes 1048592 | tf_op jit(solution)/shard_map/psum | solution.py:120
  183.9 1.7 multiply_reduce_fusion.1
  185.6 2.9 fusion.42
  188.6 2.4 fusion.57
  191.0 2.4 fusion.30
  194.4 2.3 fusion.54
  197.0 51.8 %all-reduce.14.cloned.1.call-done = (bf16[8,64,1024]{2,1,0:T(8,128)(2,1)}, bf16[8,64,1024]{2,1,0:T(8,128)(2,1)}) async-done(((bf16[8,64,1024]{2,1,0:T(8,128)(2,1)}, bf16[8,64,1024]{2,1,0:T(8,128)(2,1)}), (bf16[8,64,1024]{2,1,0:T(8,128)(2,1)}, bf16[8,64,1024]{2,1,0:T(8,128)(2,1)})) %all-reduce.14.cloned.1.call-update) | async-done | bytes 2097168 | tf_op jit(solution)/shard_map/psum | solution.py:130
  248.8 3.6 fusion.22
  255.1 4.4 fusion.125
  259.5 19.0 %fusion.13 = f32[8,4,64,512]{3,2,1,0:T(8,128)} fusion(bf16[8,64,4,64]{1,3,2,0:T(8,128)(2,1)S(1)} %bitcast.128, f32[8,4,64,512]{3,2,1,0:T(8,128)} %fusion.125, f32[8,4,64,512]{3,2,1,0:T(8,128)} %copy-done.3, f32[8,4,64]{2,1,0:T(4,128)S(1)} %bitcast.133, pred[8,64,512]{2,1,0:T(8,128)(4,1)S(1)} %and_and_fusion), kind=kOutput, calls=%fused_computation.38 | convolution fusion | flops 147851776 | bytes 13115392 | tf_op jit(solution)/shard_map/shqk,sqhe->skhe/dot_general | solution.py:173
  278.5 5.3 copy.64
  283.9 5.7 fusion.44
  289.6 5.4 copy.66
  295.3 18.4 %fusion.64 = bf16[8,4,64,64]{3,2,1,0:T(8,128)(2,1)S(1)} fusion(bf16[8,512,4,64]{1,3,2,0:T(8,128)(2,1)} %bitcast.121, f32[8,4,64,512]{3,2,1,0:T(8,128)} %fusion.125, f32[8,4,64,512]{3,2,1,0:T(8,128)} %copy-done.3, f32[8,4,64]{2,1,0:T(4,128)S(1)} %bitcast.135, pred[8,64,512]{2,1,0:T(8,128)(4,1)S(1)} %and_and_fusion), kind=kOutput, calls=%fused_computation.90 | convolution fusion | flops 147982848 | bytes 11018240 | tf_op jit(solution)/shard_map/shqk,skhe->sqhe/dot_general | solution.py:168
  313.9 58.4 %reduce-scatter.7.cloned.1.call-done = f32[8,64,256]{2,1,0:T(8,128)} async-done(((f32[8,512,256]{2,1,0:T(8,128)}), f32[8,64,256]{2,1,0:T(8,128)}) %reduce-scatter.7.cloned.1.call-update) | async-done | bytes 524304 | tf_op jit(solution)/shard_map/reduce_scatter | solution.py:180
  372.4 1.1 convert_bitcast_fusion.1
  373.4 90.4 %reduce-scatter.9.cloned.1.call-done = f32[8,64,256]{2,1,0:T(8,128)} async-done(((f32[8,512,256]{2,1,0:T(8,128)}), f32[8,64,256]{2,1,0:T(8,128)}) %reduce-scatter.9.cloned.1.call-update) | async-done | bytes 524304 | tf_op jit(solution)/shard_map/reduce_scatter | solution.py:181
  463.8 1.1 convert_bitcast_fusion
  464.9 3.5 bitcast_convert_fusion
  468.5 2.9 convolution_bitcast_fusion.3
  471.5 5.1 convolution_bitcast_fusion
  476.7 1.1 copy-done.27
  477.9 3.4 convolution_bitcast_fusion.1
  482.3 2.9 convolution_bitcast_fusion.2
  487.7 4.7 add_convert_fusion
  492.4 12.1 %all-reduce.12.cloned.1.call-done = bf16[8,64,1024]{2,1,0:T(8,128)(2,1)} async-done(((bf16[8,64,1024]{2,1,0:T(8,128)(2,1)}), bf16[8,64,1024]{2,1,0:T(8,128)(2,1)}) %all-reduce.12.cloned.1.call-update) | async-done | bytes 1048592 | tf_op jit(solution)/shard_map/psum | solution.py:188
  504.5 2.2 fusion.23
  506.7 37.3 %all-reduce.4 = (f32[1024]{0:T(1024)S(1)}, f32[1024]{0:T(1024)S(1)}, f32[1024]{0:T(1024)S(1)}) all-reduce(f32[1024]{0:T(1024)S(1)} %get-tuple-element.12, f32[1024]{0:T(1024)S(1)} %get-tuple-element.10, f32[1024]{0:T(1024)S(1)} %bitcast.140), channel_id=6, replica_groups=mesh['seq'=8,'tp'=4] {'seq'}, use_global_device_ids=true, to_apply=%region_18.20.clone | all-reduce | flops 3072 | bytes 24576
  545.8 9.2 %convert_add_fusion = f32[8,256,1024]{2,1,0:T(8,128)} fusion(bf16[8,256,1024]{2,1,0:T(8,128)(2,1)} %param.23, bf16[8,64,1024]{2,1,0:T(8,128)(2,1)} %all-reduce.12.cloned.1.call-done, bf16[8,64,1024]{2,1,0:T(8,128)(2,1)S(1)} %get-tuple-element.32, bf16[8,64,1024]{2,1,0:T(8,128)(2,1)} %all-reduce.10.cloned.1.call-done, ...), kind=kOutput, calls=%fused_computation.5 | convolution fusion | flops 282853376 | bytes 16802304 | tf_op jit(solution)/shard_map/sqc,sqd->scd/dot_general | solution.py:32
  554.9 18.8 %reduce-scatter.13.cloned.1.call-done = f32[256,128]{1,0:T(8,128)} async-done(((f32[256,1024]{1,0:T(8,128)}), f32[256,128]{1,0:T(8,128)}) %reduce-scatter.13.cloned.1.call-update) | async-done | bytes 131088 | tf_op jit(solution)/shard_map/reduce_scatter | solution.py:204
  573.7 91.9 %reduce-scatter.17.cloned.1.call-done = f32[1024,128]{1,0:T(8,128)} async-done(((f32[1024,1024]{1,0:T(8,128)}), f32[1024,128]{1,0:T(8,128)}) %reduce-scatter.17.cloned.1.call-update) | async-done | bytes 524304 | tf_op jit(solution)/shard_map/reduce_scatter | solution.py:207
  665.6 92.0 %reduce-scatter.15.cloned.1.call-done = f32[128,1024]{1,0:T(8,128)} async-done(((f32[1024,1024]{1,0:T(8,128)}), f32[128,1024]{1,0:T(8,128)}) %reduce-scatter.15.cloned.1.call-update) | async-done | bytes 524304 | tf_op jit(solution)/shard_map/reduce_scatter | solution.py:206
  757.6 78.6 %reduce-scatter.11.cloned.1.call-done = f32[128,3,256]{2,0,1:T(8,128)} async-done(((f32[1024,3,256]{2,0,1:T(8,128)}), f32[128,3,256]{2,0,1:T(8,128)}) %reduce-scatter.11.cloned.1.call-update) | async-done | bytes 393232 | tf_op jit(solution)/shard_map/reduce_scatter | solution.py:203
  (128 shorter events, 18.2 us)
Async XLA Ops:
  7.2 181.4 %copy-start = (bf16[1024,1024]{1,0:T(8,128)(2,1)S(1)}, bf16[1024,1024]{1,0:T(8,128)(2,1)}, u32[]{:S(2)}) copy-start(bf16[1024,1024]{1,0:T(8,128)(2,1)} %param.21) | copy-start | bytes 6291460
  7.2 80.6 %all-gather.7.cloned.1.call-start = ((), (), s32[]{:S(2)}) async-start(), calls=%async_computation.15 | async-start | bytes 2359296 | tf_op jit(solution)/shard_map/all_gather | solution.py:99
  8.8 14.0 %copy-start.2 = (s32[8,256]{1,0:T(8,128)S(1)}, s32[8,256]{1,0:T(8,128)}, u32[]{:S(2)}) copy-start(s32[8,256]{1,0:T(8,128)} %param.15) | copy-start | bytes 24580
  30.6 3.3 copy-start.23
  35.0 2.3 copy-start.21
  35.0 2.3 copy-start.20
  35.9 102.4 %all-gather.5.cloned.1.call-start = ((), (), s32[]{:S(2)}) async-start(), calls=%async_computation.14 | async-start | bytes 2359296 | tf_op jit(solution)/shard_map/all_gather | solution.py:100
  36.6 147.3 %all-reduce.10.cloned.1.call-start = ((), (), s32[]{:S(2)}) async-start(), calls=%async_computation.6 | async-start | bytes 2097152 | tf_op jit(solution)/shard_map/psum | solution.py:120
  94.5 2.0 copy-start.3
  142.1 5.3 copy-start.13
  146.6 0.8 copy-start.15
  148.9 99.9 %all-reduce.14.cloned.1.call-start = ((), (), s32[]{:S(2)}) async-start(), calls=%async_computation.16 | async-start | bytes 4194304 | tf_op jit(solution)/shard_map/psum | solution.py:130
  183.9 1.7 copy-start.4
  188.6 2.5 copy-start.25
  188.6 2.5 copy-start.7
  191.0 3.4 copy-start.22
  193.4 1.0 copy-start.26
  196.7 52.1 %copy-start.5 = (bf16[8,64,1024]{2,1,0:T(8,128)(2,1)S(1)}, bf16[8,64,1024]{2,1,0:T(8,128)(2,1)}, u32[]{:S(2)}) copy-start(bf16[8,64,1024]{2,1,0:T(8,128)(2,1)} %all-reduce.10.cloned.1.call-done) | copy-start | bytes 3145732
  196.8 175.6 %reduce-scatter.7.cloned.1.call-start = ((), (), s32[]{:S(2)}) async-start(), calls=%async_computation.7 | async-start | bytes 4718592 | tf_op jit(solution)/shard_map/reduce_scatter | solution.py:180
  248.8 3.6 copy-start.6
  248.8 3.6 copy-start.8
  252.4 1.9 copy-start.14
  253.3 1.0 copy-start.12
  255.1 4.4 copy-start.11
  283.8 180.0 %reduce-scatter.9.cloned.1.call-start = ((), (), s32[]{:S(2)}) async-start(), calls=%async_computation.8 | async-start | bytes 4718592 | tf_op jit(solution)/shard_map/reduce_scatter | solution.py:181
  295.1 209.4 %all-reduce.12.cloned.1.call-start = ((), (), s32[]{:S(2)}) async-start(), calls=%async_computation.9 | async-start | bytes 2097152 | tf_op jit(solution)/shard_map/psum | solution.py:188
  373.4 95.0 %copy-start.16 = (bf16[8,64,1,256]{3,1,2,0:T(8,128)(2,1)}, bf16[8,64,1,256]{3,1,2,0:T(8,128)(2,1)S(1)}, u32[]{:S(2)}) copy-start(bf16[8,64,1,256]{3,1,2,0:T(8,128)(2,1)S(1)} %convert_bitcast_fusion.1) | copy-start | bytes 786436
  464.9 3.5 copy-start.18
  468.4 3.1 copy-start.9
  468.4 105.3 %reduce-scatter.13.cloned.1.call-start = ((), (), s32[]{:S(2)}) async-start(), calls=%async_computation.11 | async-start | bytes 1179648 | tf_op jit(solution)/shard_map/reduce_scatter | solution.py:204
  471.4 194.2 %reduce-scatter.17.cloned.1.call-start = ((), (), s32[]{:S(2)}) async-start(), calls=%async_computation.13 | async-start | bytes 4718592 | tf_op jit(solution)/shard_map/reduce_scatter | solution.py:207
  476.6 1.2 copy-start.27
  476.7 281.0 %reduce-scatter.15.cloned.1.call-start = ((), (), s32[]{:S(2)}) async-start(), calls=%async_computation.12 | async-start | bytes 4718592 | tf_op jit(solution)/shard_map/reduce_scatter | solution.py:206
  481.3 1.0 copy-start.17
  481.3 1.0 copy-start.19
  481.3 354.9 %reduce-scatter.11.cloned.1.call-start = ((), (), s32[]{:S(2)}) async-start(), calls=%async_computation.10 | async-start | bytes 3538944 | tf_op jit(solution)/shard_map/reduce_scatter | solution.py:203
  485.2 0.7 copy-start.24
  485.2 2.5 copy-start.10
  545.8 290.5 %copy-start.1 = (bf16[1024,1024]{1,0:T(8,128)(2,1)S(1)}, bf16[1024,1024]{1,0:T(8,128)(2,1)}, u32[]{:S(2)}) copy-start(bf16[1024,1024]{1,0:T(8,128)(2,1)} %param.21) | copy-start | bytes 6291460
Sparse Core Ops, SparseCore 0:
  36.0 51.7 all-gather.6
  90.6 47.5 all-gather.4
  149.0 34.8 all-reduce.9
  196.9 51.8 all-reduce.13
  284.0 88.3 reduce-scatter.6
  375.8 87.9 reduce-scatter.8
  468.5 35.8 all-reduce.11
  508.5 65.1 reduce-scatter.12
  577.9 87.6 reduce-scatter.16
  669.7 87.9 reduce-scatter.14
  761.8 74.3 reduce-scatter.10
where the time goes:
time: 851 us; the launch traced here: 843 us
  waiting for transfers between devices  588 us (69%)
  matrix products  108 us (13%)
  local copies, waits for them, and re-layouts  78 us (9%)
  blocking collectives  37.3 us (4%)
  between operations  15.2 us (2%)
  other arithmetic  14.6 us (2%)
    reduce_scatter x1, waiting for transfers between devices, on_device(): lax.psum_scatter(grad_up, 'seq', scatter_dimension=0, tiled=True)  92 us
    reduce_scatter x1, waiting for transfers between devices, on_device(): lax.psum_scatter(grad_down, 'seq', scatter_dimension=1, tiled=True)  91.9 us
    reduce_scatter x1, waiting for transfers between devices, on_device(): lax.psum_scatter(key_pair[1], 'seq', scatter_dimension=1, tiled=True)  90.4 us
    reduce_scatter x1, waiting for transfers between devices, on_device(): lax.psum_scatter(grad_qkv, 'seq', scatter_dimension=0, tiled=True)  78.6 us
    reduce_scatter x1, waiting for transfers between devices, on_device(): lax.psum_scatter(key_pair[0], 'seq', scatter_dimension=1, tiled=True)  58.4 us
    psum x1, waiting for transfers between devices, on_device(): lax.psum(jnp.einsum('sqf,fd->sqd', hidden, w_down, preferred_element_type...  51.8 us
    all_gather x1, waiting for transfers between devices, on_device(): all_values = lax.all_gather(key_pair[1], 'seq', axis=1, tiled=True)  40.3 us
    unnamed x1, blocking collectives  37.3 us
  transfers between devices with their start and end apart: 11, of which 11 were waited for; matrix products, arithmetic and copies ran while one was open for 12% of the time, Pallas kernels for 0%

commit v1 on v0

--- a/solution.py
+++ b/solution.py
@@ -32,7 +32,7 @@
     return jnp.einsum("sqc,sqd->scd", table, routed_rows, preferred_element_type=jnp.float32)
 
 
-def on_device(
+def on_device_split(
     tokens,
     seg_ids,
     routed_index,
@@ -210,7 +210,259 @@
     return (block_out, grad_tokens) + tuple(reduced)
 
 
+def ring_order(size):
+    return list(range(0, size, 2)) + list(range(size - 1, 0, -2))
+
+
+def ring_permute(values, order, step):
+    size = len(order)
+    pairs = [(order[i], order[(i + step) % size]) for i in range(size)]
+    return lax.ppermute(values, "seq", pairs)
+
+
+def ring_scatter(parts, direction):
+    size = parts.shape[0]
+    order = ring_order(size)
+    place = [order.index(i) for i in range(size)]
+    table = [
+        [order[(place[i] - direction * (1 + k)) % size] for k in range(size)] for i in range(size)
+    ]
+    mine = jnp.asarray(table, dtype=jnp.int32)[lax.axis_index("seq")]
+    total = lax.dynamic_index_in_dim(parts, mine[0], 0, False)
+    for k in range(1, size):
+        moved = ring_permute(total, order, direction)
+        own = lax.dynamic_index_in_dim(parts, mine[k], 0, False)
+        total = moved.astype(jnp.float32) + own.astype(jnp.float32)
+        if k < size - 1:
+            total = total.astype(jnp.bfloat16)
+    return total
+
+
+def tp_permute(values, mask):
+    size = lax.axis_size("tp")
+    return lax.ppermute(values, "tp", [(i, i ^ mask) for i in range(size)])
+
+
+def pick_half(values, which):
+    width = values.shape[-1] // 2
+    return jnp.where(which == 0, values[..., :width], values[..., width:])
+
+
+def join_halves(own, other, which):
+    return jnp.where(
+        which == 0,
+        jnp.concatenate([own, other], axis=-1),
+        jnp.concatenate([other, own], axis=-1),
+    )
+
+
+def tp_sum(partial, which):
+    narrow = partial.astype(jnp.bfloat16)
+    moved = tp_permute(pick_half(narrow, 1 - which), 1)
+    half = pick_half(partial, which) + moved.astype(jnp.float32)
+    half = half.astype(jnp.bfloat16)
+    moved = tp_permute(half, 2)
+    half = (half.astype(jnp.float32) + moved.astype(jnp.float32)).astype(jnp.bfloat16)
+    return join_halves(half, tp_permute(half, 1), which).astype(jnp.float32)
+
+
+def to_owners(rows, share):
+    groups = rows.reshape(-1, share, rows.shape[-1])
+    later = jnp.concatenate([groups[1:], jnp.zeros_like(groups[:1])], axis=0)
+    return jnp.concatenate([groups, later], axis=1)
+
+
+def from_owners(slots, share):
+    later = jnp.concatenate([jnp.zeros_like(slots[:1, share:]), slots[:-1, share:]], axis=0)
+    return (slots[:, :share] + later).reshape(-1, slots.shape[-1])
+
+
+def on_device_whole(
+    tokens,
+    seg_ids,
+    routed_index,
+    gain_attn,
+    w_qkv,
+    w_out,
+    gain_mlp,
+    w_up,
+    w_down,
+    w_router,
+    out_grad,
+):
+    f32, bf16 = jnp.float32, jnp.bfloat16
+    seq_count, group_len, model_width = tokens.shape
+    routed_len = routed_index.shape[1]
+    dev_count = lax.axis_size("seq")
+    dev_index = lax.axis_index("seq")
+    core = lax.axis_index("tp") % 2
+    share = routed_len // dev_count
+    half_width = model_width // 2
+
+    padded_index = jnp.concatenate(
+        [routed_index, jnp.full((seq_count, share), -1, jnp.int32)], axis=1
+    )
+    slots = lax.dynamic_slice(padded_index, (0, dev_index * share), (seq_count, 2 * share))
+    offsets = jnp.arange(group_len, dtype=jnp.int32)
+    table = ((slots - dev_index * group_len)[:, :, None] == offsets).astype(bf16)
+
+    index_row = lax.dynamic_index_in_dim(routed_index, dev_index, 0, False)
+    seg_row = lax.dynamic_index_in_dim(seg_ids, dev_index, 0, False)
+    seg_routed = sum(
+        (index_row >= jnp.sum((seg_row < t).astype(jnp.int32))).astype(jnp.int32)
+        for t in range(1, 4)
+    )
+    ranks = jnp.arange(routed_len, dtype=jnp.int32)
+    allowed = jnp.logical_and(
+        ranks[None, :] <= ranks[:, None], seg_routed[None, :] == seg_routed[:, None]
+    )[None]
+
+    def fetch(source):
+        own = lax.dynamic_slice_in_dim(source, core * half_width, half_width, 2)
+        return compact(table, own).astype(bf16)
+
+    sent = jnp.concatenate([fetch(tokens), fetch(out_grad)], axis=-1)
+    got = lax.all_to_all(sent, "seq", 0, 0, tiled=True)
+    got = from_owners(got, share)
+    other = tp_permute(got, 1)
+    routed_rows = join_halves(got[:, :half_width], other[:, :half_width], core)
+    routed_grads = join_halves(got[:, half_width:], other[:, half_width:], core)
+
+    rows = routed_rows.astype(f32)
+    grad_rows = routed_grads.astype(f32)
+    gain_first = gain_attn.astype(f32)
+    gain_second = gain_mlp.astype(f32)
+    router = w_router.astype(f32)
+    gating = jax.nn.sigmoid(jnp.sum(rows * router, axis=-1, keepdims=True))
+    factor_first = lax.rsqrt(jnp.mean(rows * rows, axis=-1, keepdims=True) + 1e-05)
+    attn_input = (rows * factor_first * gain_first).astype(bf16)
+    weights = jnp.transpose(w_qkv, (1, 0, 2))
+    qkv = jnp.einsum("rd,cdh->crh", attn_input, weights, preferred_element_type=f32).astype(bf16)
+    head_count = qkv.shape[2] // HEAD_DIM
+    scaling = HEAD_DIM ** (-0.5)
+
+    def heads(values):
+        return values.reshape(routed_len, head_count, HEAD_DIM)
+
+    queries, keys, values = heads(qkv[0]), heads(qkv[1]), heads(qkv[2])
+    raw = jnp.einsum("qhe,khe->hqk", queries, keys, preferred_element_type=f32)
+    logits = jnp.where(allowed, raw * scaling, -1e30)
+    powered = jnp.exp(logits - jnp.max(logits, axis=-1, keepdims=True))
+    probs = powered / jnp.sum(powered, axis=-1, keepdims=True)
+    probs_low = probs.astype(bf16)
+    mixed = jnp.einsum("hqk,khe->qhe", probs_low, values, preferred_element_type=f32)
+    mixed = mixed.reshape(routed_len, -1).astype(bf16)
+    attn_out = tp_sum(jnp.dot(mixed, w_out, preferred_element_type=f32), core)
+
+    residual = rows + attn_out
+    factor_second = lax.rsqrt(jnp.mean(residual * residual, axis=-1, keepdims=True) + 1e-05)
+    mlp_input = (residual * factor_second * gain_second).astype(bf16)
+    scaled_grad = gating * grad_rows
+    grad_mlp = scaled_grad.astype(bf16)
+    pre_act = jnp.dot(mlp_input, w_up, preferred_element_type=f32)
+    hidden, gelu_pull = jax.vjp(gelu_tanh, pre_act)
+    hidden = hidden.astype(bf16)
+    grad_hidden = lax.dot_general(
+        grad_mlp, w_down, (((1,), (1,)), ((), ())), preferred_element_type=f32
+    )
+    grad_pre = gelu_pull(grad_hidden)[0].astype(bf16)
+    grad_mlp_input = tp_sum(
+        lax.dot_general(grad_pre, w_up, (((1,), (1,)), ((), ())), preferred_element_type=f32), core
+    )
+    mlp_out = tp_sum(jnp.dot(hidden, w_down, preferred_element_type=f32), core)
+
+    def outer(left, right):
+        product = lax.dot_general(
+            left, right, (((0,), (0,)), ((), ())), preferred_element_type=f32
+        )
+        return product.astype(bf16).reshape(dev_count, -1, right.shape[1])
+
+    grad_up = ring_scatter(outer(mlp_input, grad_pre), 1)
+    grad_down = ring_scatter(outer(grad_mlp, hidden), -1).T
+
+    weighted = grad_mlp_input * gain_second
+    grad_residual = factor_second * weighted - residual * factor_second**3 * jnp.mean(
+        residual * weighted, axis=-1, keepdims=True
+    )
+    grad_gain_mlp = jnp.sum(grad_mlp_input * residual * factor_second, axis=0)
+    grad_attn = (grad_residual + scaled_grad).astype(bf16)
+    grad_mixed = lax.dot_general(
+        grad_attn, w_out, (((1,), (1,)), ((), ())), preferred_element_type=f32
+    ).astype(bf16)
+    grad_heads = heads(grad_mixed)
+    grad_probs = jnp.einsum("qhe,khe->hqk", grad_heads, values, preferred_element_type=f32)
+    inner_sum = jnp.sum(probs * grad_probs, axis=-1, keepdims=True)
+    grad_raw = (probs * (grad_probs - inner_sum) * scaling).astype(bf16)
+
+    def flat(products):
+        return products.reshape(routed_len, -1).astype(bf16)
+
+    grad_query = flat(jnp.einsum("hqk,khe->qhe", grad_raw, keys, preferred_element_type=f32))
+    grad_key = flat(jnp.einsum("hqk,qhe->khe", grad_raw, queries, preferred_element_type=f32))
+    grad_value = flat(jnp.einsum("hqk,qhe->khe", probs_low, grad_heads, preferred_element_type=f32))
+    grad_parts = (grad_query, grad_key, grad_value)
+    grad_attn_input = tp_sum(
+        sum(
+            lax.dot_general(
+                grad_parts[c], weights[c], (((1,), (1,)), ((), ())), preferred_element_type=f32
+            )
+            for c in range(3)
+        ),
+        core,
+    )
+    forth = jnp.concatenate([outer(attn_input, grad_query), outer(attn_input, grad_key)], axis=-1)
+    back = jnp.concatenate([outer(attn_input, grad_value), outer(grad_attn, mixed)], axis=-1)
+    forth = ring_scatter(forth, 1)
+    back = ring_scatter(back, -1)
+    width = grad_query.shape[1]
+    grad_qkv = jnp.stack([forth[:, :width], forth[:, width:], back[:, :width]], axis=1)
+    grad_out = back[:, width:].T
+
+    branch = attn_out + mlp_out
+    update = (gating * branch).astype(bf16)
+    grad_score = gating * (1.0 - gating) * jnp.sum(grad_rows * branch, axis=-1, keepdims=True)
+    weighted = grad_attn_input * gain_first
+    grad_norm = factor_first * weighted - rows * factor_first**3 * jnp.mean(
+        rows * weighted, axis=-1, keepdims=True
+    )
+    grad_gain_attn = jnp.sum(grad_attn_input * rows * factor_first, axis=0)
+    grad_router = jnp.sum(grad_score * rows, axis=0)
+    grad_routed_in = (grad_residual + grad_norm + grad_score * router).astype(bf16)
+
+    small = jnp.stack([grad_gain_attn, grad_gain_mlp, grad_router]).astype(bf16)
+    small = small.reshape(3, dev_count, -1).transpose(1, 0, 2)
+    small = jnp.pad(small, ((0, 0), (0, 13), (0, half_width - small.shape[2])))
+    sent = to_owners(pick_half(update, core), share)
+    got_update = lax.all_to_all(sent, "seq", 0, 0, tiled=True)
+    sent = jnp.concatenate([to_owners(pick_half(grad_routed_in, core), share), small], axis=1)
+    got = lax.all_to_all(sent, "seq", 0, 0, tiled=True)
+    small = jnp.sum(got[:, 2 * share : 2 * share + 3, : model_width // dev_count].astype(f32), axis=0)
+    got_grad = got[:, : 2 * share]
+    block_rows = join_halves(got_update, tp_permute(got_update, 1), core)
+    grad_slots = join_halves(got_grad, tp_permute(got_grad, 1), core)
+    block_out = (tokens.astype(f32) + spread(table, block_rows)).astype(bf16)
+    grad_tokens = out_grad.astype(f32) + spread(table, grad_slots)
+    return (
+        block_out,
+        grad_tokens,
+        small[0],
+        grad_qkv,
+        grad_out,
+        small[1],
+        grad_up,
+        grad_down,
+        small[2],
+    )
+
+
 def solution(mesh):
+    def on_device(*arrays):
+        seq_count, routed_len = arrays[2].shape
+        dev_count = mesh.shape["seq"]
+        whole = seq_count == dev_count and mesh.shape["tp"] == 4 and dev_count % 2 == 0
+        body = on_device_whole if whole else on_device_split
+        return body(*arrays)
+
     return jax.shard_map(
         on_device,
         mesh=mesh,

time: 851 us -> 278 us (0.33)
  waiting for transfers between devices: 588 us -> 70 us
  matrix products: 108 us -> 47.8 us
  local copies, waits for them, and re-layouts: 78 us -> 21.3 us
  starting transfers between devices: 1.61 us -> 54.9 us
  blocking collectives: 37.3 us -> 0 us
  other arithmetic: 14.6 us -> 47.3 us
  between operations: 15.2 us -> 31.9 us
    reduce_scatter x6 -> x0, waiting for transfers between devices: 430 us -> none  [the longest x1 92 us: on_device(): lax.psum_scatter(grad_up, 'seq', scatter_dimension=0, tiled=True)]
    psum x3 -> x0, waiting for transfers between devices: 94.2 us -> none  [the longest x1 51.8 us: on_device(): lax.psum(jnp.einsum('sqf,fd->sqd', hidden, w_down, preferred_element_type...]
    all_gather x2 -> x0, waiting for transfers between devices: 63.2 us -> none  [the longest x1 40.3 us: on_device(): all_values = lax.all_gather(key_pair[1], 'seq', axis=1, tiled=True)]
    dot_general x20 -> x21, matrix products: 86.8 us -> 30.2 us  [the longest x6 7.45 us: outer(): lax.dot_general(left, right, (((0,), (0,)), ((), ())), preferred_element_...]
    gather x9 -> x0, local copies, waits for them, and re-layouts: 46.9 us -> none  [the longest x2 25.5 us: on_device(): jnp.take_along_axis(seg_routed, jnp.minimum(key_rank, routed_len - 1), ax...]
    ppermute x0 -> x43, starting transfers between devices: none -> 38.7 us  [the longest x28 31.1 us: ring_permute(): return lax.ppermute(values, 'seq', pairs)]
    ppermute x0 -> x43, waiting for transfers between devices: none -> 38.2 us  [the longest x28 20.2 us: ring_permute(): return lax.ppermute(values, 'seq', pairs)]
    unnamed x1 -> x0, blocking collectives: 37.3 us -> none
  transfers between devices with their start and end apart: 11 -> 46, of which waited for: 11 -> 16; matrix products, arithmetic and copies ran while one was open for 12% -> 29% of each run, Pallas kernels for 0% -> 0%
where the time goes in v1:
time: 278 us; the launch traced here: 273 us
  waiting for transfers between devices  70 us (25%)
  starting transfers between devices  54.9 us (20%)
  matrix products  47.8 us (17%)
  other arithmetic  47.3 us (17%)
  between operations  31.9 us (11%)
  local copies, waits for them, and re-layouts  21.3 us (8%)
    all_to_all x2, waiting for transfers between devices, on_device_whole(): got = lax.all_to_all(sent, 'seq', 0, 0, tiled=True)  31.8 us
    ppermute x28, starting transfers between devices, ring_permute(): return lax.ppermute(values, 'seq', pairs)  31.1 us
    ppermute x28, waiting for transfers between devices, ring_permute(): return lax.ppermute(values, 'seq', pairs)  20.2 us
    ppermute x15, waiting for transfers between devices, tp_permute(): return lax.ppermute(values, 'tp', [(i, i ^ mask) for i in range(size)])  18 us
    convert_element_type x24, other arithmetic, ring_scatter(): total = total.astype(jnp.bfloat16)  15.9 us
    all_to_all x2, starting transfers between devices, on_device_whole(): got = lax.all_to_all(sent, 'seq', 0, 0, tiled=True)  12 us
    dot_general x2, matrix products, spread(): jnp.einsum('sqc,sqd->scd', table, routed_rows, preferred_element_type=jnp...  11.8 us
    unnamed x127, local copies, waits for them, and re-layouts  8.99 us
  transfers between devices with their start and end apart: 46, of which 16 were waited for; matrix products, arithmetic and copies ran while one was open for 29% of the time, Pallas kernels for 0%

profile of v1, /device:TPU:0, one launch (start us, length us, event | category | flops | bytes accessed | tf_op | source)
XLA Modules:
  0.0 273.2 jit_solution(15818292859874346152)
XLA Ops:
  1.6 2.1 fusion.19
  3.7 2.1 fusion.16
  6.9 7.4 %all-to-all-start = ((bf16[8,64,1024]{2,1,0:T(8,128)(2,1)}), bf16[8,64,1024]{2,1,0:T(8,128)(2,1)S(1)}, u32[]{:S(2)}, u32[]{:S(2)}) async-start(bf16[8,64,1024]{2,1,0:T(8,128)(2,1)} %pad_maximum_fusion), calls=%async_computation | async-start | bytes 2097152 | tf_op jit(solution)/shard_map/all_to_all | solution.py:325
  15.9 24.2 %all-to-all-done = bf16[8,64,1024]{2,1,0:T(8,128)(2,1)S(1)} async-done(((bf16[8,64,1024]{2,1,0:T(8,128)(2,1)}), bf16[8,64,1024]{2,1,0:T(8,128)(2,1)S(1)}, u32[]{:S(2)}, u32[]{:S(2)}) %all-to-all-start) | async-done | bytes 1048608 | tf_op jit(solution)/shard_map/all_to_all | solution.py:325
  41.0 2.6 fusion.149
  43.8 1.9 fusion.167
  49.7 1.7 convolution_convert_fusion.11
  55.3 7.1 %collective-permute-done.2 = bf16[256,512]{1,0:T(8,128)(2,1)S(1)} collective-permute-done((bf16[256,512]{1,0:T(8,128)(2,1)S(1)}, bf16[256,512]{1,0:T(8,128)(2,1)S(1)}, u32[]{:S(2)}, u32[]{:S(2)}) %collective-permute-start.2) | collective-permute-done | bytes 262176 | tf_op jit(solution)/shard_map/ppermute | solution.py:243
  70.7 6.9 %collective-permute-done.5 = bf16[256,512]{1,0:T(8,128)(2,1)S(1)} collective-permute-done((bf16[256,512]{1,0:T(8,128)(2,1)S(1)}, bf16[256,512]{1,0:T(8,128)(2,1)S(1)}, u32[]{:S(2)}, u32[]{:S(2)}) %collective-permute-start.5) | collective-permute-done | bytes 262176 | tf_op jit(solution)/shard_map/ppermute | solution.py:243
  109.8 1.8 fusion.35
  112.9 3.7 %fusion.44 = bf16[256,1024]{1,0:T(8,128)(2,1)} fusion(f32[256,1024]{1,0:T(8,128)} %copy-done.56, bf16[1024,1024]{1,0:T(8,128)(2,1)S(1)} %copy-done, f32[256]{0:T(256)S(1)} %get-tuple-element.37, bf16[256,512]{1,0:T(8,128)(2,1)} %get-tuple-element.46, bf16[256,512]{1,0:T(8,128)(2,1)} %get-tuple-element.48, pred[]{:T(512)S(6)} %eq.25), kind=kOutput, calls=%fused_computation.108 | convolution fusion | flops 545259520 | bytes 4195329 | tf_op jit(solution)/shard_map/dot_general | solution.py:365
  116.7 2.3 convolution_convert_fusion
  121.1 4.1 %all-to-all-start.1 = ((bf16[8,64,512]{2,1,0:T(8,128)(2,1)}), bf16[8,64,512]{2,1,0:T(8,128)(2,1)}, u32[]{:S(2)}, u32[]{:S(2)}) async-start(bf16[8,64,512]{2,1,0:T(8,128)(2,1)} %fusion.73), calls=%async_computation.1 | async-start | bytes 1048576 | tf_op jit(solution)/shard_map/all_to_all | solution.py:436
  125.3 2.6 constant_dynamic-slice_fusion.7
  128.7 1.9 collective-permute-start.36
  130.6 2.5 fusion.174
  136.8 1.8 copy.72
  138.6 1.8 copy.71
  146.7 1.7 collective-permute-start.37
  148.4 3.2 %collective-permute-done.29 = bf16[128,1024]{1,0:T(8,128)(2,1)S(1)} collective-permute-done((bf16[128,1024]{1,0:T(8,128)(2,1)}, bf16[128,1024]{1,0:T(8,128)(2,1)S(1)}, u32[]{:S(2)}, u32[]{:S(2)}) %collective-permute-start.29) | collective-permute-done | bytes 262176 | tf_op jit(solution)/shard_map/ppermute | solution.py:220
  153.1 1.7 collective-permute-done.37
  155.6 1.7 collective-permute-start.38
  157.3 3.2 %collective-permute-done.30 = bf16[128,1024]{1,0:T(8,128)(2,1)S(1)} collective-permute-done((bf16[128,1024]{1,0:T(8,128)(2,1)S(1)}, bf16[128,1024]{1,0:T(8,128)(2,1)S(1)}, u32[]{:S(2)}, u32[]{:S(2)}) %collective-permute-start.30) | collective-permute-done | bytes 262176 | tf_op jit(solution)/shard_map/ppermute | solution.py:220
  160.6 1.7 fusion.94
  165.7 1.7 convolution_convert_fusion.7
  168.7 2.8 %convolution_convert_fusion.9 = bf16[4,64,256]{2,1,0:T(8,128)(2,1)} fusion(bf16[256,4,64]{0,2,1:T(8,128)(2,1)} %bitcast.246, f32[4,256,256]{1,2,0:T(8,128)S(1)} %fusion.176, f32[4,256,256]{1,2,0:T(8,128)} %get-tuple-element.81, f32[4,256]{1,0:T(4,128)} %copy-done.58), kind=kOutput, calls=%fused_computation.89 | convolution fusion | flops 35456256 | bytes 2363392 | tf_op jit(solution)/shard_map/hqk,khe->qhe/dot_general | solution.py:400
  171.5 2.7 convolution_convert_fusion.8
  174.6 1.7 fusion.87
  176.3 1.7 collective-permute-start.39
  182.8 2.1 convolution_convert_fusion.4
  191.5 1.8 fusion.93
  195.0 1.8 collective-permute-start.23
  199.1 1.6 collective-permute-done.23
  200.7 1.7 collective-permute-start.40
  202.5 2.5 collective-permute-done.16
  211.3 1.7 collective-permute-start.33
  213.5 1.8 collective-permute-start.18
  215.3 2.7 %collective-permute-done.25 = bf16[128,512]{0,1:T(8,128)(2,1)S(1)} collective-permute-done((bf16[128,512]{0,1:T(8,128)(2,1)S(1)}, bf16[128,512]{0,1:T(8,128)(2,1)S(1)}, u32[]{:S(2)}, u32[]{:S(2)}) %collective-permute-start.25) | collective-permute-done | bytes 131104 | tf_op jit(solution)/shard_map/ppermute | solution.py:220
  218.4 2.8 %collective-permute-done.18 = bf16[128,512]{0,1:T(8,128)(2,1)S(1)} collective-permute-done((bf16[128,512]{0,1:T(8,128)(2,1)S(1)}, bf16[128,512]{0,1:T(8,128)(2,1)S(1)}, u32[]{:S(2)}, u32[]{:S(2)}) %collective-permute-start.18) | collective-permute-done | bytes 131104 | tf_op jit(solution)/shard_map/ppermute | solution.py:220
  223.5 1.7 fusion.91
  226.7 4.7 %add_convert_fusion = bf16[8,256,1024]{2,1,0:T(8,128)(2,1)} fusion(bf16[8,256,1024]{2,1,0:T(8,128)(2,1)S(1)} %copy-done.2, bf16[8,64,512]{2,1,0:T(8,128)(2,1)S(1)} %collective-permute-done.7, bf16[8,64,512]{2,1,0:T(8,128)(2,1)} %all-to-all-done.1, pred[]{:T(512)S(6)} %eq.25, s32[8,64]{1,0:T(8,128)S(1)} %fusion.146), kind=kOutput, calls=%fused_computation.3 | convolution fusion | flops 279576576 | bytes 9439233 | tf_op jit(solution)/shard_map/sqc,sqd->scd/dot_general | solution.py:32
  235.1 2.2 collective-permute-done.27
  242.9 4.6 %all-to-all-start.2 = ((bf16[8,80,512]{2,1,0:T(8,128)(2,1)}), bf16[8,80,512]{2,1,0:T(8,128)(2,1)S(1)}, u32[]{:S(2)}, u32[]{:S(2)}) async-start(bf16[8,80,512]{2,1,0:T(8,128)(2,1)} %fusion.72), calls=%async_computation.2 | async-start | bytes 1310720 | tf_op jit(solution)/shard_map/all_to_all | solution.py:438
  248.6 2.1 collective-permute-start.35
  254.2 1.8 fusion.83
  256.0 7.6 %all-to-all-done.2 = bf16[8,80,512]{2,1,0:T(8,128)(2,1)S(1)} async-done(((bf16[8,80,512]{2,1,0:T(8,128)(2,1)}), bf16[8,80,512]{2,1,0:T(8,128)(2,1)S(1)}, u32[]{:S(2)}, u32[]{:S(2)}) %all-to-all-start.2) | async-done | bytes 655392 | tf_op jit(solution)/shard_map/all_to_all | solution.py:438
  263.7 1.8 convert_add_fusion.10
  266.1 7.1 %convert_add_fusion = f32[8,256,1024]{2,1,0:T(8,128)} fusion(bf16[8,256,1024]{2,1,0:T(8,128)(2,1)} %param.25, bf16[8,64,512]{2,1,0:T(8,128)(2,1)S(1)} %collective-permute-done.14, bf16[8,64,512]{2,1,0:T(8,128)(2,1)S(1)} %slice.374, pred[]{:T(512)S(6)} %eq.25, s32[8,64]{1,0:T(8,128)S(1)} %fusion.146), kind=kOutput, calls=%fused_computation.2 | convolution fusion | flops 277479424 | bytes 13633537 | tf_op jit(solution)/shard_map/sqc,sqd->scd/dot_general | solution.py:32
  (289 shorter events, 84.6 us)
Async XLA Ops:
  0.6 65.8 %copy-start = (bf16[1024,1024]{1,0:T(8,128)(2,1)S(1)}, bf16[1024,1024]{1,0:T(8,128)(2,1)}, u32[]{:S(2)}) copy-start(bf16[1024,1024]{1,0:T(8,128)(2,1)} %param.23) | copy-start | bytes 6291460
  6.9 36.7 %copy-start.53 = (bf16[1024]{0:T(1024)(128)(2,1)S(1)}, bf16[1024]{0:T(1024)(128)(2,1)}, u32[]{:S(2)}) copy-start(bf16[1024]{0:T(1024)(128)(2,1)} %param.18) | copy-start | bytes 6148
  6.9 33.2 %all-to-all-start = ((bf16[8,64,1024]{2,1,0:T(8,128)(2,1)}), bf16[8,64,1024]{2,1,0:T(8,128)(2,1)S(1)}, u32[]{:S(2)}, u32[]{:S(2)}) async-start(bf16[8,64,1024]{2,1,0:T(8,128)(2,1)} %pad_maximum_fusion), calls=%async_computation | async-start | bytes 2097152 | tf_op jit(solution)/shard_map/all_to_all | solution.py:325
  41.0 4.7 %collective-permute-start = (bf16[256,1024]{1,0:T(8,128)(2,1)}, bf16[256,1024]{1,0:T(8,128)(2,1)S(1)}, u32[]{:S(2)}, u32[]{:S(2)}) collective-permute-start(bf16[256,1024]{1,0:T(8,128)(2,1)} %bitcast), channel_id=1, source_target_pairs={{0,1},{1,0},{2,3},{3,2},{4,5},{5,4},{6,7},{7,6},{8,9},{9,8},{10,11... | collective-permute-start | bytes 1572872 | tf_op jit(solution)/shard_map/ppermute | solution.py:243
  51.9 1.7 collective-permute-start.1
  53.7 8.7 %collective-permute-start.2 = (bf16[256,512]{1,0:T(8,128)(2,1)S(1)}, bf16[256,512]{1,0:T(8,128)(2,1)S(1)}, u32[]{:S(2)}, u32[]{:S(2)}) collective-permute-start(bf16[256,512]{1,0:T(8,128)(2,1)S(1)} %fusion.82), channel_id=1, source_target_pairs={{0,2},{1,3},{2,0},{3,1},{4,6},{5,7},{6,4},{7,5},{8,10},{9,11},{10,... | collective-permute-start | bytes 786440 | tf_op jit(solution)/shard_map/ppermute | solution.py:243
  62.4 1.6 collective-permute-start.3
  67.4 1.6 collective-permute-start.4
  69.2 8.4 %collective-permute-start.5 = (bf16[256,512]{1,0:T(8,128)(2,1)S(1)}, bf16[256,512]{1,0:T(8,128)(2,1)S(1)}, u32[]{:S(2)}, u32[]{:S(2)}) collective-permute-start(bf16[256,512]{1,0:T(8,128)(2,1)S(1)} %fusion.80), channel_id=1, source_target_pairs={{0,2},{1,3},{2,0},{3,1},{4,6},{5,7},{6,4},{7,5},{8,10},{9,11},{10,... | collective-permute-start | bytes 786440 | tf_op jit(solution)/shard_map/ppermute | solution.py:243
  77.7 32.2 %collective-permute-start.6 = (bf16[256,512]{1,0:T(8,128)(2,1)S(1)}, bf16[256,512]{1,0:T(8,128)(2,1)}, u32[]{:S(2)}, u32[]{:S(2)}) collective-permute-start(bf16[256,512]{1,0:T(8,128)(2,1)S(1)} %add_convert_fusion.3), channel_id=1, source_target_pairs={{0,1},{1,0},{2,3},{3,2},{4,5},{5,4},{6,7},{7,6},{8,9},{9,8},{10,11... | collective-permute-start | bytes 786440 | tf_op jit(solution)/shard_map/ppermute | solution.py:243
  121.1 73.5 %all-to-all-start.1 = ((bf16[8,64,512]{2,1,0:T(8,128)(2,1)}), bf16[8,64,512]{2,1,0:T(8,128)(2,1)}, u32[]{:S(2)}, u32[]{:S(2)}) async-start(bf16[8,64,512]{2,1,0:T(8,128)(2,1)} %fusion.73), calls=%async_computation.1 | async-start | bytes 1048576 | tf_op jit(solution)/shard_map/all_to_all | solution.py:436
  128.7 17.0 %collective-permute-start.36 = (bf16[128,1024]{0,1:T(8,128)(2,1)}, bf16[128,1024]{0,1:T(8,128)(2,1)}, u32[]{:S(2)}, u32[]{:S(2)}) collective-permute-start(bf16[128,1024]{0,1:T(8,128)(2,1)} %bitcast.84), channel_id=1, source_target_pairs={{0,4},{8,0},{16,8},{24,16},{28,24},{20,28},{12,20},{4,12},{1,5},{9... | collective-permute-start | bytes 786440 | tf_op jit(solution)/shard_map/ppermute | solution.py:220
  133.8 9.2 %collective-permute-start.8 = (bf16[256,512]{1,0:T(8,128)(2,1)}, bf16[256,512]{1,0:T(8,128)(2,1)}, u32[]{:S(2)}, u32[]{:S(2)}) collective-permute-start(bf16[256,512]{1,0:T(8,128)(2,1)} %slice_select_fusion.6), channel_id=1, source_target_pairs={{0,1},{1,0},{2,3},{3,2},{4,5},{5,4},{6,7},{7,6},{8,9},{9,8},{10,11... | collective-permute-start | bytes 786440 | tf_op jit(solution)/shard_map/ppermute | solution.py:243
  142.6 9.0 %collective-permute-start.29 = (bf16[128,1024]{1,0:T(8,128)(2,1)}, bf16[128,1024]{1,0:T(8,128)(2,1)S(1)}, u32[]{:S(2)}, u32[]{:S(2)}) collective-permute-start(bf16[128,1024]{1,0:T(8,128)(2,1)} %dynamic-slice_bitcast_fusion), channel_id=1, source_target_pairs={{0,8},{8,16},{16,24},{24,28},{28,20},{20,12},{12,4},{4,0},{1,9},{9... | collective-permute-start | bytes 786440 | tf_op jit(solution)/shard_map/ppermute | solution.py:220
  144.1 8.8 %collective-permute-start.9 = (bf16[256,512]{1,0:T(8,128)(2,1)S(1)}, bf16[256,512]{1,0:T(8,128)(2,1)S(1)}, u32[]{:S(2)}, u32[]{:S(2)}) collective-permute-start(bf16[256,512]{1,0:T(8,128)(2,1)S(1)} %fusion.78), channel_id=1, source_target_pairs={{0,2},{1,3},{2,0},{3,1},{4,6},{5,7},{6,4},{7,5},{8,10},{9,11},{10,... | collective-permute-start | bytes 786440 | tf_op jit(solution)/shard_map/ppermute | solution.py:243
  146.7 8.1 %collective-permute-start.37 = (bf16[128,1024]{0,1:T(8,128)(2,1)S(1)}, bf16[128,1024]{0,1:T(8,128)(2,1)S(1)}, u32[]{:S(2)}, u32[]{:S(2)}) collective-permute-start(bf16[128,1024]{0,1:T(8,128)(2,1)S(1)} %fusion.89), channel_id=1, source_target_pairs={{0,4},{8,0},{16,8},{24,16},{28,24},{20,28},{12,20},{4,12},{1,5},{9... | collective-permute-start | bytes 786440 | tf_op jit(solution)/shard_map/ppermute | solution.py:220
  152.6 7.9 %collective-permute-start.30 = (bf16[128,1024]{1,0:T(8,128)(2,1)S(1)}, bf16[128,1024]{1,0:T(8,128)(2,1)S(1)}, u32[]{:S(2)}, u32[]{:S(2)}) collective-permute-start(bf16[128,1024]{1,0:T(8,128)(2,1)S(1)} %fusion.95), channel_id=1, source_target_pairs={{0,8},{8,16},{16,24},{24,28},{28,20},{20,12},{12,4},{4,0},{1,9},{9... | collective-permute-start | bytes 786440 | tf_op jit(solution)/shard_map/ppermute | solution.py:220
  153.1 9.5 %collective-permute-start.10 = (bf16[256,512]{1,0:T(8,128)(2,1)S(1)}, bf16[256,512]{1,0:T(8,128)(2,1)S(1)}, u32[]{:S(2)}, u32[]{:S(2)}) collective-permute-start(bf16[256,512]{1,0:T(8,128)(2,1)S(1)} %add_convert_fusion.2), channel_id=1, source_target_pairs={{0,1},{1,0},{2,3},{3,2},{4,5},{5,4},{6,7},{7,6},{8,9},{9,8},{10,11... | collective-permute-start | bytes 786440 | tf_op jit(solution)/shard_map/ppermute | solution.py:243
  155.6 19.0 %collective-permute-start.38 = (bf16[128,1024]{0,1:T(8,128)(2,1)}, bf16[128,1024]{0,1:T(8,128)(2,1)}, u32[]{:S(2)}, u32[]{:S(2)}) collective-permute-start(bf16[128,1024]{0,1:T(8,128)(2,1)} %fusion.88), channel_id=1, source_target_pairs={{0,4},{8,0},{16,8},{24,16},{28,24},{20,28},{12,20},{4,12},{1,5},{9... | collective-permute-start | bytes 786440 | tf_op jit(solution)/shard_map/ppermute | solution.py:220
  162.3 29.2 %collective-permute-start.31 = (bf16[128,1024]{1,0:T(8,128)(2,1)}, bf16[128,1024]{1,0:T(8,128)(2,1)}, u32[]{:S(2)}, u32[]{:S(2)}) collective-permute-start(bf16[128,1024]{1,0:T(8,128)(2,1)} %fusion.94), channel_id=1, source_target_pairs={{0,8},{8,16},{16,24},{24,28},{28,20},{20,12},{12,4},{4,0},{1,9},{9... | collective-permute-start | bytes 786440 | tf_op jit(solution)/shard_map/ppermute | solution.py:220
  176.3 21.4 %collective-permute-start.39 = (bf16[128,1024]{0,1:T(8,128)(2,1)}, bf16[128,1024]{0,1:T(8,128)(2,1)}, u32[]{:S(2)}, u32[]{:S(2)}) collective-permute-start(bf16[128,1024]{0,1:T(8,128)(2,1)} %fusion.87), channel_id=1, source_target_pairs={{0,4},{8,0},{16,8},{24,16},{28,24},{20,28},{12,20},{4,12},{1,5},{9... | collective-permute-start | bytes 786440 | tf_op jit(solution)/shard_map/ppermute | solution.py:220
  179.7 14.9 %collective-permute-start.22 = (bf16[128,512]{0,1:T(8,128)(2,1)}, bf16[128,512]{0,1:T(8,128)(2,1)S(1)}, u32[]{:S(2)}, u32[]{:S(2)}) collective-permute-start(bf16[128,512]{0,1:T(8,128)(2,1)} %fusion.140), channel_id=1, source_target_pairs={{0,4},{8,0},{16,8},{24,16},{28,24},{20,28},{12,20},{4,12},{1,5},{9... | collective-permute-start | bytes 393224 | tf_op jit(solution)/shard_map/ppermute | solution.py:220
  187.0 8.0 %collective-permute-start.15 = (bf16[128,512]{0,1:T(8,128)(2,1)}, bf16[128,512]{0,1:T(8,128)(2,1)}, u32[]{:S(2)}, u32[]{:S(2)}) collective-permute-start(bf16[128,512]{0,1:T(8,128)(2,1)} %fusion.139), channel_id=1, source_target_pairs={{0,8},{8,16},{16,24},{24,28},{28,20},{20,12},{12,4},{4,0},{1,9},{9... | collective-permute-start | bytes 393224 | tf_op jit(solution)/shard_map/ppermute | solution.py:220
  191.5 15.1 %collective-permute-start.11 = (bf16[256,512]{1,0:T(8,128)(2,1)}, bf16[256,512]{1,0:T(8,128)(2,1)}, u32[]{:S(2)}, u32[]{:S(2)}) collective-permute-start(bf16[256,512]{1,0:T(8,128)(2,1)} %slice_select_fusion.5), channel_id=1, source_target_pairs={{0,1},{1,0},{2,3},{3,2},{4,5},{5,4},{6,7},{7,6},{8,9},{9,8},{10,11... | collective-permute-start | bytes 786440 | tf_op jit(solution)/shard_map/ppermute | solution.py:243
  193.3 15.2 %collective-permute-start.32 = (bf16[128,1024]{1,0:T(8,128)(2,1)}, bf16[128,1024]{1,0:T(8,128)(2,1)}, u32[]{:S(2)}, u32[]{:S(2)}) collective-permute-start(bf16[128,1024]{1,0:T(8,128)(2,1)} %fusion.93), channel_id=1, source_target_pairs={{0,8},{8,16},{16,24},{24,28},{28,20},{20,12},{12,4},{4,0},{1,9},{9... | collective-permute-start | bytes 786440 | tf_op jit(solution)/shard_map/ppermute | solution.py:220
  194.6 30.6 %collective-permute-start.7 = (bf16[8,64,512]{2,1,0:T(8,128)(2,1)}, bf16[8,64,512]{2,1,0:T(8,128)(2,1)S(1)}, u32[]{:S(2)}, u32[]{:S(2)}) collective-permute-start(bf16[8,64,512]{2,1,0:T(8,128)(2,1)} %all-to-all-done.1), channel_id=1, source_target_pairs={{0,1},{1,0},{2,3},{3,2},{4,5},{5,4},{6,7},{7,6},{8,9},{9,8},{10,11... | collective-permute-start | bytes 1572872 | tf_op jit(solution)/shard_map/ppermute | solution.py:243
  195.0 5.7 %collective-permute-start.23 = (bf16[128,512]{0,1:T(8,128)(2,1)S(1)}, bf16[128,512]{0,1:T(8,128)(2,1)S(1)}, u32[]{:S(2)}, u32[]{:S(2)}) collective-permute-start(bf16[128,512]{0,1:T(8,128)(2,1)S(1)} %fusion.104), channel_id=1, source_target_pairs={{0,4},{8,0},{16,8},{24,16},{28,24},{20,28},{12,20},{4,12},{1,5},{9... | collective-permute-start | bytes 393224 | tf_op jit(solution)/shard_map/ppermute | solution.py:220
  197.7 7.3 %collective-permute-start.16 = (bf16[128,512]{0,1:T(8,128)(2,1)S(1)}, bf16[128,512]{0,1:T(8,128)(2,1)S(1)}, u32[]{:S(2)}, u32[]{:S(2)}) collective-permute-start(bf16[128,512]{0,1:T(8,128)(2,1)S(1)} %fusion.110), channel_id=1, source_target_pairs={{0,8},{8,16},{16,24},{24,28},{28,20},{20,12},{12,4},{4,0},{1,9},{9... | collective-permute-start | bytes 393224 | tf_op jit(solution)/shard_map/ppermute | solution.py:220
  200.7 12.7 %collective-permute-start.40 = (bf16[128,1024]{0,1:T(8,128)(2,1)S(1)}, bf16[128,1024]{0,1:T(8,128)(2,1)S(1)}, u32[]{:S(2)}, u32[]{:S(2)}) collective-permute-start(bf16[128,1024]{0,1:T(8,128)(2,1)S(1)} %fusion.86), channel_id=1, source_target_pairs={{0,4},{8,0},{16,8},{24,16},{28,24},{20,28},{12,20},{4,12},{1,5},{9... | collective-permute-start | bytes 786440 | tf_op jit(solution)/shard_map/ppermute | solution.py:220
  205.0 6.2 %collective-permute-start.24 = (bf16[128,512]{0,1:T(8,128)(2,1)S(1)}, bf16[128,512]{0,1:T(8,128)(2,1)S(1)}, u32[]{:S(2)}, u32[]{:S(2)}) collective-permute-start(bf16[128,512]{0,1:T(8,128)(2,1)S(1)} %fusion.103), channel_id=1, source_target_pairs={{0,4},{8,0},{16,8},{24,16},{28,24},{20,28},{12,20},{4,12},{1,5},{9... | collective-permute-start | bytes 393224 | tf_op jit(solution)/shard_map/ppermute | solution.py:220
  206.6 6.5 %collective-permute-start.17 = (bf16[128,512]{0,1:T(8,128)(2,1)S(1)}, bf16[128,512]{0,1:T(8,128)(2,1)S(1)}, u32[]{:S(2)}, u32[]{:S(2)}) collective-permute-start(bf16[128,512]{0,1:T(8,128)(2,1)S(1)} %fusion.109), channel_id=1, source_target_pairs={{0,8},{8,16},{16,24},{24,28},{28,20},{20,12},{12,4},{4,0},{1,9},{9... | collective-permute-start | bytes 393224 | tf_op jit(solution)/shard_map/ppermute | solution.py:220
  208.5 14.2 %collective-permute-start.12 = (bf16[256,512]{1,0:T(8,128)(2,1)S(1)}, bf16[256,512]{1,0:T(8,128)(2,1)S(1)}, u32[]{:S(2)}, u32[]{:S(2)}) collective-permute-start(bf16[256,512]{1,0:T(8,128)(2,1)S(1)} %fusion.75), channel_id=1, source_target_pairs={{0,2},{1,3},{2,0},{3,1},{4,6},{5,7},{6,4},{7,5},{8,10},{9,11},{10,... | collective-permute-start | bytes 786440 | tf_op jit(solution)/shard_map/ppermute | solution.py:243
  211.3 12.2 %collective-permute-start.33 = (bf16[128,1024]{1,0:T(8,128)(2,1)S(1)}, bf16[128,1024]{1,0:T(8,128)(2,1)S(1)}, u32[]{:S(2)}, u32[]{:S(2)}) collective-permute-start(bf16[128,1024]{1,0:T(8,128)(2,1)S(1)} %fusion.92), channel_id=1, source_target_pairs={{0,8},{8,16},{16,24},{24,28},{28,20},{20,12},{12,4},{4,0},{1,9},{9... | collective-permute-start | bytes 786440 | tf_op jit(solution)/shard_map/ppermute | solution.py:220
  213.1 5.0 %collective-permute-start.25 = (bf16[128,512]{0,1:T(8,128)(2,1)S(1)}, bf16[128,512]{0,1:T(8,128)(2,1)S(1)}, u32[]{:S(2)}, u32[]{:S(2)}) collective-permute-start(bf16[128,512]{0,1:T(8,128)(2,1)S(1)} %fusion.102), channel_id=1, source_target_pairs={{0,4},{8,0},{16,8},{24,16},{28,24},{20,28},{12,20},{4,12},{1,5},{9... | collective-permute-start | bytes 393224 | tf_op jit(solution)/shard_map/ppermute | solution.py:220
  213.5 7.8 %collective-permute-start.18 = (bf16[128,512]{0,1:T(8,128)(2,1)S(1)}, bf16[128,512]{0,1:T(8,128)(2,1)S(1)}, u32[]{:S(2)}, u32[]{:S(2)}) collective-permute-start(bf16[128,512]{0,1:T(8,128)(2,1)S(1)} %fusion.108), channel_id=1, source_target_pairs={{0,8},{8,16},{16,24},{24,28},{28,20},{20,12},{12,4},{4,0},{1,9},{9... | collective-permute-start | bytes 393224 | tf_op jit(solution)/shard_map/ppermute | solution.py:220
  218.1 15.7 %collective-permute-start.41 = (bf16[128,1024]{0,1:T(8,128)(2,1)S(1)}, bf16[128,1024]{0,1:T(8,128)(2,1)S(1)}, u32[]{:S(2)}, u32[]{:S(2)}) collective-permute-start(bf16[128,1024]{0,1:T(8,128)(2,1)S(1)} %fusion.85), channel_id=1, source_target_pairs={{0,4},{8,0},{16,8},{24,16},{28,24},{20,28},{12,20},{4,12},{1,5},{9... | collective-permute-start | bytes 786440 | tf_op jit(solution)/shard_map/ppermute | solution.py:220
  221.2 10.2 %collective-permute-start.26 = (bf16[128,512]{0,1:T(8,128)(2,1)S(1)}, bf16[128,512]{0,1:T(8,128)(2,1)S(1)}, u32[]{:S(2)}, u32[]{:S(2)}) collective-permute-start(bf16[128,512]{0,1:T(8,128)(2,1)S(1)} %fusion.101), channel_id=1, source_target_pairs={{0,4},{8,0},{16,8},{24,16},{28,24},{20,28},{12,20},{4,12},{1,5},{9... | collective-permute-start | bytes 393224 | tf_op jit(solution)/shard_map/ppermute | solution.py:220
  222.8 9.3 %collective-permute-start.19 = (bf16[128,512]{0,1:T(8,128)(2,1)S(1)}, bf16[128,512]{0,1:T(8,128)(2,1)S(1)}, u32[]{:S(2)}, u32[]{:S(2)}) collective-permute-start(bf16[128,512]{0,1:T(8,128)(2,1)S(1)} %fusion.107), channel_id=1, source_target_pairs={{0,8},{8,16},{16,24},{24,28},{28,20},{20,12},{12,4},{4,0},{1,9},{9... | collective-permute-start | bytes 393224 | tf_op jit(solution)/shard_map/ppermute | solution.py:220
  223.4 16.7 %collective-permute-start.13 = (bf16[256,512]{1,0:T(8,128)(2,1)S(1)}, bf16[256,512]{1,0:T(8,128)(2,1)S(1)}, u32[]{:S(2)}, u32[]{:S(2)}) collective-permute-start(bf16[256,512]{1,0:T(8,128)(2,1)S(1)} %add_convert_fusion.1), channel_id=1, source_target_pairs={{0,1},{1,0},{2,3},{3,2},{4,5},{5,4},{6,7},{7,6},{8,9},{9,8},{10,11... | collective-permute-start | bytes 786440 | tf_op jit(solution)/shard_map/ppermute | solution.py:243
  225.3 22.2 %collective-permute-start.34 = (bf16[128,1024]{1,0:T(8,128)(2,1)}, bf16[128,1024]{1,0:T(8,128)(2,1)}, u32[]{:S(2)}, u32[]{:S(2)}) collective-permute-start(bf16[128,1024]{1,0:T(8,128)(2,1)} %fusion.91), channel_id=1, source_target_pairs={{0,8},{8,16},{16,24},{24,28},{28,20},{20,12},{12,4},{4,0},{1,9},{9... | collective-permute-start | bytes 786440 | tf_op jit(solution)/shard_map/ppermute | solution.py:220
  231.5 5.8 %collective-permute-start.27 = (bf16[128,512]{0,1:T(8,128)(2,1)S(1)}, bf16[128,512]{0,1:T(8,128)(2,1)S(1)}, u32[]{:S(2)}, u32[]{:S(2)}) collective-permute-start(bf16[128,512]{0,1:T(8,128)(2,1)S(1)} %fusion.100), channel_id=1, source_target_pairs={{0,4},{8,0},{16,8},{24,16},{28,24},{20,28},{12,20},{4,12},{1,5},{9... | collective-permute-start | bytes 393224 | tf_op jit(solution)/shard_map/ppermute | solution.py:220
  232.2 5.7 %collective-permute-start.20 = (bf16[128,512]{0,1:T(8,128)(2,1)S(1)}, bf16[128,512]{0,1:T(8,128)(2,1)S(1)}, u32[]{:S(2)}, u32[]{:S(2)}) collective-permute-start(bf16[128,512]{0,1:T(8,128)(2,1)S(1)} %fusion.106), channel_id=1, source_target_pairs={{0,8},{8,16},{16,24},{24,28},{28,20},{20,12},{12,4},{4,0},{1,9},{9... | collective-permute-start | bytes 393224 | tf_op jit(solution)/shard_map/ppermute | solution.py:220
  234.5 19.7 %collective-permute-start.42 = (bf16[128,1024]{0,1:T(8,128)(2,1)}, bf16[128,1024]{0,1:T(8,128)(2,1)}, u32[]{:S(2)}, u32[]{:S(2)}) collective-permute-start(bf16[128,1024]{0,1:T(8,128)(2,1)} %fusion.84), channel_id=1, source_target_pairs={{0,4},{8,0},{16,8},{24,16},{28,24},{20,28},{12,20},{4,12},{1,5},{9... | collective-permute-start | bytes 786440 | tf_op jit(solution)/shard_map/ppermute | solution.py:220
  237.4 14.3 %collective-permute-start.28 = (bf16[128,512]{0,1:T(8,128)(2,1)S(1)}, bf16[128,512]{0,1:T(8,128)(2,1)}, u32[]{:S(2)}, u32[]{:S(2)}) collective-permute-start(bf16[128,512]{0,1:T(8,128)(2,1)S(1)} %fusion.99), channel_id=1, source_target_pairs={{0,4},{8,0},{16,8},{24,16},{28,24},{20,28},{12,20},{4,12},{1,5},{9... | collective-permute-start | bytes 393224 | tf_op jit(solution)/shard_map/ppermute | solution.py:220
  238.7 12.0 %collective-permute-start.21 = (bf16[128,512]{0,1:T(8,128)(2,1)}, bf16[128,512]{0,1:T(8,128)(2,1)}, u32[]{:S(2)}, u32[]{:S(2)}) collective-permute-start(bf16[128,512]{0,1:T(8,128)(2,1)} %fusion.105), channel_id=1, source_target_pairs={{0,8},{8,16},{16,24},{24,28},{28,20},{20,12},{12,4},{4,0},{1,9},{9... | collective-permute-start | bytes 393224 | tf_op jit(solution)/shard_map/ppermute | solution.py:220
  242.9 20.7 %all-to-all-start.2 = ((bf16[8,80,512]{2,1,0:T(8,128)(2,1)}), bf16[8,80,512]{2,1,0:T(8,128)(2,1)S(1)}, u32[]{:S(2)}, u32[]{:S(2)}) async-start(bf16[8,80,512]{2,1,0:T(8,128)(2,1)} %fusion.72), calls=%async_computation.2 | async-start | bytes 1310720 | tf_op jit(solution)/shard_map/all_to_all | solution.py:438
  248.6 15.1 %collective-permute-start.35 = (bf16[128,1024]{1,0:T(8,128)(2,1)S(1)}, bf16[128,1024]{1,0:T(8,128)(2,1)S(1)}, u32[]{:S(2)}, u32[]{:S(2)}) collective-permute-start(bf16[128,1024]{1,0:T(8,128)(2,1)S(1)} %fusion.90), channel_id=1, source_target_pairs={{0,8},{8,16},{16,24},{24,28},{28,20},{20,12},{12,4},{4,0},{1,9},{9... | collective-permute-start | bytes 786440 | tf_op jit(solution)/shard_map/ppermute | solution.py:220
  263.6 2.4 collective-permute-start.14
  (57 other events, 334.3 us)

commit v2 on v1

--- a/solution.py
+++ b/solution.py
@@ -214,25 +214,35 @@
     return list(range(0, size, 2)) + list(range(size - 1, 0, -2))
 
 
-def ring_permute(values, order, step):
+def ring_place(index, size):
+    return jnp.where(index % 2 == 0, index // 2, size - 1 - index // 2)
+
+
+def ring_owner(place, size):
+    place = place % size
+    return jnp.where(place < size // 2, 2 * place, 2 * (size - place) - 1)
+
+
+def ring_permute(values, direction):
+    order = ring_order(lax.axis_size("seq"))
     size = len(order)
-    pairs = [(order[i], order[(i + step) % size]) for i in range(size)]
+    pairs = [(order[i], order[(i + direction) % size]) for i in range(size)]
     return lax.ppermute(values, "seq", pairs)
 
 
-def ring_scatter(parts, direction):
-    size = parts.shape[0]
-    order = ring_order(size)
-    place = [order.index(i) for i in range(size)]
-    table = [
-        [order[(place[i] - direction * (1 + k)) % size] for k in range(size)] for i in range(size)
-    ]
-    mine = jnp.asarray(table, dtype=jnp.int32)[lax.axis_index("seq")]
-    total = lax.dynamic_index_in_dim(parts, mine[0], 0, False)
+def ring_scatter(whole, axis, direction):
+    size = lax.axis_size("seq")
+    place = ring_place(lax.axis_index("seq"), size)
+    width = whole.shape[axis] // size
+
+    def chunk(k):
+        owner = ring_owner(place + size - direction * (1 + k), size)
+        return lax.dynamic_slice_in_dim(whole, owner * width, width, axis)
+
+    total = chunk(0)
     for k in range(1, size):
-        moved = ring_permute(total, order, direction)
-        own = lax.dynamic_index_in_dim(parts, mine[k], 0, False)
-        total = moved.astype(jnp.float32) + own.astype(jnp.float32)
+        moved = ring_permute(total, direction)
+        total = moved.astype(jnp.float32) + chunk(k).astype(jnp.float32)
         if k < size - 1:
             total = total.astype(jnp.bfloat16)
     return total
@@ -319,14 +329,12 @@
 
     def fetch(source):
         own = lax.dynamic_slice_in_dim(source, core * half_width, half_width, 2)
-        return compact(table, own).astype(bf16)
-
-    sent = jnp.concatenate([fetch(tokens), fetch(out_grad)], axis=-1)
-    got = lax.all_to_all(sent, "seq", 0, 0, tiled=True)
-    got = from_owners(got, share)
-    other = tp_permute(got, 1)
-    routed_rows = join_halves(got[:, :half_width], other[:, :half_width], core)
-    routed_grads = join_halves(got[:, half_width:], other[:, half_width:], core)
+        own = compact(table, own).astype(bf16)
+        own = from_owners(lax.all_to_all(own, "seq", 0, 0, tiled=True), share)
+        return join_halves(own, tp_permute(own, 1), core)
+
+    routed_rows = fetch(tokens)
+    routed_grads = fetch(out_grad)
 
     rows = routed_rows.astype(f32)
     grad_rows = routed_grads.astype(f32)
@@ -375,10 +383,10 @@
         product = lax.dot_general(
             left, right, (((0,), (0,)), ((), ())), preferred_element_type=f32
         )
-        return product.astype(bf16).reshape(dev_count, -1, right.shape[1])
-
-    grad_up = ring_scatter(outer(mlp_input, grad_pre), 1)
-    grad_down = ring_scatter(outer(grad_mlp, hidden), -1).T
+        return product.astype(bf16)
+
+    grad_up = ring_scatter(outer(mlp_input, grad_pre), 0, 1)
+    grad_down = ring_scatter(outer(hidden, grad_mlp), 1, -1)
 
     weighted = grad_mlp_input * gain_second
     grad_residual = factor_second * weighted - residual * factor_second**3 * jnp.mean(
@@ -410,13 +418,14 @@
         ),
         core,
     )
-    forth = jnp.concatenate([outer(attn_input, grad_query), outer(attn_input, grad_key)], axis=-1)
-    back = jnp.concatenate([outer(attn_input, grad_value), outer(grad_attn, mixed)], axis=-1)
-    forth = ring_scatter(forth, 1)
-    back = ring_scatter(back, -1)
-    width = grad_query.shape[1]
-    grad_qkv = jnp.stack([forth[:, :width], forth[:, width:], back[:, :width]], axis=1)
-    grad_out = back[:, width:].T
+    grad_qkv = jnp.stack(
+        [
+            ring_scatter(outer(attn_input, grad_parts[c]), 0, -1 if c == 2 else 1)
+            for c in range(3)
+        ],
+        axis=1,
+    )
+    grad_out = ring_scatter(outer(mixed, grad_attn), 1, -1)
 
     branch = attn_out + mlp_out
     update = (gating * branch).astype(bf16)

time: 278 us -> 267 us (0.960)
  between operations: 31.9 us -> 1.86 us
  starting transfers between devices: 54.9 us -> 77.2 us
  local copies, waits for them, and re-layouts: 21.3 us -> 2.44 us
  waiting for transfers between devices: 70 us -> 88.2 us
    ppermute x28 -> x42, waiting for transfers between devices: 20.2 us -> 58.6 us  [ring_permute(): return lax.ppermute(values, 'seq', pairs)]
    all_to_all x2 -> x1, waiting for transfers between devices: 31.8 us -> 0.01 us  [on_device_whole(): got = lax.all_to_all(sent, 'seq', 0, 0, tiled=True)]
    all_to_all x0 -> x2, waiting for transfers between devices: none -> 18.7 us  [fetch(): own = from_owners(lax.all_to_all(own, 'seq', 0, 0, tiled=True), share)]
    ppermute x28 -> x42, starting transfers between devices: 31.1 us -> 48.4 us  [ring_permute(): return lax.ppermute(values, 'seq', pairs)]
    all_to_all x0 -> x2, starting transfers between devices: none -> 11.4 us  [fetch(): own = from_owners(lax.all_to_all(own, 'seq', 0, 0, tiled=True), share)]
    unnamed x127 -> x99, local copies, waits for them, and re-layouts: 8.99 us -> 0.68 us
    all_to_all x2 -> x1, starting transfers between devices: 12 us -> 4 us  [on_device_whole(): got = lax.all_to_all(sent, 'seq', 0, 0, tiled=True)]
    ppermute x15 -> x16, waiting for transfers between devices: 18 us -> 11 us  [tp_permute(): return lax.ppermute(values, 'tp', [(i, i ^ mask) for i in range(size)])]
  transfers between devices with their start and end apart: 46 -> 62, of which waited for: 16 -> 28; matrix products, arithmetic and copies ran while one was open for 29% -> 27% of each run, Pallas kernels for 0% -> 0%
where the time goes in v2:
time: 267 us; the launch traced here: 262 us
  waiting for transfers between devices  88.2 us (33%)
  starting transfers between devices  77.2 us (29%)
  matrix products  46.4 us (17%)
  other arithmetic  46.3 us (17%)
    ppermute x42, waiting for transfers between devices, ring_permute(): return lax.ppermute(values, 'seq', pairs)  58.6 us
    ppermute x42, starting transfers between devices, ring_permute(): return lax.ppermute(values, 'seq', pairs)  48.4 us
    all_to_all x2, waiting for transfers between devices, fetch(): own = from_owners(lax.all_to_all(own, 'seq', 0, 0, tiled=True), share)  18.7 us
    convert_element_type x36, other arithmetic, ring_scatter(): total = total.astype(jnp.bfloat16)  14.9 us
    dot_general x2, matrix products, spread(): jnp.einsum('sqc,sqd->scd', table, routed_rows, preferred_element_type=jnp...  13.4 us
    all_to_all x2, starting transfers between devices, fetch(): own = from_owners(lax.all_to_all(own, 'seq', 0, 0, tiled=True), share)  11.4 us
    ppermute x16, waiting for transfers between devices, tp_permute(): return lax.ppermute(values, 'tp', [(i, i ^ mask) for i in range(size)])  11 us
    ppermute x16, starting transfers between devices, tp_permute(): return lax.ppermute(values, 'tp', [(i, i ^ mask) for i in range(size)])  8.19 us
  transfers between devices with their start and end apart: 62, of which 28 were waited for; matrix products, arithmetic and copies ran while one was open for 27% of the time, Pallas kernels for 0%

profile of v2, /device:TPU:0, one launch (start us, length us, event | category | flops | bytes accessed | tf_op | source)
XLA Modules:
  0.0 262.4 jit_solution(6057266792738477971)
XLA Ops:
  1.6 2.9 %fusion.16 = bf16[8,64,512]{2,1,0:T(8,128)(2,1)} fusion(bf16[8,256,1024]{2,1,0:T(8,128)(2,1)} %param.11, s32[]{:T(128)S(6)} %select_n.442, s32[8,64]{1,0:T(8,128)S(1)} %fusion.103), kind=kOutput, calls=%fused_computation.46 | convolution fusion | flops 134610944 | bytes 2623492 | tf_op jit(solution)/shard_map/sqc,scd->sqd/dot_general | solution.py:28
  4.5 7.3 %all-to-all-start = ((bf16[8,64,512]{2,1,0:T(8,128)(2,1)}), bf16[8,64,512]{2,1,0:T(8,128)(2,1)S(1)}, u32[]{:S(2)}, u32[]{:S(2)}) async-start(bf16[8,64,512]{2,1,0:T(8,128)(2,1)} %fusion.16), calls=%async_computation | async-start | bytes 1048576 | tf_op jit(solution)/shard_map/all_to_all | solution.py:333
  13.4 12.9 %all-to-all-done = bf16[8,64,512]{2,1,0:T(8,128)(2,1)S(1)} async-done(((bf16[8,64,512]{2,1,0:T(8,128)(2,1)}), bf16[8,64,512]{2,1,0:T(8,128)(2,1)S(1)}, u32[]{:S(2)}, u32[]{:S(2)}) %all-to-all-start) | async-done | bytes 524320 | tf_op jit(solution)/shard_map/all_to_all | solution.py:333
  26.4 2.6 %fusion.106 = s32[1,256]{1,0:T(1,128)S(1)} fusion(s32[8,256]{1,0:T(8,128)} %param.13, s32[]{:T(128)S(6)} %select_n.444, s32[]{:T(128)} %get-tuple-element.17, s32[]{:T(128)} %get-tuple-element.16, s32[]{:T(128)} %get-tuple-element.15), kind=kLoop, calls=%fused_computation.234 | loop fusion | flops 2048 | bytes 2064 | tf_op jit(solution)/shard_map/add | solution.py:321
  30.1 2.2 fusion.27
  39.4 7.1 %collective-permute-done.2 = bf16[256,512]{1,0:T(8,128)(2,1)S(1)} collective-permute-done((bf16[256,512]{1,0:T(8,128)(2,1)S(1)}, bf16[256,512]{1,0:T(8,128)(2,1)S(1)}, u32[]{:S(2)}, u32[]{:S(2)}) %collective-permute-start.2) | collective-permute-done | bytes 262176 | tf_op jit(solution)/shard_map/ppermute | solution.py:253
  48.0 4.1 %all-to-all-start.2 = ((bf16[8,64,512]{2,1,0:T(8,128)(2,1)}), bf16[8,64,512]{2,1,0:T(8,128)(2,1)}, u32[]{:S(2)}, u32[]{:S(2)}) async-start(bf16[8,64,512]{2,1,0:T(8,128)(2,1)} %fusion.19), calls=%async_computation.2 | async-start | bytes 1048576 | tf_op jit(solution)/shard_map/all_to_all | solution.py:333
  54.4 2.4 fusion.117
  61.8 5.7 %all-to-all-done.2 = bf16[8,64,512]{2,1,0:T(8,128)(2,1)} async-done(((bf16[8,64,512]{2,1,0:T(8,128)(2,1)}), bf16[8,64,512]{2,1,0:T(8,128)(2,1)}, u32[]{:S(2)}, u32[]{:S(2)}) %all-to-all-start.2) | async-done | bytes 524320 | tf_op jit(solution)/shard_map/all_to_all | solution.py:333
  69.6 1.8 add_convert_fusion.15
  73.4 1.8 fusion.35
  78.8 5.1 %all-to-all-start.1 = ((bf16[8,64,512]{2,1,0:T(8,128)(2,1)}), bf16[8,64,512]{2,1,0:T(8,128)(2,1)}, u32[]{:S(2)}, u32[]{:S(2)}) async-start(bf16[8,64,512]{2,1,0:T(8,128)(2,1)} %fusion.73), calls=%async_computation.1 | async-start | bytes 1048576 | tf_op jit(solution)/shard_map/all_to_all | solution.py:445
  83.9 2.5 convolution_convert_fusion
  86.5 2.2 collective-permute-start.51
  88.8 2.3 fusion.44
  95.6 5.0 %collective-permute-done.51 = bf16[1024,128]{1,0:T(8,128)(2,1)S(1)} collective-permute-done((bf16[1024,128]{1,0:T(8,128)(2,1)S(1)}, bf16[1024,128]{1,0:T(8,128)(2,1)S(1)}, u32[]{:S(2)}, u32[]{:S(2)}) %collective-permute-start.51) | collective-permute-done | bytes 262176 | tf_op jit(solution)/shard_map/ppermute | solution.py:230
  102.5 2.7 %collective-permute-start.45 = (bf16[128,1024]{1,0:T(8,128)(2,1)S(1)}, bf16[128,1024]{1,0:T(8,128)(2,1)S(1)}, u32[]{:S(2)}, u32[]{:S(2)}) collective-permute-start(bf16[128,1024]{1,0:T(8,128)(2,1)S(1)} %add_convert_fusion.12), channel_id=1, source_target_pairs={{0,8},{8,16},{16,24},{24,28},{28,20},{20,12},{12,4},{4,0},{1,9},{9... | collective-permute-start | bytes 786440 | tf_op jit(solution)/shard_map/ppermute | solution.py:230
  105.3 5.1 %collective-permute-done.52 = bf16[1024,128]{1,0:T(8,128)(2,1)S(1)} collective-permute-done((bf16[1024,128]{1,0:T(8,128)(2,1)S(1)}, bf16[1024,128]{1,0:T(8,128)(2,1)S(1)}, u32[]{:S(2)}, u32[]{:S(2)}) %collective-permute-start.52) | collective-permute-done | bytes 262176 | tf_op jit(solution)/shard_map/ppermute | solution.py:230
  114.5 2.0 fusion.34
  116.8 2.5 convolution_convert_fusion.7
  120.6 3.3 %convolution_convert_fusion.9 = bf16[4,64,256]{2,1,0:T(8,128)(2,1)} fusion(bf16[256,4,64]{0,2,1:T(8,128)(2,1)S(1)} %bitcast.136, f32[4,256,256]{1,2,0:T(8,128)} %fusion.129, f32[4,256,256]{1,2,0:T(8,128)} %get-tuple-element.31, f32[4,256]{1,0:T(4,128)S(1)} %copy-done.48), kind=kOutput, calls=%fused_computation.57 | convolution fusion | flops 35456256 | bytes 2363392 | tf_op jit(solution)/shard_map/hqk,khe->qhe/dot_general | solution.py:408
  123.9 3.3 %convolution_convert_fusion.8 = bf16[4,64,256]{2,1,0:T(8,128)(2,1)} fusion(bf16[256,4,64]{0,2,1:T(8,128)(2,1)S(1)} %bitcast.132, f32[4,256,256]{1,2,0:T(8,128)} %fusion.129, f32[4,256,256]{1,2,0:T(8,128)} %get-tuple-element.31, f32[4,256]{1,0:T(4,128)S(1)} %copy-done.48), kind=kOutput, calls=%fused_computation.56 | convolution fusion | flops 35456256 | bytes 2363392 | tf_op jit(solution)/shard_map/hqk,qhe->khe/dot_general | solution.py:409
  130.1 2.1 collective-permute-start.37
  132.7 2.1 collective-permute-start.30
  139.0 1.8 add_convert_fusion.10
  143.3 2.0 collective-permute-start.31
  147.0 1.8 collective-permute-start.17
  149.6 2.4 collective-permute-done.17
  154.4 2.0 collective-permute-start.32
  159.4 2.2 collective-permute-done.18
  163.2 2.0 collective-permute-start.40
  171.8 2.0 collective-permute-start.55
  176.8 4.1 %collective-permute-done.41 = bf16[256,128]{1,0:T(8,128)(2,1)S(1)} collective-permute-done((bf16[256,128]{1,0:T(8,128)(2,1)S(1)}, bf16[256,128]{1,0:T(8,128)(2,1)S(1)}, u32[]{:S(2)}, u32[]{:S(2)}) %collective-permute-start.41) | collective-permute-done | bytes 65568 | tf_op jit(solution)/shard_map/ppermute | solution.py:230
  187.4 2.7 %collective-permute-done.42 = bf16[256,128]{1,0:T(8,128)(2,1)S(1)} collective-permute-done((bf16[256,128]{1,0:T(8,128)(2,1)S(1)}, bf16[256,128]{1,0:T(8,128)(2,1)S(1)}, u32[]{:S(2)}, u32[]{:S(2)}) %collective-permute-start.42) | collective-permute-done | bytes 65568 | tf_op jit(solution)/shard_map/ppermute | solution.py:230
  191.7 2.7 %collective-permute-done.35 = bf16[128,256]{1,0:T(8,128)(2,1)S(1)} collective-permute-done((bf16[128,256]{1,0:T(8,128)(2,1)S(1)}, bf16[128,256]{1,0:T(8,128)(2,1)S(1)}, u32[]{:S(2)}, u32[]{:S(2)}) %collective-permute-start.35) | collective-permute-done | bytes 65568 | tf_op jit(solution)/shard_map/ppermute | solution.py:230
  194.9 3.7 %collective-permute-done.21 = bf16[128,256]{1,0:T(8,128)(2,1)S(1)} collective-permute-done((bf16[128,256]{1,0:T(8,128)(2,1)S(1)}, bf16[128,256]{1,0:T(8,128)(2,1)S(1)}, u32[]{:S(2)}, u32[]{:S(2)}) %collective-permute-start.21) | collective-permute-done | bytes 65568 | tf_op jit(solution)/shard_map/ppermute | solution.py:230
  199.2 3.7 %collective-permute-done.28 = bf16[128,256]{1,0:T(8,128)(2,1)S(1)} collective-permute-done((bf16[128,256]{1,0:T(8,128)(2,1)S(1)}, bf16[128,256]{1,0:T(8,128)(2,1)S(1)}, u32[]{:S(2)}, u32[]{:S(2)}) %collective-permute-start.28) | collective-permute-done | bytes 65568 | tf_op jit(solution)/shard_map/ppermute | solution.py:230
  204.5 2.7 %collective-permute-done.43 = bf16[256,128]{1,0:T(8,128)(2,1)S(1)} collective-permute-done((bf16[256,128]{1,0:T(8,128)(2,1)S(1)}, bf16[256,128]{1,0:T(8,128)(2,1)S(1)}, u32[]{:S(2)}, u32[]{:S(2)}) %collective-permute-start.43) | collective-permute-done | bytes 65568 | tf_op jit(solution)/shard_map/ppermute | solution.py:230
  209.4 2.0 collective-permute-done.36
  212.0 3.7 %collective-permute-done.22 = bf16[128,256]{1,0:T(8,128)(2,1)S(1)} collective-permute-done((bf16[128,256]{1,0:T(8,128)(2,1)S(1)}, bf16[128,256]{1,0:T(8,128)(2,1)S(1)}, u32[]{:S(2)}, u32[]{:S(2)}) %collective-permute-start.22) | collective-permute-done | bytes 65568 | tf_op jit(solution)/shard_map/ppermute | solution.py:230
  216.3 3.7 %collective-permute-done.29 = bf16[128,256]{1,0:T(8,128)(2,1)S(1)} collective-permute-done((bf16[128,256]{1,0:T(8,128)(2,1)S(1)}, bf16[128,256]{1,0:T(8,128)(2,1)S(1)}, u32[]{:S(2)}, u32[]{:S(2)}) %collective-permute-start.29) | collective-permute-done | bytes 65568 | tf_op jit(solution)/shard_map/ppermute | solution.py:230
  228.5 4.0 %all-to-all-start.3 = ((bf16[8,80,512]{2,1,0:T(8,128)(2,1)}), bf16[8,80,512]{2,1,0:T(8,128)(2,1)S(1)}, u32[]{:S(2)}, u32[]{:S(2)}) async-start(bf16[8,80,512]{2,1,0:T(8,128)(2,1)} %fusion.72), calls=%async_computation.3 | async-start | bytes 1310720 | tf_op jit(solution)/shard_map/all_to_all | solution.py:447
  233.6 2.1 collective-permute-start.57
  236.7 6.3 %add_convert_fusion = bf16[8,256,1024]{2,1,0:T(8,128)(2,1)} fusion(bf16[8,256,1024]{2,1,0:T(8,128)(2,1)} %param.11, bf16[8,64,512]{2,1,0:T(8,128)(2,1)} %collective-permute-done.7, bf16[8,64,512]{2,1,0:T(8,128)(2,1)} %all-to-all-done.1, pred[]{:T(512)S(6)} %eq.119, s32[8,64]{1,0:T(8,128)S(1)} %fusion.103), kind=kOutput, calls=%fused_computation.3 | convolution fusion | flops 279576576 | bytes 9439233 | tf_op jit(solution)/shard_map/sqc,sqd->scd/dot_general | solution.py:32
  243.0 8.0 %collective-permute-done.57 = bf16[1024,128]{1,0:T(8,128)(2,1)S(1)} collective-permute-done((bf16[1024,128]{1,0:T(8,128)(2,1)S(1)}, bf16[1024,128]{1,0:T(8,128)(2,1)S(1)}, u32[]{:S(2)}, u32[]{:S(2)}) %collective-permute-start.57) | collective-permute-done | bytes 262176 | tf_op jit(solution)/shard_map/ppermute | solution.py:230
  251.0 1.8 convert_add_fusion.3
  252.9 1.8 convert_add_fusion.4
  255.3 7.1 %convert_add_fusion = f32[8,256,1024]{2,1,0:T(8,128)} fusion(bf16[8,256,1024]{2,1,0:T(8,128)(2,1)} %param.21, bf16[8,64,512]{2,1,0:T(8,128)(2,1)S(1)} %collective-permute-done.15, bf16[8,64,512]{2,1,0:T(8,128)(2,1)S(1)} %slice.188, pred[]{:T(512)S(6)} %eq.119, s32[8,64]{1,0:T(8,128)S(1)} %fusion.103), kind=kOutput, calls=%fused_computation.2 | convolution fusion | flops 277479424 | bytes 13633537 | tf_op jit(solution)/shard_map/sqc,sqd->scd/dot_general | solution.py:32
  (298 shorter events, 93.1 us)
Async XLA Ops:
  4.5 21.8 %all-to-all-start = ((bf16[8,64,512]{2,1,0:T(8,128)(2,1)}), bf16[8,64,512]{2,1,0:T(8,128)(2,1)S(1)}, u32[]{:S(2)}, u32[]{:S(2)}) async-start(bf16[8,64,512]{2,1,0:T(8,128)(2,1)} %fusion.16), calls=%async_computation | async-start | bytes 1048576 | tf_op jit(solution)/shard_map/all_to_all | solution.py:333
  37.8 8.7 %collective-permute-start.2 = (bf16[256,512]{1,0:T(8,128)(2,1)S(1)}, bf16[256,512]{1,0:T(8,128)(2,1)S(1)}, u32[]{:S(2)}, u32[]{:S(2)}) collective-permute-start(bf16[256,512]{1,0:T(8,128)(2,1)S(1)} %fusion.82), channel_id=1, source_target_pairs={{0,2},{1,3},{2,0},{3,1},{4,6},{5,7},{6,4},{7,5},{8,10},{9,11},{10,... | collective-permute-start | bytes 786440 | tf_op jit(solution)/shard_map/ppermute | solution.py:253
  46.6 6.3 %collective-permute-start.3 = (bf16[256,512]{1,0:T(8,128)(2,1)S(1)}, bf16[256,512]{1,0:T(8,128)(2,1)S(1)}, u32[]{:S(2)}, u32[]{:S(2)}) collective-permute-start(bf16[256,512]{1,0:T(8,128)(2,1)S(1)} %add_convert_fusion.16), channel_id=1, source_target_pairs={{0,1},{1,0},{2,3},{3,2},{4,5},{5,4},{6,7},{7,6},{8,9},{9,8},{10,11... | collective-permute-start | bytes 786440 | tf_op jit(solution)/shard_map/ppermute | solution.py:253
  48.0 19.6 %all-to-all-start.2 = ((bf16[8,64,512]{2,1,0:T(8,128)(2,1)}), bf16[8,64,512]{2,1,0:T(8,128)(2,1)}, u32[]{:S(2)}, u32[]{:S(2)}) async-start(bf16[8,64,512]{2,1,0:T(8,128)(2,1)} %fusion.19), calls=%async_computation.2 | async-start | bytes 1048576 | tf_op jit(solution)/shard_map/all_to_all | solution.py:333
  60.3 9.2 %collective-permute-start.5 = (bf16[256,512]{1,0:T(8,128)(2,1)}, bf16[256,512]{1,0:T(8,128)(2,1)}, u32[]{:S(2)}, u32[]{:S(2)}) collective-permute-start(bf16[256,512]{1,0:T(8,128)(2,1)} %fusion.80), channel_id=1, source_target_pairs={{0,2},{1,3},{2,0},{3,1},{4,6},{5,7},{6,4},{7,5},{8,10},{9,11},{10,... | collective-permute-start | bytes 786440 | tf_op jit(solution)/shard_map/ppermute | solution.py:253
  78.8 80.6 %all-to-all-start.1 = ((bf16[8,64,512]{2,1,0:T(8,128)(2,1)}), bf16[8,64,512]{2,1,0:T(8,128)(2,1)}, u32[]{:S(2)}, u32[]{:S(2)}) async-start(bf16[8,64,512]{2,1,0:T(8,128)(2,1)} %fusion.73), calls=%async_computation.1 | async-start | bytes 1048576 | tf_op jit(solution)/shard_map/all_to_all | solution.py:445
  86.5 14.1 %collective-permute-start.51 = (bf16[1024,128]{1,0:T(8,128)(2,1)S(1)}, bf16[1024,128]{1,0:T(8,128)(2,1)S(1)}, u32[]{:S(2)}, u32[]{:S(2)}) collective-permute-start(bf16[1024,128]{1,0:T(8,128)(2,1)S(1)} %constant_dynamic-slice_fusion), channel_id=1, source_target_pairs={{0,4},{8,0},{16,8},{24,16},{28,24},{20,28},{12,20},{4,12},{1,5},{9... | collective-permute-start | bytes 786440 | tf_op jit(solution)/shard_map/ppermute | solution.py:230
  93.0 9.4 %collective-permute-start.44 = (bf16[128,1024]{1,0:T(8,128)(2,1)S(1)}, bf16[128,1024]{1,0:T(8,128)(2,1)S(1)}, u32[]{:S(2)}, u32[]{:S(2)}) collective-permute-start(bf16[128,1024]{1,0:T(8,128)(2,1)S(1)} %constant_dynamic-slice_fusion.1), channel_id=1, source_target_pairs={{0,8},{8,16},{16,24},{24,28},{28,20},{20,12},{12,4},{4,0},{1,9},{9... | collective-permute-start | bytes 786440 | tf_op jit(solution)/shard_map/ppermute | solution.py:230
  94.0 11.2 %collective-permute-start.10 = (bf16[256,512]{1,0:T(8,128)(2,1)S(1)}, bf16[256,512]{1,0:T(8,128)(2,1)S(1)}, u32[]{:S(2)}, u32[]{:S(2)}) collective-permute-start(bf16[256,512]{1,0:T(8,128)(2,1)S(1)} %fusion.78), channel_id=1, source_target_pairs={{0,2},{1,3},{2,0},{3,1},{4,6},{5,7},{6,4},{7,5},{8,10},{9,11},{10,... | collective-permute-start | bytes 786440 | tf_op jit(solution)/shard_map/ppermute | solution.py:253
  100.7 9.8 %collective-permute-start.52 = (bf16[1024,128]{1,0:T(8,128)(2,1)S(1)}, bf16[1024,128]{1,0:T(8,128)(2,1)S(1)}, u32[]{:S(2)}, u32[]{:S(2)}) collective-permute-start(bf16[1024,128]{1,0:T(8,128)(2,1)S(1)} %add_convert_fusion.6), channel_id=1, source_target_pairs={{0,4},{8,0},{16,8},{24,16},{28,24},{20,28},{12,20},{4,12},{1,5},{9... | collective-permute-start | bytes 786440 | tf_op jit(solution)/shard_map/ppermute | solution.py:230
  102.5 8.5 %collective-permute-start.45 = (bf16[128,1024]{1,0:T(8,128)(2,1)S(1)}, bf16[128,1024]{1,0:T(8,128)(2,1)S(1)}, u32[]{:S(2)}, u32[]{:S(2)}) collective-permute-start(bf16[128,1024]{1,0:T(8,128)(2,1)S(1)} %add_convert_fusion.12), channel_id=1, source_target_pairs={{0,8},{8,16},{16,24},{24,28},{28,20},{20,12},{12,4},{4,0},{1,9},{9... | collective-permute-start | bytes 786440 | tf_op jit(solution)/shard_map/ppermute | solution.py:230
  105.3 8.2 %collective-permute-start.11 = (bf16[256,512]{1,0:T(8,128)(2,1)S(1)}, bf16[256,512]{1,0:T(8,128)(2,1)S(1)}, u32[]{:S(2)}, u32[]{:S(2)}) collective-permute-start(bf16[256,512]{1,0:T(8,128)(2,1)S(1)} %add_convert_fusion.14), channel_id=1, source_target_pairs={{0,1},{1,0},{2,3},{3,2},{4,5},{5,4},{6,7},{7,6},{8,9},{9,8},{10,11... | collective-permute-start | bytes 786440 | tf_op jit(solution)/shard_map/ppermute | solution.py:253
  110.6 16.9 %collective-permute-start.53 = (bf16[1024,128]{1,0:T(8,128)(2,1)S(1)}, bf16[1024,128]{1,0:T(8,128)(2,1)S(1)}, u32[]{:S(2)}, u32[]{:S(2)}) collective-permute-start(bf16[1024,128]{1,0:T(8,128)(2,1)S(1)} %add_convert_fusion.5), channel_id=1, source_target_pairs={{0,4},{8,0},{16,8},{24,16},{28,24},{20,28},{12,20},{4,12},{1,5},{9... | collective-permute-start | bytes 786440 | tf_op jit(solution)/shard_map/ppermute | solution.py:230
  111.7 27.3 %collective-permute-start.46 = (bf16[128,1024]{1,0:T(8,128)(2,1)}, bf16[128,1024]{1,0:T(8,128)(2,1)}, u32[]{:S(2)}, u32[]{:S(2)}) collective-permute-start(bf16[128,1024]{1,0:T(8,128)(2,1)} %add_convert_fusion.11), channel_id=1, source_target_pairs={{0,8},{8,16},{16,24},{24,28},{28,20},{20,12},{12,4},{4,0},{1,9},{9... | collective-permute-start | bytes 786440 | tf_op jit(solution)/shard_map/ppermute | solution.py:230
  129.3 36.8 %collective-permute-start.54 = (bf16[1024,128]{1,0:T(8,128)(2,1)}, bf16[1024,128]{1,0:T(8,128)(2,1)S(1)}, u32[]{:S(2)}, u32[]{:S(2)}) collective-permute-start(bf16[1024,128]{1,0:T(8,128)(2,1)} %add_convert_fusion.4), channel_id=1, source_target_pairs={{0,4},{8,0},{16,8},{24,16},{28,24},{20,28},{12,20},{4,12},{1,5},{9... | collective-permute-start | bytes 786440 | tf_op jit(solution)/shard_map/ppermute | solution.py:230
  130.1 10.7 %collective-permute-start.37 = (bf16[256,128]{1,0:T(8,128)(2,1)S(1)}, bf16[256,128]{1,0:T(8,128)(2,1)S(1)}, u32[]{:S(2)}, u32[]{:S(2)}) collective-permute-start(bf16[256,128]{1,0:T(8,128)(2,1)S(1)} %constant_dynamic-slice_fusion.2), channel_id=1, source_target_pairs={{0,4},{8,0},{16,8},{24,16},{28,24},{20,28},{12,20},{4,12},{1,5},{9... | collective-permute-start | bytes 196616 | tf_op jit(solution)/shard_map/ppermute | solution.py:230
  132.7 8.2 %collective-permute-start.30 = (bf16[128,256]{1,0:T(8,128)(2,1)S(1)}, bf16[128,256]{1,0:T(8,128)(2,1)S(1)}, u32[]{:S(2)}, u32[]{:S(2)}) collective-permute-start(bf16[128,256]{1,0:T(8,128)(2,1)S(1)} %constant_dynamic-slice_fusion.3), channel_id=1, source_target_pairs={{0,4},{8,0},{16,8},{24,16},{28,24},{20,28},{12,20},{4,12},{1,5},{9... | collective-permute-start | bytes 196616 | tf_op jit(solution)/shard_map/ppermute | solution.py:230
  135.2 7.0 %collective-permute-start.16 = (bf16[128,256]{1,0:T(8,128)(2,1)S(1)}, bf16[128,256]{1,0:T(8,128)(2,1)S(1)}, u32[]{:S(2)}, u32[]{:S(2)}) collective-permute-start(bf16[128,256]{1,0:T(8,128)(2,1)S(1)} %constant_dynamic-slice_fusion.5), channel_id=1, source_target_pairs={{0,8},{8,16},{16,24},{24,28},{28,20},{20,12},{12,4},{4,0},{1,9},{9... | collective-permute-start | bytes 196616 | tf_op jit(solution)/shard_map/ppermute | solution.py:230
  139.0 4.3 %collective-permute-start.23 = (bf16[128,256]{1,0:T(8,128)(2,1)S(1)}, bf16[128,256]{1,0:T(8,128)(2,1)S(1)}, u32[]{:S(2)}, u32[]{:S(2)}) collective-permute-start(bf16[128,256]{1,0:T(8,128)(2,1)S(1)} %constant_dynamic-slice_fusion.4), channel_id=1, source_target_pairs={{0,8},{8,16},{16,24},{24,28},{28,20},{20,12},{12,4},{4,0},{1,9},{9... | collective-permute-start | bytes 196616 | tf_op jit(solution)/shard_map/ppermute | solution.py:230
  140.8 27.2 %collective-permute-start.12 = (bf16[256,512]{1,0:T(8,128)(2,1)}, bf16[256,512]{1,0:T(8,128)(2,1)}, u32[]{:S(2)}, u32[]{:S(2)}) collective-permute-start(bf16[256,512]{1,0:T(8,128)(2,1)} %slice_select_fusion.5), channel_id=1, source_target_pairs={{0,1},{1,0},{2,3},{3,2},{4,5},{5,4},{6,7},{7,6},{8,9},{9,8},{10,11... | collective-permute-start | bytes 786440 | tf_op jit(solution)/shard_map/ppermute | solution.py:253
  140.9 29.7 %collective-permute-start.47 = (bf16[128,1024]{1,0:T(8,128)(2,1)}, bf16[128,1024]{1,0:T(8,128)(2,1)}, u32[]{:S(2)}, u32[]{:S(2)}) collective-permute-start(bf16[128,1024]{1,0:T(8,128)(2,1)} %add_convert_fusion.10), channel_id=1, source_target_pairs={{0,8},{8,16},{16,24},{24,28},{28,20},{20,12},{12,4},{4,0},{1,9},{9... | collective-permute-start | bytes 786440 | tf_op jit(solution)/shard_map/ppermute | solution.py:230
  142.2 4.9 %collective-permute-start.38 = (bf16[256,128]{1,0:T(8,128)(2,1)S(1)}, bf16[256,128]{1,0:T(8,128)(2,1)S(1)}, u32[]{:S(2)}, u32[]{:S(2)}) collective-permute-start(bf16[256,128]{1,0:T(8,128)(2,1)S(1)} %add_convert_fusion.22), channel_id=1, source_target_pairs={{0,4},{8,0},{16,8},{24,16},{28,24},{20,28},{12,20},{4,12},{1,5},{9... | collective-permute-start | bytes 196616 | tf_op jit(solution)/shard_map/ppermute | solution.py:230
  143.3 5.6 %collective-permute-start.31 = (bf16[128,256]{1,0:T(8,128)(2,1)S(1)}, bf16[128,256]{1,0:T(8,128)(2,1)S(1)}, u32[]{:S(2)}, u32[]{:S(2)}) collective-permute-start(bf16[128,256]{1,0:T(8,128)(2,1)S(1)} %add_convert_fusion.28), channel_id=1, source_target_pairs={{0,4},{8,0},{16,8},{24,16},{28,24},{20,28},{12,20},{4,12},{1,5},{9... | collective-permute-start | bytes 196616 | tf_op jit(solution)/shard_map/ppermute | solution.py:230
  147.0 5.0 %collective-permute-start.17 = (bf16[128,256]{1,0:T(8,128)(2,1)S(1)}, bf16[128,256]{1,0:T(8,128)(2,1)S(1)}, u32[]{:S(2)}, u32[]{:S(2)}) collective-permute-start(bf16[128,256]{1,0:T(8,128)(2,1)S(1)} %add_convert_fusion.40), channel_id=1, source_target_pairs={{0,8},{8,16},{16,24},{24,28},{28,20},{20,12},{12,4},{4,0},{1,9},{9... | collective-permute-start | bytes 196616 | tf_op jit(solution)/shard_map/ppermute | solution.py:230
  148.9 5.4 %collective-permute-start.24 = (bf16[128,256]{1,0:T(8,128)(2,1)S(1)}, bf16[128,256]{1,0:T(8,128)(2,1)S(1)}, u32[]{:S(2)}, u32[]{:S(2)}) collective-permute-start(bf16[128,256]{1,0:T(8,128)(2,1)S(1)} %add_convert_fusion.34), channel_id=1, source_target_pairs={{0,8},{8,16},{16,24},{24,28},{28,20},{20,12},{12,4},{4,0},{1,9},{9... | collective-permute-start | bytes 196616 | tf_op jit(solution)/shard_map/ppermute | solution.py:230
  152.0 5.0 %collective-permute-start.39 = (bf16[256,128]{1,0:T(8,128)(2,1)S(1)}, bf16[256,128]{1,0:T(8,128)(2,1)S(1)}, u32[]{:S(2)}, u32[]{:S(2)}) collective-permute-start(bf16[256,128]{1,0:T(8,128)(2,1)S(1)} %add_convert_fusion.21), channel_id=1, source_target_pairs={{0,4},{8,0},{16,8},{24,16},{28,24},{20,28},{12,20},{4,12},{1,5},{9... | collective-permute-start | bytes 196616 | tf_op jit(solution)/shard_map/ppermute | solution.py:230
  154.4 4.3 %collective-permute-start.32 = (bf16[128,256]{1,0:T(8,128)(2,1)S(1)}, bf16[128,256]{1,0:T(8,128)(2,1)S(1)}, u32[]{:S(2)}, u32[]{:S(2)}) collective-permute-start(bf16[128,256]{1,0:T(8,128)(2,1)S(1)} %add_convert_fusion.27), channel_id=1, source_target_pairs={{0,4},{8,0},{16,8},{24,16},{28,24},{20,28},{12,20},{4,12},{1,5},{9... | collective-permute-start | bytes 196616 | tf_op jit(solution)/shard_map/ppermute | solution.py:230
  157.0 4.6 %collective-permute-start.18 = (bf16[128,256]{1,0:T(8,128)(2,1)}, bf16[128,256]{1,0:T(8,128)(2,1)}, u32[]{:S(2)}, u32[]{:S(2)}) collective-permute-start(bf16[128,256]{1,0:T(8,128)(2,1)} %add_convert_fusion.39), channel_id=1, source_target_pairs={{0,8},{8,16},{16,24},{24,28},{28,20},{20,12},{12,4},{4,0},{1,9},{9... | collective-permute-start | bytes 196616 | tf_op jit(solution)/shard_map/ppermute | solution.py:230
  158.6 4.6 %collective-permute-start.25 = (bf16[128,256]{1,0:T(8,128)(2,1)}, bf16[128,256]{1,0:T(8,128)(2,1)}, u32[]{:S(2)}, u32[]{:S(2)}) collective-permute-start(bf16[128,256]{1,0:T(8,128)(2,1)} %add_convert_fusion.33), channel_id=1, source_target_pairs={{0,8},{8,16},{16,24},{24,28},{28,20},{20,12},{12,4},{4,0},{1,9},{9... | collective-permute-start | bytes 196616 | tf_op jit(solution)/shard_map/ppermute | solution.py:230
  161.6 75.1 %collective-permute-start.7 = (bf16[8,64,512]{2,1,0:T(8,128)(2,1)}, bf16[8,64,512]{2,1,0:T(8,128)(2,1)}, u32[]{:S(2)}, u32[]{:S(2)}) collective-permute-start(bf16[8,64,512]{2,1,0:T(8,128)(2,1)} %all-to-all-done.1), channel_id=1, source_target_pairs={{0,1},{1,0},{2,3},{3,2},{4,5},{5,4},{6,7},{7,6},{8,9},{9,8},{10,11... | collective-permute-start | bytes 1572872 | tf_op jit(solution)/shard_map/ppermute | solution.py:253
  163.2 8.6 %collective-permute-start.40 = (bf16[256,128]{1,0:T(8,128)(2,1)S(1)}, bf16[256,128]{1,0:T(8,128)(2,1)S(1)}, u32[]{:S(2)}, u32[]{:S(2)}) collective-permute-start(bf16[256,128]{1,0:T(8,128)(2,1)S(1)} %add_convert_fusion.20), channel_id=1, source_target_pairs={{0,4},{8,0},{16,8},{24,16},{28,24},{20,28},{12,20},{4,12},{1,5},{9... | collective-permute-start | bytes 196616 | tf_op jit(solution)/shard_map/ppermute | solution.py:230
  166.1 7.8 %collective-permute-start.33 = (bf16[128,256]{1,0:T(8,128)(2,1)S(1)}, bf16[128,256]{1,0:T(8,128)(2,1)S(1)}, u32[]{:S(2)}, u32[]{:S(2)}) collective-permute-start(bf16[128,256]{1,0:T(8,128)(2,1)S(1)} %add_convert_fusion.26), channel_id=1, source_target_pairs={{0,4},{8,0},{16,8},{24,16},{28,24},{20,28},{12,20},{4,12},{1,5},{9... | collective-permute-start | bytes 196616 | tf_op jit(solution)/shard_map/ppermute | solution.py:230
  168.1 6.5 %collective-permute-start.19 = (bf16[128,256]{1,0:T(8,128)(2,1)S(1)}, bf16[128,256]{1,0:T(8,128)(2,1)S(1)}, u32[]{:S(2)}, u32[]{:S(2)}) collective-permute-start(bf16[128,256]{1,0:T(8,128)(2,1)S(1)} %add_convert_fusion.38), channel_id=1, source_target_pairs={{0,8},{8,16},{16,24},{24,28},{28,20},{20,12},{12,4},{4,0},{1,9},{9... | collective-permute-start | bytes 196616 | tf_op jit(solution)/shard_map/ppermute | solution.py:230
  170.6 5.2 %collective-permute-start.26 = (bf16[128,256]{1,0:T(8,128)(2,1)S(1)}, bf16[128,256]{1,0:T(8,128)(2,1)S(1)}, u32[]{:S(2)}, u32[]{:S(2)}) collective-permute-start(bf16[128,256]{1,0:T(8,128)(2,1)S(1)} %add_convert_fusion.32), channel_id=1, source_target_pairs={{0,8},{8,16},{16,24},{24,28},{28,20},{20,12},{12,4},{4,0},{1,9},{9... | collective-permute-start | bytes 196616 | tf_op jit(solution)/shard_map/ppermute | solution.py:230
  171.8 49.2 %collective-permute-start.55 = (bf16[1024,128]{1,0:T(8,128)(2,1)S(1)}, bf16[1024,128]{1,0:T(8,128)(2,1)S(1)}, u32[]{:S(2)}, u32[]{:S(2)}) collective-permute-start(bf16[1024,128]{1,0:T(8,128)(2,1)S(1)} %add_convert_fusion.3), channel_id=1, source_target_pairs={{0,4},{8,0},{16,8},{24,16},{28,24},{20,28},{12,20},{4,12},{1,5},{9... | collective-permute-start | bytes 786440 | tf_op jit(solution)/shard_map/ppermute | solution.py:230
  173.9 7.0 %collective-permute-start.41 = (bf16[256,128]{1,0:T(8,128)(2,1)S(1)}, bf16[256,128]{1,0:T(8,128)(2,1)S(1)}, u32[]{:S(2)}, u32[]{:S(2)}) collective-permute-start(bf16[256,128]{1,0:T(8,128)(2,1)S(1)} %add_convert_fusion.19), channel_id=1, source_target_pairs={{0,4},{8,0},{16,8},{24,16},{28,24},{20,28},{12,20},{4,12},{1,5},{9... | collective-permute-start | bytes 196616 | tf_op jit(solution)/shard_map/ppermute | solution.py:230
  174.6 7.0 %collective-permute-start.34 = (bf16[128,256]{1,0:T(8,128)(2,1)S(1)}, bf16[128,256]{1,0:T(8,128)(2,1)S(1)}, u32[]{:S(2)}, u32[]{:S(2)}) collective-permute-start(bf16[128,256]{1,0:T(8,128)(2,1)S(1)} %add_convert_fusion.25), channel_id=1, source_target_pairs={{0,4},{8,0},{16,8},{24,16},{28,24},{20,28},{12,20},{4,12},{1,5},{9... | collective-permute-start | bytes 196616 | tf_op jit(solution)/shard_map/ppermute | solution.py:230
  175.9 7.3 %collective-permute-start.20 = (bf16[128,256]{1,0:T(8,128)(2,1)S(1)}, bf16[128,256]{1,0:T(8,128)(2,1)S(1)}, u32[]{:S(2)}, u32[]{:S(2)}) collective-permute-start(bf16[128,256]{1,0:T(8,128)(2,1)S(1)} %add_convert_fusion.37), channel_id=1, source_target_pairs={{0,8},{8,16},{16,24},{24,28},{28,20},{20,12},{12,4},{4,0},{1,9},{9... | collective-permute-start | bytes 196616 | tf_op jit(solution)/shard_map/ppermute | solution.py:230
  180.9 5.0 %collective-permute-start.27 = (bf16[128,256]{1,0:T(8,128)(2,1)S(1)}, bf16[128,256]{1,0:T(8,128)(2,1)S(1)}, u32[]{:S(2)}, u32[]{:S(2)}) collective-permute-start(bf16[128,256]{1,0:T(8,128)(2,1)S(1)} %add_convert_fusion.31), channel_id=1, source_target_pairs={{0,8},{8,16},{16,24},{24,28},{28,20},{20,12},{12,4},{4,0},{1,9},{9... | collective-permute-start | bytes 196616 | tf_op jit(solution)/shard_map/ppermute | solution.py:230
  181.6 39.3 %collective-permute-start.13 = (bf16[256,512]{1,0:T(8,128)(2,1)S(1)}, bf16[256,512]{1,0:T(8,128)(2,1)S(1)}, u32[]{:S(2)}, u32[]{:S(2)}) collective-permute-start(bf16[256,512]{1,0:T(8,128)(2,1)S(1)} %fusion.75), channel_id=1, source_target_pairs={{0,2},{1,3},{2,0},{3,1},{4,6},{5,7},{6,4},{7,5},{8,10},{9,11},{10,... | collective-permute-start | bytes 786440 | tf_op jit(solution)/shard_map/ppermute | solution.py:253
  183.1 41.2 %collective-permute-start.48 = (bf16[128,1024]{1,0:T(8,128)(2,1)S(1)}, bf16[128,1024]{1,0:T(8,128)(2,1)S(1)}, u32[]{:S(2)}, u32[]{:S(2)}) collective-permute-start(bf16[128,1024]{1,0:T(8,128)(2,1)S(1)} %add_convert_fusion.9), channel_id=1, source_target_pairs={{0,8},{8,16},{16,24},{24,28},{28,20},{20,12},{12,4},{4,0},{1,9},{9... | collective-permute-start | bytes 786440 | tf_op jit(solution)/shard_map/ppermute | solution.py:230
  185.9 4.3 %collective-permute-start.42 = (bf16[256,128]{1,0:T(8,128)(2,1)S(1)}, bf16[256,128]{1,0:T(8,128)(2,1)S(1)}, u32[]{:S(2)}, u32[]{:S(2)}) collective-permute-start(bf16[256,128]{1,0:T(8,128)(2,1)S(1)} %add_convert_fusion.18), channel_id=1, source_target_pairs={{0,4},{8,0},{16,8},{24,16},{28,24},{20,28},{12,20},{4,12},{1,5},{9... | collective-permute-start | bytes 196616 | tf_op jit(solution)/shard_map/ppermute | solution.py:230
  220.9 4.9 %collective-permute-start.14 = (bf16[256,512]{1,0:T(8,128)(2,1)S(1)}, bf16[256,512]{1,0:T(8,128)(2,1)S(1)}, u32[]{:S(2)}, u32[]{:S(2)}) collective-permute-start(bf16[256,512]{1,0:T(8,128)(2,1)S(1)} %add_convert_fusion.13), channel_id=1, source_target_pairs={{0,1},{1,0},{2,3},{3,2},{4,5},{5,4},{6,7},{7,6},{8,9},{9,8},{10,11... | collective-permute-start | bytes 786440 | tf_op jit(solution)/shard_map/ppermute | solution.py:253
  222.7 9.8 %collective-permute-start.56 = (bf16[1024,128]{1,0:T(8,128)(2,1)}, bf16[1024,128]{1,0:T(8,128)(2,1)S(1)}, u32[]{:S(2)}, u32[]{:S(2)}) collective-permute-start(bf16[1024,128]{1,0:T(8,128)(2,1)} %add_convert_fusion.2), channel_id=1, source_target_pairs={{0,4},{8,0},{16,8},{24,16},{28,24},{20,28},{12,20},{4,12},{1,5},{9... | collective-permute-start | bytes 786440 | tf_op jit(solution)/shard_map/ppermute | solution.py:230
  225.3 10.3 %collective-permute-start.49 = (bf16[128,1024]{1,0:T(8,128)(2,1)S(1)}, bf16[128,1024]{1,0:T(8,128)(2,1)S(1)}, u32[]{:S(2)}, u32[]{:S(2)}) collective-permute-start(bf16[128,1024]{1,0:T(8,128)(2,1)S(1)} %add_convert_fusion.8), channel_id=1, source_target_pairs={{0,8},{8,16},{16,24},{24,28},{28,20},{20,12},{12,4},{4,0},{1,9},{9... | collective-permute-start | bytes 786440 | tf_op jit(solution)/shard_map/ppermute | solution.py:230
  228.5 24.3 %all-to-all-start.3 = ((bf16[8,80,512]{2,1,0:T(8,128)(2,1)}), bf16[8,80,512]{2,1,0:T(8,128)(2,1)S(1)}, u32[]{:S(2)}, u32[]{:S(2)}) async-start(bf16[8,80,512]{2,1,0:T(8,128)(2,1)} %fusion.72), calls=%async_computation.3 | async-start | bytes 1310720 | tf_op jit(solution)/shard_map/all_to_all | solution.py:447
  233.6 17.4 %collective-permute-start.57 = (bf16[1024,128]{1,0:T(8,128)(2,1)S(1)}, bf16[1024,128]{1,0:T(8,128)(2,1)S(1)}, u32[]{:S(2)}, u32[]{:S(2)}) collective-permute-start(bf16[1024,128]{1,0:T(8,128)(2,1)S(1)} %add_convert_fusion.1), channel_id=1, source_target_pairs={{0,4},{8,0},{16,8},{24,16},{28,24},{20,28},{12,20},{4,12},{1,5},{9... | collective-permute-start | bytes 786440 | tf_op jit(solution)/shard_map/ppermute | solution.py:230
  236.7 16.3 %collective-permute-start.50 = (bf16[128,1024]{1,0:T(8,128)(2,1)S(1)}, bf16[128,1024]{1,0:T(8,128)(2,1)S(1)}, u32[]{:S(2)}, u32[]{:S(2)}) collective-permute-start(bf16[128,1024]{1,0:T(8,128)(2,1)S(1)} %add_convert_fusion.7), channel_id=1, source_target_pairs={{0,8},{8,16},{16,24},{24,28},{28,20},{20,12},{12,4},{4,0},{1,9},{9... | collective-permute-start | bytes 786440 | tf_op jit(solution)/shard_map/ppermute | solution.py:230
  (63 other events, 489.3 us)

commit v3 on v2

--- a/solution.py
+++ b/solution.py
@@ -223,17 +223,22 @@
     return jnp.where(place < size // 2, 2 * place, 2 * (size - place) - 1)
 
 
-def ring_permute(values, direction):
+def ring_permute(values):
     order = ring_order(lax.axis_size("seq"))
-    size = len(order)
-    pairs = [(order[i], order[(i + direction) % size]) for i in range(size)]
-    return lax.ppermute(values, "seq", pairs)
-
-
-def ring_scatter(whole, axis, direction):
+    size, width = len(order), lax.axis_size("tp")
+    pairs = []
+    for i in range(size):
+        for t in range(width):
+            after = (i + 1 - 2 * (t % 2)) % size
+            pairs.append((order[i] * width + t, order[after] * width + t))
+    return lax.ppermute(values, ("seq", "tp"), pairs)
+
+
+def ring_scatter(whole, axis, core):
     size = lax.axis_size("seq")
     place = ring_place(lax.axis_index("seq"), size)
     width = whole.shape[axis] // size
+    direction = 1 - 2 * core
 
     def chunk(k):
         owner = ring_owner(place + size - direction * (1 + k), size)
@@ -241,7 +246,7 @@
 
     total = chunk(0)
     for k in range(1, size):
-        moved = ring_permute(total, direction)
+        moved = ring_permute(total)
         total = moved.astype(jnp.float32) + chunk(k).astype(jnp.float32)
         if k < size - 1:
             total = total.astype(jnp.bfloat16)
@@ -385,8 +390,14 @@
         )
         return product.astype(bf16)
 
-    grad_up = ring_scatter(outer(mlp_input, grad_pre), 0, 1)
-    grad_down = ring_scatter(outer(hidden, grad_mlp), 1, -1)
+    mlp_pairs = lax.dot_general(
+        jnp.stack([mlp_input, grad_mlp]),
+        jnp.stack([grad_pre, hidden]),
+        (((1,), (1,)), ((0,), (0,))),
+        preferred_element_type=f32,
+    )
+    mlp_grads = ring_scatter(mlp_pairs.astype(bf16), 1, core)
+    grad_up, grad_down = mlp_grads[0], mlp_grads[1].T
 
     weighted = grad_mlp_input * gain_second
     grad_residual = factor_second * weighted - residual * factor_second**3 * jnp.mean(
@@ -418,14 +429,14 @@
         ),
         core,
     )
-    grad_qkv = jnp.stack(
-        [
-            ring_scatter(outer(attn_input, grad_parts[c]), 0, -1 if c == 2 else 1)
-            for c in range(3)
-        ],
-        axis=1,
-    )
-    grad_out = ring_scatter(outer(mixed, grad_attn), 1, -1)
+    grad_rows_flat = jnp.concatenate(grad_parts, axis=1)
+    attn_pairs = jnp.concatenate(
+        [outer(attn_input, grad_rows_flat), outer(grad_attn, mixed)], axis=1
+    )
+    attn_grads = ring_scatter(attn_pairs, 0, core)
+    split = 3 * mixed.shape[1]
+    grad_qkv = attn_grads[:, :split].reshape(-1, 3, mixed.shape[1])
+    grad_out = attn_grads[:, split:].T
 
     branch = attn_out + mlp_out
     update = (gating * branch).astype(bf16)

time: 267 us -> 211 us (0.79); the launches traced: 262 us -> 210 us
  starting transfers between devices: 77.2 us -> 52.2 us
  waiting for transfers between devices: 88.2 us -> 68.3 us
  other arithmetic: 46.3 us -> 36.2 us
  local copies, waits for them, and re-layouts: 2.44 us -> 9.45 us
  matrix products: 46.4 us -> 41.8 us
    ppermute x42 -> x14, waiting for transfers between devices: 58.6 us -> 22.6 us  [ring_permute(): return lax.ppermute(values, ('seq', 'tp'), pairs)]
    ppermute x42 -> x14, starting transfers between devices: 48.4 us -> 24.2 us  [ring_permute(): return lax.ppermute(values, ('seq', 'tp'), pairs)]
    ppermute x16, waiting for transfers between devices: 11 us -> 24.4 us  [tp_permute(): return lax.ppermute(values, 'tp', [(i, i ^ mask) for i in range(size)])]
    dot_general x6 -> x2, matrix products: 5.02 us -> 0.97 us  [outer(): lax.dot_general(left, right, (((0,), (0,)), ((), ())), preferred_element_...]
    unnamed x99 -> x113, local copies, waits for them, and re-layouts: 0.68 us -> 4.28 us
    dot_general x3, matrix products: 1.06 us -> 4.3 us  [on_device_whole(): lax.dot_general(grad_parts[c], weights[c], (((1,), (1,)), ((), ())), pref...]
    add x3 -> x2, other arithmetic: 4.29 us -> 1.44 us  [ring_scatter(): total = moved.astype(jnp.float32) + chunk(k).astype(jnp.float32)]
    convert_element_type x36 -> x12, other arithmetic: 14.9 us -> 13.6 us  [ring_scatter(): total = total.astype(jnp.bfloat16)]
  transfers between devices with their start and end apart: 62 -> 34, of which waited for: 28 -> 15; matrix products, arithmetic and copies ran while one was open for 27% -> 32% of each run, Pallas kernels for 0% -> 0%
where the time goes in v3:
time: 211 us; the launch traced here: 210 us
  waiting for transfers between devices  68.3 us (32%)
  starting transfers between devices  52.2 us (25%)
  matrix products  41.8 us (20%)
  other arithmetic  36.2 us (17%)
  local copies, waits for them, and re-layouts  9.45 us (4%)
    ppermute x16, waiting for transfers between devices, tp_permute(): return lax.ppermute(values, 'tp', [(i, i ^ mask) for i in range(size)])  24.4 us
    ppermute x14, starting transfers between devices, ring_permute(): return lax.ppermute(values, ('seq', 'tp'), pairs)  24.2 us
    ppermute x14, waiting for transfers between devices, ring_permute(): return lax.ppermute(values, ('seq', 'tp'), pairs)  22.6 us
    all_to_all x2, waiting for transfers between devices, fetch(): own = from_owners(lax.all_to_all(own, 'seq', 0, 0, tiled=True), share)  21.3 us
    convert_element_type x12, other arithmetic, ring_scatter(): total = total.astype(jnp.bfloat16)  13.6 us
    dot_general x2, matrix products, spread(): jnp.einsum('sqc,sqd->scd', table, routed_rows, preferred_element_type=jnp...  12 us
    all_to_all x2, starting transfers between devices, fetch(): own = from_owners(lax.all_to_all(own, 'seq', 0, 0, tiled=True), share)  11.4 us
    ppermute x16, starting transfers between devices, tp_permute(): return lax.ppermute(values, 'tp', [(i, i ^ mask) for i in range(size)])  8.78 us
  transfers between devices with their start and end apart: 34, of which 15 were waited for; matrix products, arithmetic and copies ran while one was open for 32% of the time, Pallas kernels for 0%

profile of v3, /device:TPU:0, one launch (start us, length us, event | category | flops | bytes accessed | tf_op | source)
XLA Modules:
  0.0 209.7 jit_solution(9762333416073536468)
XLA Ops:
  1.6 2.9 %fusion.16 = bf16[8,64,512]{2,1,0:T(8,128)(2,1)} fusion(bf16[8,256,1024]{2,1,0:T(8,128)(2,1)} %param.11, s32[]{:T(128)S(6)} %select_n.275, s32[8,64]{1,0:T(8,128)S(1)} %fusion.127), kind=kOutput, calls=%fused_computation.59 | convolution fusion | flops 134610944 | bytes 2623492 | tf_op jit(solution)/shard_map/sqc,scd->sqd/dot_general | solution.py:28
  4.5 7.3 %all-to-all-start = ((bf16[8,64,512]{2,1,0:T(8,128)(2,1)}), bf16[8,64,512]{2,1,0:T(8,128)(2,1)S(1)}, u32[]{:S(2)}, u32[]{:S(2)}) async-start(bf16[8,64,512]{2,1,0:T(8,128)(2,1)} %fusion.16), calls=%async_computation | async-start | bytes 1048576 | tf_op jit(solution)/shard_map/all_to_all | solution.py:338
  11.8 1.5 fusion.122
  13.4 12.9 %all-to-all-done = bf16[8,64,512]{2,1,0:T(8,128)(2,1)S(1)} async-done(((bf16[8,64,512]{2,1,0:T(8,128)(2,1)}), bf16[8,64,512]{2,1,0:T(8,128)(2,1)S(1)}, u32[]{:S(2)}, u32[]{:S(2)}) %all-to-all-start) | async-done | bytes 524320 | tf_op jit(solution)/shard_map/all_to_all | solution.py:338
  26.4 2.6 %fusion.130 = s32[1,256]{1,0:T(1,128)S(1)} fusion(s32[8,256]{1,0:T(8,128)} %param.13, s32[]{:T(128)S(6)} %select_n.277, s32[]{:T(128)} %get-tuple-element.35, s32[]{:T(128)} %get-tuple-element.34, s32[]{:T(128)} %get-tuple-element.33), kind=kLoop, calls=%fused_computation.244 | loop fusion | flops 2048 | bytes 2064 | tf_op jit(solution)/shard_map/add | solution.py:326
  30.1 2.2 %fusion.27 = bf16[3,256,256]{1,2,0:T(8,128)(2,1)S(1)} fusion(f32[1024]{0:T(1024)S(1)} %convert_element_type.420, f32[256]{0:T(256)S(1)} %get-tuple-element.47, bf16[1024,3,256]{2,0,1:T(8,128)(2,1)} %param.15, bf16[256,512]{1,0:T(8,128)(2,1)S(1)} %collective-permute-done, bf16[256,512]{1,0:T(8,128)(2,1)S(1)} %bitcast.106, pred[]{:T(512)S(6)} %eq.79), kind=kOutput, calls=%fused_computation.67 | convolution fusion | flops 406257664 | bytes 2495489 | tf_op jit(solution)/shard_map/rd,cdh->crh/dot_general | solution.py:353
  33.9 1.7 convolution_convert_fusion.8
  37.8 1.6 collective-permute-start.2
  39.4 7.1 %collective-permute-done.2 = bf16[256,512]{1,0:T(8,128)(2,1)S(1)} collective-permute-done((bf16[256,512]{1,0:T(8,128)(2,1)S(1)}, bf16[256,512]{1,0:T(8,128)(2,1)S(1)}, u32[]{:S(2)}, u32[]{:S(2)}) %collective-permute-start.2) | collective-permute-done | bytes 262176 | tf_op jit(solution)/shard_map/ppermute | solution.py:258
  48.0 4.1 %all-to-all-start.2 = ((bf16[8,64,512]{2,1,0:T(8,128)(2,1)}), bf16[8,64,512]{2,1,0:T(8,128)(2,1)}, u32[]{:S(2)}, u32[]{:S(2)}) async-start(bf16[8,64,512]{2,1,0:T(8,128)(2,1)} %fusion.19), calls=%async_computation.2 | async-start | bytes 1048576 | tf_op jit(solution)/shard_map/all_to_all | solution.py:338
  53.7 2.4 %fusion.80 = f32[256,1024]{1,0:T(8,128)S(1)} fusion(bf16[1024,1024]{1,0:T(8,128)(2,1)} %param.18, f32[1024]{0:T(1024)S(1)} %convert_element_type.441, f32[256]{0:T(256)S(1)} %get-tuple-element.49, bf16[256,512]{1,0:T(8,128)(2,1)S(1)} %collective-permute-done.3, bf16[256,512]{1,0:T(8,128)(2,1)S(1)} %add_convert_fusion.16, pred[]{:T(512)S(6)} %eq.79, ...), kind=kOutput, calls=%fused_computation.140 | convolution fusion | flops 543162368 | bytes 4199425 | tf_op jit(solution)/shard_map/dot_general | solution.py:375
  56.1 1.8 fusion.148
  59.2 8.4 %all-to-all-done.2 = bf16[8,64,512]{2,1,0:T(8,128)(2,1)} async-done(((bf16[8,64,512]{2,1,0:T(8,128)(2,1)}), bf16[8,64,512]{2,1,0:T(8,128)(2,1)}, u32[]{:S(2)}, u32[]{:S(2)}) %all-to-all-start.2) | async-done | bytes 524320 | tf_op jit(solution)/shard_map/all_to_all | solution.py:338
  69.9 1.6 collective-permute-start.5
  72.9 5.0 %collective-permute-done.5 = bf16[256,512]{1,0:T(8,128)(2,1)S(1)} collective-permute-done((bf16[256,512]{1,0:T(8,128)(2,1)S(1)}, bf16[256,512]{1,0:T(8,128)(2,1)S(1)}, u32[]{:S(2)}, u32[]{:S(2)}) %collective-permute-start.5) | collective-permute-done | bytes 262176 | tf_op jit(solution)/shard_map/ppermute | solution.py:258
  85.6 1.6 collective-permute-start.10
  87.5 6.8 %collective-permute-done.10 = bf16[256,512]{1,0:T(8,128)(2,1)S(1)} collective-permute-done((bf16[256,512]{1,0:T(8,128)(2,1)S(1)}, bf16[256,512]{1,0:T(8,128)(2,1)S(1)}, u32[]{:S(2)}, u32[]{:S(2)}) %collective-permute-start.10) | collective-permute-done | bytes 262176 | tf_op jit(solution)/shard_map/ppermute | solution.py:258
  95.9 4.3 %all-to-all-start.1 = ((bf16[8,64,512]{2,1,0:T(8,128)(2,1)}), bf16[8,64,512]{2,1,0:T(8,128)(2,1)}, u32[]{:S(2)}, u32[]{:S(2)}) async-start(bf16[8,64,512]{2,1,0:T(8,128)(2,1)} %fusion.79), calls=%async_computation.1 | async-start | bytes 1048576 | tf_op jit(solution)/shard_map/all_to_all | solution.py:456
  100.3 2.0 add_convert_fusion.6
  102.3 1.9 collective-permute-start.24
  106.7 2.3 %convolution_convert_fusion.4 = bf16[4,64,256]{2,1,0:T(8,128)(2,1)} fusion(bf16[256,4,64]{0,2,1:T(8,128)(2,1)S(1)} %bitcast.135, f32[4,256]{1,0:T(4,128)} %copy-done.53, bf16[256,4,64]{0,2,1:T(8,128)(2,1)S(1)} %bitcast.143, bf16[256,4,64]{0,2,1:T(8,128)(2,1)S(1)} %bitcast.147, pred[256,256]{0,1:T(8,128)(4,1)} %copy-done.31), kind=kOutput, calls=%fused_computation.68 | convolution fusion | flops 68486400 | bytes 593920 | tf_op jit(solution)/shard_map/hqk,qhe->khe/dot_general | solution.py:421
  109.4 2.0 convolution_convert_fusion.6
  111.4 2.0 convolution_convert_fusion.5
  119.1 1.5 collective-permute-start.16
  120.6 2.2 %add_convert_fusion.5 = bf16[2,128,1024]{2,1,0:T(8,128)(2,1)} fusion(bf16[2,128,1024]{2,1,0:T(8,128)(2,1)} %collective-permute-done.24, bf16[2,1024,1024]{2,1,0:T(8,128)(2,1)} %copy-done.2, s32[]{:T(128)S(6)} %select_n.308), kind=kLoop, calls=%fused_computation.123 | loop fusion | flops 1048576 | bytes 1572868 | tf_op jit(solution)/shard_map/convert_element_type | solution.py:252
  125.1 1.5 collective-permute-start.13
  129.5 3.2 %collective-permute-done.13 = bf16[256,512]{1,0:T(8,128)(2,1)} collective-permute-done((bf16[256,512]{1,0:T(8,128)(2,1)}, bf16[256,512]{1,0:T(8,128)(2,1)}, u32[]{:S(2)}, u32[]{:S(2)}) %collective-permute-start.13) | collective-permute-done | bytes 262176 | tf_op jit(solution)/shard_map/ppermute | solution.py:258
  136.2 1.5 collective-permute-start.18
  137.7 2.2 %add_convert_fusion.4 = bf16[2,128,1024]{2,1,0:T(8,128)(2,1)} fusion(bf16[2,128,1024]{2,1,0:T(8,128)(2,1)} %collective-permute-done.25, bf16[2,1024,1024]{2,1,0:T(8,128)(2,1)} %copy-done.2, s32[]{:T(128)S(6)} %select_n.311), kind=kLoop, calls=%fused_computation.122 | loop fusion | flops 1048576 | bytes 1572868 | tf_op jit(solution)/shard_map/convert_element_type | solution.py:252
  139.9 1.5 collective-permute-start.26
  142.7 1.5 collective-permute-start.19
  145.5 6.7 %collective-permute-done.19 = bf16[128,1024]{0,1:T(8,128)(2,1)S(1)} collective-permute-done((bf16[128,1024]{0,1:T(8,128)(2,1)S(1)}, bf16[128,1024]{0,1:T(8,128)(2,1)S(1)}, u32[]{:S(2)}, u32[]{:S(2)}) %collective-permute-start.19) | collective-permute-done | bytes 262176 | tf_op jit(solution)/shard_map/ppermute | solution.py:234
  152.3 1.5 collective-permute-start.20
  153.8 4.8 %collective-permute-done.20 = bf16[128,1024]{0,1:T(8,128)(2,1)S(1)} collective-permute-done((bf16[128,1024]{0,1:T(8,128)(2,1)S(1)}, bf16[128,1024]{0,1:T(8,128)(2,1)S(1)}, u32[]{:S(2)}, u32[]{:S(2)}) %collective-permute-start.20) | collective-permute-done | bytes 262176 | tf_op jit(solution)/shard_map/ppermute | solution.py:234
  158.8 1.5 collective-permute-start.21
  161.2 3.5 %all-to-all-start.3 = ((bf16[8,80,512]{2,1,0:T(8,128)(2,1)}), bf16[8,80,512]{2,1,0:T(8,128)(2,1)S(1)}, u32[]{:S(2)}, u32[]{:S(2)}) async-start(bf16[8,80,512]{2,1,0:T(8,128)(2,1)} %fusion.78), calls=%async_computation.3 | async-start | bytes 1310720 | tf_op jit(solution)/shard_map/all_to_all | solution.py:458
  164.7 1.5 add_convert_fusion.3
  166.3 2.0 collective-permute-start.27
  168.4 1.7 collective-permute-start.22
  170.1 5.0 %add_convert_fusion = bf16[8,256,1024]{2,1,0:T(8,128)(2,1)} fusion(bf16[8,256,1024]{2,1,0:T(8,128)(2,1)S(1)} %copy-done.4, bf16[8,64,512]{2,1,0:T(8,128)(2,1)} %collective-permute-done.7, bf16[8,64,512]{2,1,0:T(8,128)(2,1)} %all-to-all-done.1, pred[]{:T(512)S(6)} %eq.79, s32[8,64]{1,0:T(8,128)S(1)} %fusion.127), kind=kOutput, calls=%fused_computation.3 | convolution fusion | flops 279576576 | bytes 9439233 | tf_op jit(solution)/shard_map/sqc,sqd->scd/dot_general | solution.py:32
  175.1 5.3 %collective-permute-done.27 = bf16[2,128,1024]{2,1,0:T(8,128)(2,1)S(1)} collective-permute-done((bf16[2,128,1024]{2,1,0:T(8,128)(2,1)S(1)}, bf16[2,128,1024]{2,1,0:T(8,128)(2,1)S(1)}, u32[]{:S(2)}, u32[]{:S(2)}) %collective-permute-start.27) | collective-permute-done | bytes 524320 | tf_op jit(solution)/shard_map/ppermute | solution.py:234
  180.4 2.0 add_convert_fusion.2
  182.4 4.0 %collective-permute-start.28 = (bf16[2,128,1024]{2,1,0:T(8,128)(2,1)}, bf16[2,128,1024]{2,1,0:T(8,128)(2,1)}, u32[]{:S(2)}, u32[]{:S(2)}) collective-permute-start(bf16[2,128,1024]{2,1,0:T(8,128)(2,1)} %add_convert_fusion.2), channel_id=1, source_target_pairs={{0,8},{1,5},{2,10},{3,7},{8,16},{9,1},{10,18},{11,3},{16,24},{17,9... | collective-permute-start | bytes 1572872 | tf_op jit(solution)/shard_map/ppermute | solution.py:234
  188.3 1.6 slice_bitcast_fusion.8
  190.5 3.0 %collective-permute-done.28 = bf16[2,128,1024]{2,1,0:T(8,128)(2,1)} collective-permute-done((bf16[2,128,1024]{2,1,0:T(8,128)(2,1)}, bf16[2,128,1024]{2,1,0:T(8,128)(2,1)}, u32[]{:S(2)}, u32[]{:S(2)}) %collective-permute-start.28) | collective-permute-done | bytes 524320 | tf_op jit(solution)/shard_map/ppermute | solution.py:234
  194.9 2.5 %collective-permute-start.29 = (bf16[2,128,1024]{2,1,0:T(8,128)(2,1)S(1)}, bf16[2,128,1024]{2,1,0:T(8,128)(2,1)S(1)}, u32[]{:S(2)}, u32[]{:S(2)}) collective-permute-start(bf16[2,128,1024]{2,1,0:T(8,128)(2,1)S(1)} %add_convert_fusion.1), channel_id=1, source_target_pairs={{0,8},{1,5},{2,10},{3,7},{8,16},{9,1},{10,18},{11,3},{16,24},{17,9... | collective-permute-start | bytes 1572872 | tf_op jit(solution)/shard_map/ppermute | solution.py:234
  197.4 7.0 %convert_add_fusion = f32[8,256,1024]{2,1,0:T(8,128)} fusion(bf16[8,256,1024]{2,1,0:T(8,128)(2,1)} %param.21, bf16[8,64,512]{2,1,0:T(8,128)(2,1)S(1)} %collective-permute-done.15, bf16[8,64,512]{2,1,0:T(8,128)(2,1)S(1)} %slice.204, pred[]{:T(512)S(6)} %eq.79, s32[8,64]{1,0:T(8,128)S(1)} %fusion.127), kind=kOutput, calls=%fused_computation.2 | convolution fusion | flops 277479424 | bytes 13633537 | tf_op jit(solution)/shard_map/sqc,sqd->scd/dot_general | solution.py:32
  207.6 2.0 copy.36
  (226 shorter events, 50.9 us)
Async XLA Ops:
  0.6 55.5 %copy-start = (bf16[1024,1024]{1,0:T(8,128)(2,1)S(1)}, bf16[1024,1024]{1,0:T(8,128)(2,1)}, u32[]{:S(2)}) copy-start(bf16[1024,1024]{1,0:T(8,128)(2,1)} %param.19) | copy-start | bytes 6291460
  1.6 27.5 %copy-start.50 = (bf16[1024]{0:T(1024)(128)(2,1)S(1)}, bf16[1024]{0:T(1024)(128)(2,1)}, u32[]{:S(2)}) copy-start(bf16[1024]{0:T(1024)(128)(2,1)} %param.14) | copy-start | bytes 6148
  4.5 21.8 %all-to-all-start = ((bf16[8,64,512]{2,1,0:T(8,128)(2,1)}), bf16[8,64,512]{2,1,0:T(8,128)(2,1)S(1)}, u32[]{:S(2)}, u32[]{:S(2)}) async-start(bf16[8,64,512]{2,1,0:T(8,128)(2,1)} %fusion.16), calls=%async_computation | async-start | bytes 1048576 | tf_op jit(solution)/shard_map/all_to_all | solution.py:338
  26.4 2.9 %collective-permute-start = (bf16[256,512]{1,0:T(8,128)(2,1)S(1)}, bf16[256,512]{1,0:T(8,128)(2,1)S(1)}, u32[]{:S(2)}, u32[]{:S(2)}) collective-permute-start(bf16[256,512]{1,0:T(8,128)(2,1)S(1)} %bitcast.104), channel_id=1, source_target_pairs={{0,1},{1,0},{2,3},{3,2},{4,5},{5,4},{6,7},{7,6},{8,9},{9,8},{10,11... | collective-permute-start | bytes 786440 | tf_op jit(solution)/shard_map/ppermute | solution.py:258
  35.6 11.1 %copy-start.3 = (bf16[8,256,1024]{2,1,0:T(8,128)(2,1)S(1)}, bf16[8,256,1024]{2,1,0:T(8,128)(2,1)}, u32[]{:S(2)}) copy-start(bf16[8,256,1024]{2,1,0:T(8,128)(2,1)} %param.21) | copy-start | bytes 12582916
  36.0 1.7 collective-permute-start.1
  37.8 14.3 %copy-start.51 = (bf16[1024]{0:T(1024)(128)(2,1)S(1)}, bf16[1024]{0:T(1024)(128)(2,1)}, u32[]{:S(2)}) copy-start(bf16[1024]{0:T(1024)(128)(2,1)} %param.17) | copy-start | bytes 6148
  37.8 14.3 %copy-start.52 = (bf16[1024]{0:T(1024)(128)(2,1)S(1)}, bf16[1024]{0:T(1024)(128)(2,1)}, u32[]{:S(2)}) copy-start(bf16[1024]{0:T(1024)(128)(2,1)} %param.20) | copy-start | bytes 6148
  37.8 8.7 %collective-permute-start.2 = (bf16[256,512]{1,0:T(8,128)(2,1)S(1)}, bf16[256,512]{1,0:T(8,128)(2,1)S(1)}, u32[]{:S(2)}, u32[]{:S(2)}) collective-permute-start(bf16[256,512]{1,0:T(8,128)(2,1)S(1)} %fusion.93), channel_id=1, source_target_pairs={{0,2},{1,3},{2,0},{3,1},{4,6},{5,7},{6,4},{7,5},{8,10},{9,11},{10,... | collective-permute-start | bytes 786440 | tf_op jit(solution)/shard_map/ppermute | solution.py:258
  46.6 5.6 %collective-permute-start.3 = (bf16[256,512]{1,0:T(8,128)(2,1)S(1)}, bf16[256,512]{1,0:T(8,128)(2,1)S(1)}, u32[]{:S(2)}, u32[]{:S(2)}) collective-permute-start(bf16[256,512]{1,0:T(8,128)(2,1)S(1)} %add_convert_fusion.16), channel_id=1, source_target_pairs={{0,1},{1,0},{2,3},{3,2},{4,5},{5,4},{6,7},{7,6},{8,9},{9,8},{10,11... | collective-permute-start | bytes 786440 | tf_op jit(solution)/shard_map/ppermute | solution.py:258
  48.0 19.6 %all-to-all-start.2 = ((bf16[8,64,512]{2,1,0:T(8,128)(2,1)}), bf16[8,64,512]{2,1,0:T(8,128)(2,1)}, u32[]{:S(2)}, u32[]{:S(2)}) async-start(bf16[8,64,512]{2,1,0:T(8,128)(2,1)} %fusion.19), calls=%async_computation.2 | async-start | bytes 1048576 | tf_op jit(solution)/shard_map/all_to_all | solution.py:338
  58.7 9.8 %collective-permute-start.4 = (bf16[256,512]{1,0:T(8,128)(2,1)}, bf16[256,512]{1,0:T(8,128)(2,1)S(1)}, u32[]{:S(2)}, u32[]{:S(2)}) collective-permute-start(bf16[256,512]{1,0:T(8,128)(2,1)} %slice_select_fusion.8), channel_id=1, source_target_pairs={{0,1},{1,0},{2,3},{3,2},{4,5},{5,4},{6,7},{7,6},{8,9},{9,8},{10,11... | collective-permute-start | bytes 786440 | tf_op jit(solution)/shard_map/ppermute | solution.py:258
  68.5 9.5 %copy-start.17 = (f32[256,1024]{1,0:T(8,128)S(1)}, f32[256,1024]{1,0:T(8,128)}, u32[]{:S(2)}) copy-start(f32[256,1024]{1,0:T(8,128)} %copy-done.16) | copy-start | bytes 3145732
  69.9 7.9 %collective-permute-start.5 = (bf16[256,512]{1,0:T(8,128)(2,1)S(1)}, bf16[256,512]{1,0:T(8,128)(2,1)S(1)}, u32[]{:S(2)}, u32[]{:S(2)}) collective-permute-start(bf16[256,512]{1,0:T(8,128)(2,1)S(1)} %fusion.91), channel_id=1, source_target_pairs={{0,2},{1,3},{2,0},{3,1},{4,6},{5,7},{6,4},{7,5},{8,10},{9,11},{10,... | collective-permute-start | bytes 786440 | tf_op jit(solution)/shard_map/ppermute | solution.py:258
  72.5 10.6 %copy-start.5 = (bf16[8,32,512]{2,1,0:T(8,128)(2,1)}, bf16[8,32,512]{2,1,0:T(8,128)(2,1)S(1)}, u32[]{:S(2)}) copy-start(bf16[8,32,512]{2,1,0:T(8,128)(2,1)S(1)} %slice_add_fusion) | copy-start | bytes 786436
  72.5 5.8 %collective-permute-start.8 = (bf16[256,512]{1,0:T(8,128)(2,1)S(1)}, bf16[256,512]{1,0:T(8,128)(2,1)S(1)}, u32[]{:S(2)}, u32[]{:S(2)}) collective-permute-start(bf16[256,512]{1,0:T(8,128)(2,1)S(1)} %bitcast.118), channel_id=1, source_target_pairs={{0,1},{1,0},{2,3},{3,2},{4,5},{5,4},{6,7},{7,6},{8,9},{9,8},{10,11... | collective-permute-start | bytes 786440 | tf_op jit(solution)/shard_map/ppermute | solution.py:258
  72.9 7.0 %copy-start.49 = (f32[256]{0:T(256)S(1)}, f32[256]{0:T(256)}, u32[]{:S(2)}) copy-start(f32[256]{0:T(256)} %get-tuple-element.32) | copy-start | bytes 3076
  77.9 1.6 collective-permute-start.6
  80.5 6.7 %copy-start.36 = (f32[256]{0:T(256)}, f32[256]{0:T(256)S(1)}, u32[]{:S(2)}) copy-start(f32[256]{0:T(256)S(1)} %get-tuple-element.37) | copy-start | bytes 3076
  82.9 2.6 %collective-permute-start.9 = (bf16[256,512]{1,0:T(8,128)(2,1)S(1)}, bf16[256,512]{1,0:T(8,128)(2,1)S(1)}, u32[]{:S(2)}, u32[]{:S(2)}) collective-permute-start(bf16[256,512]{1,0:T(8,128)(2,1)S(1)} %slice_select_fusion.6), channel_id=1, source_target_pairs={{0,1},{1,0},{2,3},{3,2},{4,5},{5,4},{6,7},{7,6},{8,9},{9,8},{10,11... | collective-permute-start | bytes 786440 | tf_op jit(solution)/shard_map/ppermute | solution.py:258
  85.5 14.8 %collective-permute-start.23 = (bf16[2,128,1024]{2,1,0:T(8,128)(2,1)}, bf16[2,128,1024]{2,1,0:T(8,128)(2,1)S(1)}, u32[]{:S(2)}, u32[]{:S(2)}) collective-permute-start(bf16[2,128,1024]{2,1,0:T(8,128)(2,1)} %constant_dynamic-slice_fusion), channel_id=1, source_target_pairs={{0,8},{1,5},{2,10},{3,7},{8,16},{9,1},{10,18},{11,3},{16,24},{17,9... | collective-permute-start | bytes 1572872 | tf_op jit(solution)/shard_map/ppermute | solution.py:234
  85.6 8.7 %collective-permute-start.10 = (bf16[256,512]{1,0:T(8,128)(2,1)S(1)}, bf16[256,512]{1,0:T(8,128)(2,1)S(1)}, u32[]{:S(2)}, u32[]{:S(2)}) collective-permute-start(bf16[256,512]{1,0:T(8,128)(2,1)S(1)} %fusion.89), channel_id=1, source_target_pairs={{0,2},{1,3},{2,0},{3,1},{4,6},{5,7},{6,4},{7,5},{8,10},{9,11},{10,... | collective-permute-start | bytes 786440 | tf_op jit(solution)/shard_map/ppermute | solution.py:258
  87.5 16.7 %copy-start.45 = (f32[256]{0:T(256)S(1)}, f32[256]{0:T(256)}, u32[]{:S(2)}) copy-start(f32[256]{0:T(256)} %get-tuple-element.36) | copy-start | bytes 3076
  94.3 9.9 %collective-permute-start.11 = (bf16[256,512]{1,0:T(8,128)(2,1)S(1)}, bf16[256,512]{1,0:T(8,128)(2,1)S(1)}, u32[]{:S(2)}, u32[]{:S(2)}) collective-permute-start(bf16[256,512]{1,0:T(8,128)(2,1)S(1)} %add_convert_fusion.14), channel_id=1, source_target_pairs={{0,1},{1,0},{2,3},{3,2},{4,5},{5,4},{6,7},{7,6},{8,9},{9,8},{10,11... | collective-permute-start | bytes 786440 | tf_op jit(solution)/shard_map/ppermute | solution.py:258
  95.9 9.3 %copy-start.6 = (bf16[8,32,512]{2,1,0:T(8,128)(2,1)S(1)}, bf16[8,32,512]{2,1,0:T(8,128)(2,1)}, u32[]{:S(2)}) copy-start(bf16[8,32,512]{2,1,0:T(8,128)(2,1)} %copy-done.5) | copy-start | bytes 786436
  95.9 9.3 %copy-start.11 = (bf16[256,512]{1,0:T(8,128)(2,1)S(1)}, bf16[256,512]{1,0:T(8,128)(2,1)}, u32[]{:S(2)}) copy-start(bf16[256,512]{1,0:T(8,128)(2,1)} %copy-done.10) | copy-start | bytes 786436
  95.9 33.4 %all-to-all-start.1 = ((bf16[8,64,512]{2,1,0:T(8,128)(2,1)}), bf16[8,64,512]{2,1,0:T(8,128)(2,1)}, u32[]{:S(2)}, u32[]{:S(2)}) async-start(bf16[8,64,512]{2,1,0:T(8,128)(2,1)} %fusion.79), calls=%async_computation.1 | async-start | bytes 1048576 | tf_op jit(solution)/shard_map/all_to_all | solution.py:456
  102.3 18.3 %collective-permute-start.24 = (bf16[2,128,1024]{2,1,0:T(8,128)(2,1)}, bf16[2,128,1024]{2,1,0:T(8,128)(2,1)}, u32[]{:S(2)}, u32[]{:S(2)}) collective-permute-start(bf16[2,128,1024]{2,1,0:T(8,128)(2,1)} %add_convert_fusion.6), channel_id=1, source_target_pairs={{0,8},{1,5},{2,10},{3,7},{8,16},{9,1},{10,18},{11,3},{16,24},{17,9... | collective-permute-start | bytes 1572872 | tf_op jit(solution)/shard_map/ppermute | solution.py:234
  117.9 6.4 %collective-permute-start.12 = (bf16[256,512]{1,0:T(8,128)(2,1)S(1)}, bf16[256,512]{1,0:T(8,128)(2,1)S(1)}, u32[]{:S(2)}, u32[]{:S(2)}) collective-permute-start(bf16[256,512]{1,0:T(8,128)(2,1)S(1)} %slice_select_fusion.5), channel_id=1, source_target_pairs={{0,1},{1,0},{2,3},{3,2},{4,5},{5,4},{6,7},{7,6},{8,9},{9,8},{10,11... | collective-permute-start | bytes 786440 | tf_op jit(solution)/shard_map/ppermute | solution.py:258
  119.1 7.6 %collective-permute-start.16 = (bf16[128,1024]{0,1:T(8,128)(2,1)S(1)}, bf16[128,1024]{0,1:T(8,128)(2,1)S(1)}, u32[]{:S(2)}, u32[]{:S(2)}) collective-permute-start(bf16[128,1024]{0,1:T(8,128)(2,1)S(1)} %fusion.106), channel_id=1, source_target_pairs={{0,8},{1,5},{2,10},{3,7},{8,16},{9,1},{10,18},{11,3},{16,24},{17,9... | collective-permute-start | bytes 786440 | tf_op jit(solution)/shard_map/ppermute | solution.py:234
  122.8 14.9 %collective-permute-start.25 = (bf16[2,128,1024]{2,1,0:T(8,128)(2,1)}, bf16[2,128,1024]{2,1,0:T(8,128)(2,1)}, u32[]{:S(2)}, u32[]{:S(2)}) collective-permute-start(bf16[2,128,1024]{2,1,0:T(8,128)(2,1)} %add_convert_fusion.5), channel_id=1, source_target_pairs={{0,8},{1,5},{2,10},{3,7},{8,16},{9,1},{10,18},{11,3},{16,24},{17,9... | collective-permute-start | bytes 1572872 | tf_op jit(solution)/shard_map/ppermute | solution.py:234
  125.1 7.5 %collective-permute-start.13 = (bf16[256,512]{1,0:T(8,128)(2,1)}, bf16[256,512]{1,0:T(8,128)(2,1)}, u32[]{:S(2)}, u32[]{:S(2)}) collective-permute-start(bf16[256,512]{1,0:T(8,128)(2,1)} %fusion.86), channel_id=1, source_target_pairs={{0,2},{1,3},{2,0},{3,1},{4,6},{5,7},{6,4},{7,5},{8,10},{9,11},{10,... | collective-permute-start | bytes 786440 | tf_op jit(solution)/shard_map/ppermute | solution.py:258
  127.4 7.7 %collective-permute-start.17 = (bf16[128,1024]{0,1:T(8,128)(2,1)}, bf16[128,1024]{0,1:T(8,128)(2,1)}, u32[]{:S(2)}, u32[]{:S(2)}) collective-permute-start(bf16[128,1024]{0,1:T(8,128)(2,1)} %add_convert_fusion.12), channel_id=1, source_target_pairs={{0,8},{1,5},{2,10},{3,7},{8,16},{9,1},{10,18},{11,3},{16,24},{17,9... | collective-permute-start | bytes 786440 | tf_op jit(solution)/shard_map/ppermute | solution.py:234
  129.4 40.7 %collective-permute-start.7 = (bf16[8,64,512]{2,1,0:T(8,128)(2,1)}, bf16[8,64,512]{2,1,0:T(8,128)(2,1)}, u32[]{:S(2)}, u32[]{:S(2)}) collective-permute-start(bf16[8,64,512]{2,1,0:T(8,128)(2,1)} %all-to-all-done.1), channel_id=1, source_target_pairs={{0,1},{1,0},{2,3},{3,2},{4,5},{5,4},{6,7},{7,6},{8,9},{9,8},{10,11... | collective-permute-start | bytes 1572872 | tf_op jit(solution)/shard_map/ppermute | solution.py:258
  133.8 7.7 %copy-start.44 = (f32[256]{0:T(256)S(1)}, f32[256]{0:T(256)}, u32[]{:S(2)}) copy-start(f32[256]{0:T(256)} %copy-done.42) | copy-start | bytes 3076
  133.8 7.7 %collective-permute-start.14 = (bf16[256,512]{1,0:T(8,128)(2,1)S(1)}, bf16[256,512]{1,0:T(8,128)(2,1)S(1)}, u32[]{:S(2)}, u32[]{:S(2)}) collective-permute-start(bf16[256,512]{1,0:T(8,128)(2,1)S(1)} %add_convert_fusion.13), channel_id=1, source_target_pairs={{0,1},{1,0},{2,3},{3,2},{4,5},{5,4},{6,7},{7,6},{8,9},{9,8},{10,11... | collective-permute-start | bytes 786440 | tf_op jit(solution)/shard_map/ppermute | solution.py:258
  136.2 6.4 %collective-permute-start.18 = (bf16[128,1024]{0,1:T(8,128)(2,1)S(1)}, bf16[128,1024]{0,1:T(8,128)(2,1)S(1)}, u32[]{:S(2)}, u32[]{:S(2)}) collective-permute-start(bf16[128,1024]{0,1:T(8,128)(2,1)S(1)} %add_convert_fusion.11), channel_id=1, source_target_pairs={{0,8},{1,5},{2,10},{3,7},{8,16},{9,1},{10,18},{11,3},{16,24},{17,9... | collective-permute-start | bytes 786440 | tf_op jit(solution)/shard_map/ppermute | solution.py:234
  139.9 24.8 %collective-permute-start.26 = (bf16[2,128,1024]{2,1,0:T(8,128)(2,1)}, bf16[2,128,1024]{2,1,0:T(8,128)(2,1)}, u32[]{:S(2)}, u32[]{:S(2)}) collective-permute-start(bf16[2,128,1024]{2,1,0:T(8,128)(2,1)} %add_convert_fusion.4), channel_id=1, source_target_pairs={{0,8},{1,5},{2,10},{3,7},{8,16},{9,1},{10,18},{11,3},{16,24},{17,9... | collective-permute-start | bytes 1572872 | tf_op jit(solution)/shard_map/ppermute | solution.py:234
  142.7 9.5 %collective-permute-start.19 = (bf16[128,1024]{0,1:T(8,128)(2,1)S(1)}, bf16[128,1024]{0,1:T(8,128)(2,1)S(1)}, u32[]{:S(2)}, u32[]{:S(2)}) collective-permute-start(bf16[128,1024]{0,1:T(8,128)(2,1)S(1)} %add_convert_fusion.10), channel_id=1, source_target_pairs={{0,8},{1,5},{2,10},{3,7},{8,16},{9,1},{10,18},{11,3},{16,24},{17,9... | collective-permute-start | bytes 786440 | tf_op jit(solution)/shard_map/ppermute | solution.py:234
  144.2 9.5 %copy-start.47 = (bf16[1024]{0:T(1024)(128)(2,1)S(1)}, bf16[1024]{0:T(1024)(128)(2,1)}, u32[]{:S(2)}) copy-start(bf16[1024]{0:T(1024)(128)(2,1)} %get-tuple-element.30) | copy-start | bytes 6148
  152.3 6.4 %collective-permute-start.20 = (bf16[128,1024]{0,1:T(8,128)(2,1)S(1)}, bf16[128,1024]{0,1:T(8,128)(2,1)S(1)}, u32[]{:S(2)}, u32[]{:S(2)}) collective-permute-start(bf16[128,1024]{0,1:T(8,128)(2,1)S(1)} %add_convert_fusion.9), channel_id=1, source_target_pairs={{0,8},{1,5},{2,10},{3,7},{8,16},{9,1},{10,18},{11,3},{16,24},{17,9... | collective-permute-start | bytes 786440 | tf_op jit(solution)/shard_map/ppermute | solution.py:234
  158.8 9.5 %collective-permute-start.21 = (bf16[128,1024]{0,1:T(8,128)(2,1)S(1)}, bf16[128,1024]{0,1:T(8,128)(2,1)S(1)}, u32[]{:S(2)}, u32[]{:S(2)}) collective-permute-start(bf16[128,1024]{0,1:T(8,128)(2,1)S(1)} %add_convert_fusion.8), channel_id=1, source_target_pairs={{0,8},{1,5},{2,10},{3,7},{8,16},{9,1},{10,18},{11,3},{16,24},{17,9... | collective-permute-start | bytes 786440 | tf_op jit(solution)/shard_map/ppermute | solution.py:234
  161.2 28.7 %all-to-all-start.3 = ((bf16[8,80,512]{2,1,0:T(8,128)(2,1)}), bf16[8,80,512]{2,1,0:T(8,128)(2,1)S(1)}, u32[]{:S(2)}, u32[]{:S(2)}) async-start(bf16[8,80,512]{2,1,0:T(8,128)(2,1)} %fusion.78), calls=%async_computation.3 | async-start | bytes 1310720 | tf_op jit(solution)/shard_map/all_to_all | solution.py:458
  166.3 14.1 %collective-permute-start.27 = (bf16[2,128,1024]{2,1,0:T(8,128)(2,1)S(1)}, bf16[2,128,1024]{2,1,0:T(8,128)(2,1)S(1)}, u32[]{:S(2)}, u32[]{:S(2)}) collective-permute-start(bf16[2,128,1024]{2,1,0:T(8,128)(2,1)S(1)} %add_convert_fusion.3), channel_id=1, source_target_pairs={{0,8},{1,5},{2,10},{3,7},{8,16},{9,1},{10,18},{11,3},{16,24},{17,9... | collective-permute-start | bytes 1572872 | tf_op jit(solution)/shard_map/ppermute | solution.py:234
  168.4 18.1 %collective-permute-start.22 = (bf16[128,1024]{0,1:T(8,128)(2,1)S(1)}, bf16[128,1024]{0,1:T(8,128)(2,1)S(1)}, u32[]{:S(2)}, u32[]{:S(2)}) collective-permute-start(bf16[128,1024]{0,1:T(8,128)(2,1)S(1)} %add_convert_fusion.7), channel_id=1, source_target_pairs={{0,8},{1,5},{2,10},{3,7},{8,16},{9,1},{10,18},{11,3},{16,24},{17,9... | collective-permute-start | bytes 786440 | tf_op jit(solution)/shard_map/ppermute | solution.py:234
  182.4 11.0 %collective-permute-start.28 = (bf16[2,128,1024]{2,1,0:T(8,128)(2,1)}, bf16[2,128,1024]{2,1,0:T(8,128)(2,1)}, u32[]{:S(2)}, u32[]{:S(2)}) collective-permute-start(bf16[2,128,1024]{2,1,0:T(8,128)(2,1)} %add_convert_fusion.2), channel_id=1, source_target_pairs={{0,8},{1,5},{2,10},{3,7},{8,16},{9,1},{10,18},{11,3},{16,24},{17,9... | collective-permute-start | bytes 1572872 | tf_op jit(solution)/shard_map/ppermute | solution.py:234
  189.9 7.5 %collective-permute-start.15 = (bf16[8,64,512]{2,1,0:T(8,128)(2,1)S(1)}, bf16[8,64,512]{2,1,0:T(8,128)(2,1)S(1)}, u32[]{:S(2)}, u32[]{:S(2)}) collective-permute-start(bf16[8,64,512]{2,1,0:T(8,128)(2,1)S(1)} %slice.204), channel_id=1, source_target_pairs={{0,1},{1,0},{2,3},{3,2},{4,5},{5,4},{6,7},{7,6},{8,9},{9,8},{10,11... | collective-permute-start | bytes 1572872 | tf_op jit(solution)/shard_map/ppermute | solution.py:258
  194.9 10.3 %collective-permute-start.29 = (bf16[2,128,1024]{2,1,0:T(8,128)(2,1)S(1)}, bf16[2,128,1024]{2,1,0:T(8,128)(2,1)S(1)}, u32[]{:S(2)}, u32[]{:S(2)}) collective-permute-start(bf16[2,128,1024]{2,1,0:T(8,128)(2,1)S(1)} %add_convert_fusion.1), channel_id=1, source_target_pairs={{0,8},{1,5},{2,10},{3,7},{8,16},{9,1},{10,18},{11,3},{16,24},{17,9... | collective-permute-start | bytes 1572872 | tf_op jit(solution)/shard_map/ppermute | solution.py:234
  (41 other events, 123.7 us)

commit v4 on v3

--- a/solution.py
+++ b/solution.py
@@ -223,34 +223,47 @@
     return jnp.where(place < size // 2, 2 * place, 2 * (size - place) - 1)
 
 
-def ring_permute(values):
+def ring_permute(values, sign):
     order = ring_order(lax.axis_size("seq"))
     size, width = len(order), lax.axis_size("tp")
     pairs = []
     for i in range(size):
         for t in range(width):
-            after = (i + 1 - 2 * (t % 2)) % size
-            pairs.append((order[i] * width + t, order[after] * width + t))
+            there = (i + sign * (1 - 2 * (t % 2))) % size
+            pairs.append((order[i] * width + t, order[there] * width + t))
     return lax.ppermute(values, ("seq", "tp"), pairs)
 
 
-def ring_scatter(whole, axis, core):
+def after(value, *others):
+    return lax.optimization_barrier((value,) + others)[0]
+
+
+def ring_chunk(whole, axis, core, distance):
     size = lax.axis_size("seq")
     place = ring_place(lax.axis_index("seq"), size)
     width = whole.shape[axis] // size
-    direction = 1 - 2 * core
-
-    def chunk(k):
-        owner = ring_owner(place + size - direction * (1 + k), size)
-        return lax.dynamic_slice_in_dim(whole, owner * width, width, axis)
-
-    total = chunk(0)
-    for k in range(1, size):
-        moved = ring_permute(total)
-        total = moved.astype(jnp.float32) + chunk(k).astype(jnp.float32)
-        if k < size - 1:
-            total = total.astype(jnp.bfloat16)
-    return total
+    owner = ring_owner(place + size + distance * (1 - 2 * core), size)
+    return lax.dynamic_slice_in_dim(whole, owner * width, width, axis)
+
+
+def ring_step(whole, axis, core, state, step, *others):
+    size = lax.axis_size("seq")
+    far, near = size // 2, size // 2 - 1
+    f32, bf16 = jnp.float32, jnp.bfloat16
+
+    def chunk(distance):
+        return ring_chunk(whole, axis, core, distance)
+
+    if step == 0:
+        return chunk(far), chunk(-near)
+    ahead = after(ring_permute(state[0], 1), *others)
+    if step == far:
+        return chunk(0).astype(f32) + ahead.astype(f32) + state[1].astype(f32)
+    behind = after(ring_permute(state[1], -1), *others)
+    ahead = (ahead.astype(f32) + chunk(far - step).astype(f32)).astype(bf16)
+    if step < near:
+        behind = (behind.astype(f32) + chunk(step - near).astype(f32)).astype(bf16)
+    return ahead, behind
 
 
 def tp_permute(values, mask):
@@ -271,13 +284,19 @@
     )
 
 
-def tp_sum(partial, which):
+def tp_start(partial, which):
     narrow = partial.astype(jnp.bfloat16)
     moved = tp_permute(pick_half(narrow, 1 - which), 1)
     half = pick_half(partial, which) + moved.astype(jnp.float32)
-    half = half.astype(jnp.bfloat16)
-    moved = tp_permute(half, 2)
-    half = (half.astype(jnp.float32) + moved.astype(jnp.float32)).astype(jnp.bfloat16)
+    return half.astype(jnp.bfloat16)
+
+
+def tp_cross(half, *others):
+    moved = after(tp_permute(half, 2), *others)
+    return (half.astype(jnp.float32) + moved.astype(jnp.float32)).astype(jnp.bfloat16)
+
+
+def tp_join(half, which):
     return join_halves(half, tp_permute(half, 1), which).astype(jnp.float32)
 
 
@@ -311,6 +330,7 @@
     dev_count = lax.axis_size("seq")
     dev_index = lax.axis_index("seq")
     core = lax.axis_index("tp") % 2
+    side = lax.axis_index("tp") // 2
     share = routed_len // dev_count
     half_width = model_width // 2
 
@@ -327,22 +347,28 @@
         (index_row >= jnp.sum((seg_row < t).astype(jnp.int32))).astype(jnp.int32)
         for t in range(1, 4)
     )
+    def pick(source):
+        own = lax.dynamic_slice_in_dim(source, core * half_width, half_width, 2)
+        return compact(table, own).astype(bf16)
+
+    def exchange(own):
+        return lax.all_to_all(own, "seq", 0, 0, tiled=True)
+
+    def settle(slots):
+        own = from_owners(slots, share)
+        return join_halves(own, tp_permute(own, 1), core)
+
+    slots, seg_routed, picked_grads = lax.optimization_barrier(
+        (exchange(pick(tokens)), seg_routed, pick(out_grad))
+    )
+    routed_rows = settle(slots)
+
     ranks = jnp.arange(routed_len, dtype=jnp.int32)
     allowed = jnp.logical_and(
         ranks[None, :] <= ranks[:, None], seg_routed[None, :] == seg_routed[:, None]
     )[None]
 
-    def fetch(source):
-        own = lax.dynamic_slice_in_dim(source, core * half_width, half_width, 2)
-        own = compact(table, own).astype(bf16)
-        own = from_owners(lax.all_to_all(own, "seq", 0, 0, tiled=True), share)
-        return join_halves(own, tp_permute(own, 1), core)
-
-    routed_rows = fetch(tokens)
-    routed_grads = fetch(out_grad)
-
     rows = routed_rows.astype(f32)
-    grad_rows = routed_grads.astype(f32)
     gain_first = gain_attn.astype(f32)
     gain_second = gain_mlp.astype(f32)
     router = w_router.astype(f32)
@@ -365,7 +391,11 @@
     probs_low = probs.astype(bf16)
     mixed = jnp.einsum("hqk,khe->qhe", probs_low, values, preferred_element_type=f32)
     mixed = mixed.reshape(routed_len, -1).astype(bf16)
-    attn_out = tp_sum(jnp.dot(mixed, w_out, preferred_element_type=f32), core)
+    mixed, grad_slots = lax.optimization_barrier((mixed, exchange(picked_grads)))
+    attn_half = tp_start(jnp.dot(mixed, w_out, preferred_element_type=f32), core)
+    grad_rows = settle(grad_slots).astype(f32)
+    attn_half = tp_cross(attn_half)
+    attn_out = tp_join(attn_half, core)
 
     residual = rows + attn_out
     factor_second = lax.rsqrt(jnp.mean(residual * residual, axis=-1, keepdims=True) + 1e-05)
@@ -379,10 +409,13 @@
         grad_mlp, w_down, (((1,), (1,)), ((), ())), preferred_element_type=f32
     )
     grad_pre = gelu_pull(grad_hidden)[0].astype(bf16)
-    grad_mlp_input = tp_sum(
-        lax.dot_general(grad_pre, w_up, (((1,), (1,)), ((), ())), preferred_element_type=f32), core
-    )
-    mlp_out = tp_sum(jnp.dot(hidden, w_down, preferred_element_type=f32), core)
+    pull_part = lax.dot_general(
+        grad_pre, w_up, (((1,), (1,)), ((), ())), preferred_element_type=f32
+    )
+    pull_half = tp_start(pull_part, core)
+    mlp_half = tp_start(
+        jnp.dot(after(hidden, pull_half), w_down, preferred_element_type=f32), core
+    )
 
     def outer(left, right):
         product = lax.dot_general(
@@ -395,9 +428,19 @@
         jnp.stack([grad_pre, hidden]),
         (((1,), (1,)), ((0,), (0,))),
         preferred_element_type=f32,
-    )
-    mlp_grads = ring_scatter(mlp_pairs.astype(bf16), 1, core)
-    grad_up, grad_down = mlp_grads[0], mlp_grads[1].T
+    ).astype(bf16)
+
+    def mlp_ring(total, step, *others):
+        return ring_step(mlp_pairs, 1, core, total, step, *others)
+
+    mlp_ring_0 = mlp_ring(None, 0)
+    mlp_ring_1 = mlp_ring(mlp_ring_0, 1)
+    pull_half, mlp_half = lax.optimization_barrier(
+        (tp_cross(pull_half, *mlp_ring_1, mlp_half), mlp_half)
+    )
+    quarter = pick_half(attn_half, side).astype(f32) + pick_half(mlp_half, side).astype(f32)
+    branch_part = quarter + tp_permute(pick_half(mlp_half, 1 - side), 2).astype(f32)
+    grad_mlp_input = tp_join(pull_half, core)
 
     weighted = grad_mlp_input * gain_second
     grad_residual = factor_second * weighted - residual * factor_second**3 * jnp.mean(
@@ -412,35 +455,42 @@
     grad_probs = jnp.einsum("qhe,khe->hqk", grad_heads, values, preferred_element_type=f32)
     inner_sum = jnp.sum(probs * grad_probs, axis=-1, keepdims=True)
     grad_raw = (probs * (grad_probs - inner_sum) * scaling).astype(bf16)
-
     def flat(products):
         return products.reshape(routed_len, -1).astype(bf16)
 
     grad_query = flat(jnp.einsum("hqk,khe->qhe", grad_raw, keys, preferred_element_type=f32))
     grad_key = flat(jnp.einsum("hqk,qhe->khe", grad_raw, queries, preferred_element_type=f32))
     grad_value = flat(jnp.einsum("hqk,qhe->khe", probs_low, grad_heads, preferred_element_type=f32))
+    mlp_ring_2 = mlp_ring(mlp_ring_1, 2)
+    grad_query, grad_key, grad_value, branch_part, mlp_ring_2 = lax.optimization_barrier(
+        (grad_query, grad_key, grad_value, branch_part, mlp_ring_2)
+    )
     grad_parts = (grad_query, grad_key, grad_value)
-    grad_attn_input = tp_sum(
-        sum(
-            lax.dot_general(
-                grad_parts[c], weights[c], (((1,), (1,)), ((), ())), preferred_element_type=f32
-            )
-            for c in range(3)
-        ),
-        core,
-    )
+    update = (gating * branch_part).astype(bf16)
+    score = jnp.sum(pick_half(pick_half(grad_rows, core), side) * branch_part, axis=-1)
+    score = score + tp_permute(score, 1)
+    score = score + tp_permute(score, 2)
+    down_part = sum(
+        lax.dot_general(
+            grad_parts[c], weights[c], (((1,), (1,)), ((), ())), preferred_element_type=f32
+        )
+        for c in range(3)
+    )
+    input_half = tp_start(down_part, core)
+
     grad_rows_flat = jnp.concatenate(grad_parts, axis=1)
     attn_pairs = jnp.concatenate(
         [outer(attn_input, grad_rows_flat), outer(grad_attn, mixed)], axis=1
     )
-    attn_grads = ring_scatter(attn_pairs, 0, core)
-    split = 3 * mixed.shape[1]
-    grad_qkv = attn_grads[:, :split].reshape(-1, 3, mixed.shape[1])
-    grad_out = attn_grads[:, split:].T
-
-    branch = attn_out + mlp_out
-    update = (gating * branch).astype(bf16)
-    grad_score = gating * (1.0 - gating) * jnp.sum(grad_rows * branch, axis=-1, keepdims=True)
+
+    def attn_ring(total, step, *others):
+        return ring_step(attn_pairs, 0, core, total, step, *others)
+
+    attn_ring_0 = attn_ring(None, 0)
+
+    input_half, score = lax.optimization_barrier((tp_cross(input_half), score))
+    grad_score = gating * (1.0 - gating) * score[:, None]
+    grad_attn_input = tp_join(input_half, core)
     weighted = grad_attn_input * gain_first
     grad_norm = factor_first * weighted - rows * factor_first**3 * jnp.mean(
         rows * weighted, axis=-1, keepdims=True
@@ -452,14 +502,32 @@
     small = jnp.stack([grad_gain_attn, grad_gain_mlp, grad_router]).astype(bf16)
     small = small.reshape(3, dev_count, -1).transpose(1, 0, 2)
     small = jnp.pad(small, ((0, 0), (0, 13), (0, half_width - small.shape[2])))
-    sent = to_owners(pick_half(update, core), share)
-    got_update = lax.all_to_all(sent, "seq", 0, 0, tiled=True)
-    sent = jnp.concatenate([to_owners(pick_half(grad_routed_in, core), share), small], axis=1)
+    grads_part = pick_half(pick_half(grad_routed_in, core), side)
+    pieces = to_owners(jnp.concatenate([update, grads_part], axis=1), share)
+    sent = jnp.concatenate([pieces, small], axis=1)
     got = lax.all_to_all(sent, "seq", 0, 0, tiled=True)
+    mlp_total = mlp_ring(mlp_ring_2, 3, sent)
+    attn_total = attn_ring(attn_ring_0, 1, sent)
+    for step in range(4, dev_count // 2 + 1):
+        mlp_total = mlp_ring(mlp_total, step)
+    for step in range(2, dev_count // 2 + 1):
+        if step == 3:
+            attn_total, got = lax.optimization_barrier((attn_total, got))
+        attn_total = attn_ring(attn_total, step)
+    grad_up, grad_down = mlp_total[0], mlp_total[1].T
+    split = 3 * mixed.shape[1]
+    grad_qkv = attn_total[:, :split].reshape(-1, 3, mixed.shape[1])
+    grad_out = attn_total[:, split:].T
+
     small = jnp.sum(got[:, 2 * share : 2 * share + 3, : model_width // dev_count].astype(f32), axis=0)
-    got_grad = got[:, : 2 * share]
-    block_rows = join_halves(got_update, tp_permute(got_update, 1), core)
-    grad_slots = join_halves(got_grad, tp_permute(got_grad, 1), core)
+    width = half_width // 2
+
+    def gather(part):
+        part = join_halves(part, tp_permute(part, 2), side)
+        return join_halves(part, tp_permute(part, 1), core)
+
+    block_rows = gather(got[:, : 2 * share, :width])
+    grad_slots = gather(got[:, : 2 * share, width:])
     block_out = (tokens.astype(f32) + spread(table, block_rows)).astype(bf16)
     grad_tokens = out_grad.astype(f32) + spread(table, grad_slots)
     return (

time: 211 us -> 184 us (0.87)
  starting transfers between devices: 52.2 us -> 39.2 us
  waiting for transfers between devices: 68.3 us -> 60 us
  other arithmetic: 36.2 us -> 30.8 us
  matrix products: 41.8 us -> 39.5 us
    ppermute x14, starting transfers between devices: 24.2 us -> 12.5 us  [ring_permute(): return lax.ppermute(values, ('seq', 'tp'), pairs)]
    convert_element_type x21 -> x16, other arithmetic: 17.6 us -> 11.8 us  [the longest x4 7.49 us: ring_step(): behind = (behind.astype(f32) + chunk(step - near).astype(f32)).astype(bf16)]
    ppermute x16 -> x19, waiting for transfers between devices: 24.4 us -> 19 us  [tp_permute(): return lax.ppermute(values, 'tp', [(i, i ^ mask) for i in range(size)])]
    all_to_all x3 -> x2, waiting for transfers between devices: 21.3 us -> 16.3 us  [exchange(): return lax.all_to_all(own, 'seq', 0, 0, tiled=True)]
    all_to_all x3 -> x2, starting transfers between devices: 15.7 us -> 11.5 us  [exchange(): return lax.all_to_all(own, 'seq', 0, 0, tiled=True)]
    all_to_all x1, waiting for transfers between devices: 0.01 us -> 4.18 us  [on_device_whole(): got = lax.all_to_all(sent, 'seq', 0, 0, tiled=True)]
    dot_general x3, matrix products: 4.3 us -> 1.06 us  [on_device_whole(): lax.dot_general(grad_parts[c], weights[c], (((1,), (1,)), ((), ())), pref...]
    ppermute x16 -> x19, starting transfers between devices: 8.78 us -> 10.9 us  [tp_permute(): return lax.ppermute(values, 'tp', [(i, i ^ mask) for i in range(size)])]
  transfers between devices with their start and end apart: 34 -> 36, of which waited for: 15 -> 15; matrix products, arithmetic and copies ran while one was open for 32% -> 34% of each run, Pallas kernels for 0% -> 0%
where the time goes in v4:
time: 184 us; the launch traced here: 182 us
  waiting for transfers between devices  60 us (33%)
  matrix products  39.5 us (21%)
  starting transfers between devices  39.2 us (21%)
  other arithmetic  30.8 us (17%)
  local copies, waits for them, and re-layouts  10.4 us (6%)
    ppermute x14, waiting for transfers between devices, ring_permute(): return lax.ppermute(values, ('seq', 'tp'), pairs)  20.5 us
    ppermute x19, waiting for transfers between devices, tp_permute(): return lax.ppermute(values, 'tp', [(i, i ^ mask) for i in range(size)])  19 us
    all_to_all x2, waiting for transfers between devices, exchange(): return lax.all_to_all(own, 'seq', 0, 0, tiled=True)  16.3 us
    ppermute x14, starting transfers between devices, ring_permute(): return lax.ppermute(values, ('seq', 'tp'), pairs)  12.5 us
    dot_general x2, matrix products, spread(): jnp.einsum('sqc,sqd->scd', table, routed_rows, preferred_element_type=jnp...  12.3 us
    all_to_all x2, starting transfers between devices, exchange(): return lax.all_to_all(own, 'seq', 0, 0, tiled=True)  11.5 us
    ppermute x19, starting transfers between devices, tp_permute(): return lax.ppermute(values, 'tp', [(i, i ^ mask) for i in range(size)])  10.9 us
    convert_element_type x4, other arithmetic, ring_step(): behind = (behind.astype(f32) + chunk(step - near).astype(f32)).astype(bf16)  7.49 us
  transfers between devices with their start and end apart: 36, of which 15 were waited for; matrix products, arithmetic and copies ran while one was open for 34% of the time, Pallas kernels for 0%

profile of v4, /device:TPU:0, one launch (start us, length us, event | category | flops | bytes accessed | tf_op | source)
XLA Modules:
  0.0 181.5 jit_solution(809816705115374368)
XLA Ops:
  1.6 2.9 %fusion.16 = bf16[8,64,512]{2,1,0:T(8,128)(2,1)} fusion(bf16[8,256,1024]{2,1,0:T(8,128)(2,1)} %param.11, s32[]{:T(128)S(6)} %select_n.385, s32[8,64]{1,0:T(8,128)S(1)} %fusion.122), kind=kOutput, calls=%fused_computation.56 | convolution fusion | flops 134610944 | bytes 2623492 | tf_op jit(solution)/shard_map/sqc,scd->sqd/dot_general | solution.py:28
  4.5 7.3 %all-to-all-start = ((bf16[8,64,512]{2,1,0:T(8,128)(2,1)}), bf16[8,64,512]{2,1,0:T(8,128)(2,1)S(1)}, u32[]{:S(2)}, u32[]{:S(2)}) async-start(bf16[8,64,512]{2,1,0:T(8,128)(2,1)} %fusion.16), calls=%async_computation | async-start | bytes 1048576 | tf_op jit(solution)/shard_map/all_to_all | solution.py:355
  11.8 1.6 fusion.117
  13.4 2.6 %fusion.125 = s32[1,256]{1,0:T(1,128)S(1)} fusion(s32[8,256]{1,0:T(8,128)} %param.13, s32[]{:T(128)S(6)} %select_n.386, s32[]{:T(128)} %get-tuple-element.83, s32[]{:T(128)} %get-tuple-element.82, s32[]{:T(128)} %get-tuple-element.81), kind=kLoop, calls=%fused_computation.247 | loop fusion | flops 2048 | bytes 2064 | tf_op jit(solution)/shard_map/add | solution.py:346
  16.0 2.9 %fusion.19 = bf16[8,64,512]{2,1,0:T(8,128)(2,1)} fusion(bf16[8,256,1024]{2,1,0:T(8,128)(2,1)} %param.21, s32[]{:T(128)S(6)} %select_n.385, s32[8,64]{1,0:T(8,128)S(1)} %fusion.122), kind=kOutput, calls=%fused_computation.57 | convolution fusion | flops 134610944 | bytes 2623492 | tf_op jit(solution)/shard_map/sqc,scd->sqd/dot_general | solution.py:28
  18.9 7.4 %all-to-all-done = bf16[8,64,512]{2,1,0:T(8,128)(2,1)S(1)} async-done(((bf16[8,64,512]{2,1,0:T(8,128)(2,1)}), bf16[8,64,512]{2,1,0:T(8,128)(2,1)S(1)}, u32[]{:S(2)}, u32[]{:S(2)}) %all-to-all-start) | async-done | bytes 524320 | tf_op jit(solution)/shard_map/all_to_all | solution.py:355
  26.5 4.2 %all-to-all-start.1 = ((bf16[8,64,512]{2,1,0:T(8,128)(2,1)}), bf16[8,64,512]{2,1,0:T(8,128)(2,1)}, u32[]{:S(2)}, u32[]{:S(2)}) async-start(bf16[8,64,512]{2,1,0:T(8,128)(2,1)} %fusion.19), calls=%async_computation.1 | async-start | bytes 1048576 | tf_op jit(solution)/shard_map/all_to_all | solution.py:355
  31.6 2.2 %fusion.25 = bf16[3,256,256]{1,2,0:T(8,128)(2,1)S(1)} fusion(f32[1024]{0:T(1024)S(1)} %convert_element_type.390, f32[256]{0:T(256)S(1)} %get-tuple-element.107, bf16[1024,3,256]{2,0,1:T(8,128)(2,1)} %param.15, bf16[256,512]{1,0:T(8,128)(2,1)S(1)} %collective-permute-done, bf16[256,512]{1,0:T(8,128)(2,1)S(1)} %bitcast.103, pred[]{:T(512)S(6)} %eq.117), kind=kOutput, calls=%fused_computation.62 | convolution fusion | flops 406257664 | bytes 2495489 | tf_op jit(solution)/shard_map/rd,cdh->crh/dot_general | solution.py:379
  33.9 1.5 fusion.141
  35.4 1.7 convolution_convert_fusion.8
  37.1 8.9 %all-to-all-done.1 = bf16[8,64,512]{2,1,0:T(8,128)(2,1)} async-done(((bf16[8,64,512]{2,1,0:T(8,128)(2,1)}), bf16[8,64,512]{2,1,0:T(8,128)(2,1)}, u32[]{:S(2)}, u32[]{:S(2)}) %all-to-all-start.1) | async-done | bytes 524320 | tf_op jit(solution)/shard_map/all_to_all | solution.py:355
  46.5 1.5 collective-permute-done.1
  48.2 1.6 collective-permute-start.2
  49.7 6.9 %collective-permute-done.2 = bf16[256,512]{1,0:T(8,128)(2,1)S(1)} collective-permute-done((bf16[256,512]{1,0:T(8,128)(2,1)S(1)}, bf16[256,512]{1,0:T(8,128)(2,1)S(1)}, u32[]{:S(2)}, u32[]{:S(2)}) %collective-permute-start.2) | collective-permute-done | bytes 262176 | tf_op jit(solution)/shard_map/ppermute | solution.py:271
  61.9 1.3 fusion.40
  64.5 1.3 convolution_convert_fusion
  67.0 1.5 collective-permute-start.8
  69.2 1.7 fusion.144
  71.8 1.6 collective-permute-start.6
  75.2 6.7 %collective-permute-done.8 = bf16[2,128,1024]{2,1,0:T(8,128)(2,1)} collective-permute-done((bf16[2,128,1024]{2,1,0:T(8,128)(2,1)}, bf16[2,128,1024]{2,1,0:T(8,128)(2,1)}, u32[]{:S(2)}, u32[]{:S(2)}) %collective-permute-start.8) | collective-permute-done | bytes 524320 | tf_op jit(solution)/shard_map/ppermute | solution.py:234
  81.8 2.9 %add_convert_fusion.5 = (bf16[2,128,1024]{2,1,0:T(8,128)(2,1)}, bf16[2,128,1024]{2,1,0:T(8,128)(2,1)}) fusion(bf16[2,128,1024]{2,1,0:T(8,128)(2,1)} %collective-permute-done.8, bf16[2,1024,1024]{2,1,0:T(8,128)(2,1)} %copy-done.2, s32[]{:T(128)S(6)} %select_n.415, s32[]{:T(128)S(6)} %select_n.409, bf16[2,128,1024]{2,1,0:T(8,128)(2,1)} %collective-permute-done.7), kind=kLoop, calls=%fused_computation.115 | loop fusion | flops 2097152 | bytes 3145736 | tf_op jit(solution)/shard_map/convert_element_type | solution.py:265
  84.9 1.6 collective-permute-start.11
  87.3 1.5 collective-permute-start.13
  93.2 2.0 %convolution_convert_fusion.6 = bf16[4,64,256]{2,1,0:T(8,128)(2,1)S(1)} fusion(bf16[256,4,64]{0,2,1:T(8,128)(2,1)S(1)} %bitcast.144, f32[4,256,256]{1,2,0:T(8,128)S(1)} %fusion.146, f32[4,256,256]{1,2,0:T(8,128)} %get-tuple-element.111, f32[4,256]{1,0:T(4,128)} %copy-done.45), kind=kOutput, calls=%fused_computation.65 | convolution fusion | flops 35456256 | bytes 2363392 | tf_op jit(solution)/shard_map/hqk,khe->qhe/dot_general | solution.py:461
  95.3 2.7 %convolution_convert_fusion.5 = bf16[4,64,256]{2,1,0:T(8,128)(2,1)} fusion(bf16[256,4,64]{0,2,1:T(8,128)(2,1)S(1)} %bitcast.140, f32[4,256,256]{1,2,0:T(8,128)S(1)} %fusion.146, f32[4,256,256]{1,2,0:T(8,128)} %get-tuple-element.111, f32[4,256]{1,0:T(4,128)} %copy-done.45), kind=kOutput, calls=%fused_computation.64 | convolution fusion | flops 35456256 | bytes 2363392 | tf_op jit(solution)/shard_map/hqk,qhe->khe/dot_general | solution.py:462
  98.0 2.2 %convolution_convert_fusion.4 = bf16[4,64,256]{2,1,0:T(8,128)(2,1)} fusion(bf16[256,4,64]{0,2,1:T(8,128)(2,1)S(1)} %bitcast.133, f32[4,256]{1,0:T(4,128)} %copy-done.45, bf16[256,4,64]{0,2,1:T(8,128)(2,1)S(1)} %bitcast.141, bf16[256,4,64]{0,2,1:T(8,128)(2,1)S(1)} %bitcast.145, pred[256,256]{0,1:T(8,128)(4,1)} %copy-done.28), kind=kOutput, calls=%fused_computation.63 | convolution fusion | flops 68486400 | bytes 593920 | tf_op jit(solution)/shard_map/hqk,qhe->khe/dot_general | solution.py:463
  100.2 1.7 collective-permute-done.13
  102.0 2.7 %add_convert_fusion.2 = (bf16[2,128,1024]{2,1,0:T(8,128)(2,1)}, bf16[2,128,1024]{2,1,0:T(8,128)(2,1)S(1)}) fusion(bf16[2,128,1024]{2,1,0:T(8,128)(2,1)} %collective-permute-done.13, bf16[2,1024,1024]{2,1,0:T(8,128)(2,1)} %copy-done.2, s32[]{:T(128)S(6)} %select_n.429, s32[]{:T(128)S(6)} %select_n.426, bf16[2,128,1024]{2,1,0:T(8,128)(2,1)} %collective-permute-done.12), kind=kLoop, calls=%fused_computation.112 | loop fusion | flops 2097152 | bytes 3145736 | tf_op jit(solution)/shard_map/convert_element_type | solution.py:265
  107.4 1.7 collective-permute-start.32
  110.6 1.6 collective-permute-start.18
  113.0 1.7 collective-permute-start.21
  114.8 2.6 %collective-permute-done.18 = f32[256]{0:T(256)S(1)} collective-permute-done((f32[256]{0:T(256)S(1)}, f32[256]{0:T(256)S(1)}, u32[]{:S(2)}, u32[]{:S(2)}) %collective-permute-start.18) | collective-permute-done | bytes 1056 | tf_op jit(solution)/shard_map/ppermute | solution.py:271
  119.8 1.2 fusion.29
  122.1 1.2 add_convert_fusion.1
  123.7 4.0 %collective-permute-done.21 = bf16[128,1024]{0,1:T(8,128)(2,1)S(1)} collective-permute-done((bf16[128,1024]{0,1:T(8,128)(2,1)S(1)}, bf16[128,1024]{0,1:T(8,128)(2,1)S(1)}, u32[]{:S(2)}, u32[]{:S(2)}) %collective-permute-start.21) | collective-permute-done | bytes 262176 | tf_op jit(solution)/shard_map/ppermute | solution.py:234
  127.8 1.8 collective-permute-start.22
  129.5 4.2 %all-to-all-start.2 = ((bf16[8,80,512]{2,1,0:T(8,128)(2,1)}), bf16[8,80,512]{2,1,0:T(8,128)(2,1)}, u32[]{:S(2)}, u32[]{:S(2)}) async-start(bf16[8,80,512]{2,1,0:T(8,128)(2,1)} %fusion.73), calls=%async_computation.2 | async-start | bytes 1310720 | tf_op jit(solution)/shard_map/all_to_all | solution.py:508
  133.8 2.5 %collective-permute-done.22 = bf16[128,1024]{0,1:T(8,128)(2,1)S(1)} collective-permute-done((bf16[128,1024]{0,1:T(8,128)(2,1)S(1)}, bf16[128,1024]{0,1:T(8,128)(2,1)S(1)}, u32[]{:S(2)}, u32[]{:S(2)}) %collective-permute-start.22) | collective-permute-done | bytes 262176 | tf_op jit(solution)/shard_map/ppermute | solution.py:234
  136.3 1.8 add_convert_fusion.8
  138.1 1.6 convert_add_fusion.2
  140.8 2.0 %copy.36 = f32[1024,128]{1,0:T(8,128)} copy(f32[1024,128]{0,1:T(8,128)} %get-tuple-element.94) | data formatting | bytes 1048576
  142.9 4.4 %collective-permute-done.20 = bf16[128,1024]{0,1:T(8,128)(2,1)} collective-permute-done((bf16[128,1024]{0,1:T(8,128)(2,1)}, bf16[128,1024]{0,1:T(8,128)(2,1)}, u32[]{:S(2)}, u32[]{:S(2)}) %collective-permute-start.20) | collective-permute-done | bytes 262176 | tf_op jit(solution)/shard_map/ppermute | solution.py:234
  148.3 4.2 %all-to-all-done.2 = bf16[8,80,512]{2,1,0:T(8,128)(2,1)} async-done(((bf16[8,80,512]{2,1,0:T(8,128)(2,1)}), bf16[8,80,512]{2,1,0:T(8,128)(2,1)}, u32[]{:S(2)}, u32[]{:S(2)}) %all-to-all-start.2) | async-done | bytes 655392 | tf_op jit(solution)/shard_map/all_to_all | solution.py:508
  155.0 1.5 collective-permute-start.23
  158.4 1.2 collective-permute-done.27
  160.4 6.2 %collective-permute-done.23 = bf16[8,64,256]{2,1,0:T(8,128)(2,1)S(1)} collective-permute-done((bf16[8,64,256]{2,1,0:T(8,128)(2,1)S(1)}, bf16[8,64,256]{2,1,0:T(8,128)(2,1)S(1)}, u32[]{:S(2)}, u32[]{:S(2)}) %collective-permute-start.23) | collective-permute-done | bytes 262176 | tf_op jit(solution)/shard_map/ppermute | solution.py:271
  169.2 6.1 %add_convert_fusion = bf16[8,256,1024]{2,1,0:T(8,128)(2,1)} fusion(bf16[8,256,1024]{2,1,0:T(8,128)(2,1)} %param.11, bf16[8,64,512]{2,1,0:T(8,128)(2,1)} %collective-permute-done.24, bf16[8,64,512]{2,1,0:T(8,128)(2,1)S(1)} %maximum_select_fusion.12, pred[]{:T(512)S(6)} %eq.117, s32[8,64]{1,0:T(8,128)S(1)} %fusion.122), kind=kOutput, calls=%fused_computation.3 | convolution fusion | flops 279576576 | bytes 9439233 | tf_op jit(solution)/shard_map/sqc,sqd->scd/dot_general | solution.py:32
  175.3 6.2 %convert_add_fusion = f32[8,256,1024]{2,1,0:T(8,128)} fusion(bf16[8,256,1024]{2,1,0:T(8,128)(2,1)S(1)} %copy-done.3, bf16[8,64,512]{2,1,0:T(8,128)(2,1)} %collective-permute-done.26, bf16[8,64,512]{2,1,0:T(8,128)(2,1)S(1)} %maximum_select_fusion.13, pred[]{:T(512)S(6)} %eq.117, s32[8,64]{1,0:T(8,128)S(1)} %fusion.122), kind=kOutput, calls=%fused_computation.2 | convolution fusion | flops 277479424 | bytes 13633537 | tf_op jit(solution)/shard_map/sqc,sqd->scd/dot_general | solution.py:32
  (211 shorter events, 37.7 us)
Async XLA Ops:
  0.6 59.6 %copy-start = (bf16[1024,1024]{1,0:T(8,128)(2,1)S(1)}, bf16[1024,1024]{1,0:T(8,128)(2,1)}, u32[]{:S(2)}) copy-start(bf16[1024,1024]{1,0:T(8,128)(2,1)} %param.18) | copy-start | bytes 6291460
  4.5 21.8 %all-to-all-start = ((bf16[8,64,512]{2,1,0:T(8,128)(2,1)}), bf16[8,64,512]{2,1,0:T(8,128)(2,1)S(1)}, u32[]{:S(2)}, u32[]{:S(2)}) async-start(bf16[8,64,512]{2,1,0:T(8,128)(2,1)} %fusion.16), calls=%async_computation | async-start | bytes 1048576 | tf_op jit(solution)/shard_map/all_to_all | solution.py:355
  11.8 14.6 %copy-start.42 = (bf16[1024]{0:T(1024)(128)(2,1)S(1)}, bf16[1024]{0:T(1024)(128)(2,1)}, u32[]{:S(2)}) copy-start(bf16[1024]{0:T(1024)(128)(2,1)} %param.14) | copy-start | bytes 6148
  26.4 4.4 %collective-permute-start = (bf16[256,512]{1,0:T(8,128)(2,1)S(1)}, bf16[256,512]{1,0:T(8,128)(2,1)S(1)}, u32[]{:S(2)}, u32[]{:S(2)}) collective-permute-start(bf16[256,512]{1,0:T(8,128)(2,1)S(1)} %bitcast.101), channel_id=1, source_target_pairs={{0,1},{1,0},{2,3},{3,2},{4,5},{5,4},{6,7},{7,6},{8,9},{9,8},{10,11... | collective-permute-start | bytes 786440 | tf_op jit(solution)/shard_map/ppermute | solution.py:271
  26.5 19.6 %all-to-all-start.1 = ((bf16[8,64,512]{2,1,0:T(8,128)(2,1)}), bf16[8,64,512]{2,1,0:T(8,128)(2,1)}, u32[]{:S(2)}, u32[]{:S(2)}) async-start(bf16[8,64,512]{2,1,0:T(8,128)(2,1)} %fusion.19), calls=%async_computation.1 | async-start | bytes 1048576 | tf_op jit(solution)/shard_map/all_to_all | solution.py:355
  35.4 10.7 %copy-start.11 = (bf16[256,1024]{1,0:T(8,128)(2,1)S(1)}, bf16[256,1024]{1,0:T(8,128)(2,1)}, u32[]{:S(2)}) copy-start(bf16[256,1024]{1,0:T(8,128)(2,1)} %param.16) | copy-start | bytes 1572868
  46.4 10.4 %copy-start.43 = (bf16[1024]{0:T(1024)(128)(2,1)S(1)}, bf16[1024]{0:T(1024)(128)(2,1)}, u32[]{:S(2)}) copy-start(bf16[1024]{0:T(1024)(128)(2,1)} %param.17) | copy-start | bytes 6148
  46.4 10.5 %copy-start.44 = (bf16[1024]{0:T(1024)(128)(2,1)S(1)}, bf16[1024]{0:T(1024)(128)(2,1)}, u32[]{:S(2)}) copy-start(bf16[1024]{0:T(1024)(128)(2,1)} %param.20) | copy-start | bytes 6148
  46.4 1.6 collective-permute-start.1
  48.2 8.4 %collective-permute-start.2 = (bf16[256,512]{1,0:T(8,128)(2,1)S(1)}, bf16[256,512]{1,0:T(8,128)(2,1)S(1)}, u32[]{:S(2)}, u32[]{:S(2)}) collective-permute-start(bf16[256,512]{1,0:T(8,128)(2,1)S(1)} %fusion.84), channel_id=1, source_target_pairs={{0,2},{1,3},{2,0},{3,1},{4,6},{5,7},{6,4},{7,5},{8,10},{9,11},{10,... | collective-permute-start | bytes 786440 | tf_op jit(solution)/shard_map/ppermute | solution.py:271
  56.6 2.6 %collective-permute-start.3 = (bf16[256,512]{1,0:T(8,128)(2,1)S(1)}, bf16[256,512]{1,0:T(8,128)(2,1)S(1)}, u32[]{:S(2)}, u32[]{:S(2)}) collective-permute-start(bf16[256,512]{1,0:T(8,128)(2,1)S(1)} %add_convert_fusion.14), channel_id=1, source_target_pairs={{0,1},{1,0},{2,3},{3,2},{4,5},{5,4},{6,7},{7,6},{8,9},{9,8},{10,11... | collective-permute-start | bytes 786440 | tf_op jit(solution)/shard_map/ppermute | solution.py:271
  58.8 12.8 %copy-start.4 = (bf16[8,32,512]{2,1,0:T(8,128)(2,1)}, bf16[8,32,512]{2,1,0:T(8,128)(2,1)S(1)}, u32[]{:S(2)}) copy-start(bf16[8,32,512]{2,1,0:T(8,128)(2,1)S(1)} %pad_add_fusion) | copy-start | bytes 786436
  58.8 2.5 %collective-permute-start.4 = (bf16[256,512]{1,0:T(8,128)(2,1)S(1)}, bf16[256,512]{1,0:T(8,128)(2,1)S(1)}, u32[]{:S(2)}, u32[]{:S(2)}) collective-permute-start(bf16[256,512]{1,0:T(8,128)(2,1)S(1)} %bitcast.116), channel_id=1, source_target_pairs={{0,1},{1,0},{2,3},{3,2},{4,5},{5,4},{6,7},{7,6},{8,9},{9,8},{10,11... | collective-permute-start | bytes 786440 | tf_op jit(solution)/shard_map/ppermute | solution.py:271
  63.9 5.1 %collective-permute-start.5 = (bf16[256,512]{1,0:T(8,128)(2,1)S(1)}, bf16[256,512]{1,0:T(8,128)(2,1)S(1)}, u32[]{:S(2)}, u32[]{:S(2)}) collective-permute-start(bf16[256,512]{1,0:T(8,128)(2,1)S(1)} %slice_select_fusion.9), channel_id=1, source_target_pairs={{0,1},{1,0},{2,3},{3,2},{4,5},{5,4},{6,7},{7,6},{8,9},{9,8},{10,11... | collective-permute-start | bytes 786440 | tf_op jit(solution)/shard_map/ppermute | solution.py:271
  67.0 14.8 %collective-permute-start.8 = (bf16[2,128,1024]{2,1,0:T(8,128)(2,1)}, bf16[2,128,1024]{2,1,0:T(8,128)(2,1)}, u32[]{:S(2)}, u32[]{:S(2)}) collective-permute-start(bf16[2,128,1024]{2,1,0:T(8,128)(2,1)} %get-tuple-element.88), channel_id=1, source_target_pairs={{0,4},{1,9},{2,6},{3,11},{8,0},{9,17},{10,2},{11,19},{16,8},{17,25... | collective-permute-start | bytes 1572872 | tf_op jit(solution)/shard_map/ppermute | solution.py:234
  68.5 13.4 %collective-permute-start.7 = (bf16[2,128,1024]{2,1,0:T(8,128)(2,1)}, bf16[2,128,1024]{2,1,0:T(8,128)(2,1)}, u32[]{:S(2)}, u32[]{:S(2)}) collective-permute-start(bf16[2,128,1024]{2,1,0:T(8,128)(2,1)} %get-tuple-element.89), channel_id=1, source_target_pairs={{0,8},{1,5},{2,10},{3,7},{8,16},{9,1},{10,18},{11,3},{16,24},{17,9... | collective-permute-start | bytes 1572872 | tf_op jit(solution)/shard_map/ppermute | solution.py:234
  71.6 1.8 collective-permute-start.9
  71.8 13.0 %collective-permute-start.6 = (bf16[256,512]{1,0:T(8,128)(2,1)S(1)}, bf16[256,512]{1,0:T(8,128)(2,1)S(1)}, u32[]{:S(2)}, u32[]{:S(2)}) collective-permute-start(bf16[256,512]{1,0:T(8,128)(2,1)S(1)} %fusion.82), channel_id=1, source_target_pairs={{0,2},{1,3},{2,0},{3,1},{4,6},{5,7},{6,4},{7,5},{8,10},{9,11},{10,... | collective-permute-start | bytes 786440 | tf_op jit(solution)/shard_map/ppermute | solution.py:271
  84.9 5.3 %collective-permute-start.11 = (bf16[256,256]{1,0:T(8,128)(2,1)S(1)}, bf16[256,256]{1,0:T(8,128)(2,1)S(1)}, u32[]{:S(2)}, u32[]{:S(2)}) collective-permute-start(bf16[256,256]{1,0:T(8,128)(2,1)S(1)} %broadcast_select_fusion), channel_id=1, source_target_pairs={{0,2},{1,3},{2,0},{3,1},{4,6},{5,7},{6,4},{7,5},{8,10},{9,11},{10,... | collective-permute-start | bytes 393224 | tf_op jit(solution)/shard_map/ppermute | solution.py:271
  86.4 4.5 %collective-permute-start.10 = (bf16[256,512]{1,0:T(8,128)(2,1)S(1)}, bf16[256,512]{1,0:T(8,128)(2,1)S(1)}, u32[]{:S(2)}, u32[]{:S(2)}) collective-permute-start(bf16[256,512]{1,0:T(8,128)(2,1)S(1)} %add_convert_fusion.13), channel_id=1, source_target_pairs={{0,1},{1,0},{2,3},{3,2},{4,5},{5,4},{6,7},{7,6},{8,9},{9,8},{10,11... | collective-permute-start | bytes 786440 | tf_op jit(solution)/shard_map/ppermute | solution.py:271
  87.3 14.7 %collective-permute-start.13 = (bf16[2,128,1024]{2,1,0:T(8,128)(2,1)}, bf16[2,128,1024]{2,1,0:T(8,128)(2,1)}, u32[]{:S(2)}, u32[]{:S(2)}) collective-permute-start(bf16[2,128,1024]{2,1,0:T(8,128)(2,1)} %get-tuple-element.86), channel_id=1, source_target_pairs={{0,4},{1,9},{2,6},{3,11},{8,0},{9,17},{10,2},{11,19},{16,8},{17,25... | collective-permute-start | bytes 1572872 | tf_op jit(solution)/shard_map/ppermute | solution.py:234
  88.8 13.2 %collective-permute-start.12 = (bf16[2,128,1024]{2,1,0:T(8,128)(2,1)}, bf16[2,128,1024]{2,1,0:T(8,128)(2,1)}, u32[]{:S(2)}, u32[]{:S(2)}) collective-permute-start(bf16[2,128,1024]{2,1,0:T(8,128)(2,1)} %get-tuple-element.87), channel_id=1, source_target_pairs={{0,8},{1,5},{2,10},{3,7},{8,16},{9,1},{10,18},{11,3},{16,24},{17,9... | collective-permute-start | bytes 1572872 | tf_op jit(solution)/shard_map/ppermute | solution.py:234
  95.3 9.4 %copy-start.25 = (bf16[4,64,256]{2,1,0:T(8,128)(2,1)}, bf16[4,64,256]{2,1,0:T(8,128)(2,1)S(1)}, u32[]{:S(2)}) copy-start(bf16[4,64,256]{2,1,0:T(8,128)(2,1)S(1)} %convolution_convert_fusion.6) | copy-start | bytes 393220
  106.0 3.2 %collective-permute-start.15 = (bf16[256,512]{1,0:T(8,128)(2,1)S(1)}, bf16[256,512]{1,0:T(8,128)(2,1)S(1)}, u32[]{:S(2)}, u32[]{:S(2)}) collective-permute-start(bf16[256,512]{1,0:T(8,128)(2,1)S(1)} %slice_select_fusion.7), channel_id=1, source_target_pairs={{0,1},{1,0},{2,3},{3,2},{4,5},{5,4},{6,7},{7,6},{8,9},{9,8},{10,11... | collective-permute-start | bytes 786440 | tf_op jit(solution)/shard_map/ppermute | solution.py:271
  106.9 3.8 %collective-permute-start.17 = (f32[256]{0:T(256)S(1)}, f32[256]{0:T(256)S(1)}, u32[]{:S(2)}, u32[]{:S(2)}) collective-permute-start(f32[256]{0:T(256)S(1)} %get-tuple-element.102), channel_id=1, source_target_pairs={{0,1},{1,0},{2,3},{3,2},{4,5},{5,4},{6,7},{7,6},{8,9},{9,8},{10,11... | collective-permute-start | bytes 3080 | tf_op jit(solution)/shard_map/ppermute | solution.py:271
  107.1 14.9 %collective-permute-start.30 = (bf16[2,128,1024]{2,1,0:T(8,128)(2,1)S(1)}, bf16[2,128,1024]{2,1,0:T(8,128)(2,1)S(1)}, u32[]{:S(2)}, u32[]{:S(2)}) collective-permute-start(bf16[2,128,1024]{2,1,0:T(8,128)(2,1)S(1)} %get-tuple-element.53), channel_id=1, source_target_pairs={{0,8},{1,5},{2,10},{3,7},{8,16},{9,1},{10,18},{11,3},{16,24},{17,9... | collective-permute-start | bytes 1572872 | tf_op jit(solution)/shard_map/ppermute | solution.py:234
  107.4 26.4 %collective-permute-start.32 = (bf16[2,128,1024]{2,1,0:T(8,128)(2,1)}, bf16[2,128,1024]{2,1,0:T(8,128)(2,1)}, u32[]{:S(2)}, u32[]{:S(2)}) collective-permute-start(bf16[2,128,1024]{2,1,0:T(8,128)(2,1)} %get-tuple-element.55), channel_id=1, source_target_pairs={{0,4},{1,9},{2,6},{3,11},{8,0},{9,17},{10,2},{11,19},{16,8},{17,25... | collective-permute-start | bytes 1572872 | tf_op jit(solution)/shard_map/ppermute | solution.py:234
  109.3 8.4 %collective-permute-start.16 = (bf16[256,512]{1,0:T(8,128)(2,1)S(1)}, bf16[256,512]{1,0:T(8,128)(2,1)S(1)}, u32[]{:S(2)}, u32[]{:S(2)}) collective-permute-start(bf16[256,512]{1,0:T(8,128)(2,1)S(1)} %fusion.77), channel_id=1, source_target_pairs={{0,2},{1,3},{2,0},{3,1},{4,6},{5,7},{6,4},{7,5},{8,10},{9,11},{10,... | collective-permute-start | bytes 786440 | tf_op jit(solution)/shard_map/ppermute | solution.py:271
  110.6 7.3 %copy-start.7 = (bf16[256,512]{1,0:T(8,128)(2,1)S(1)}, bf16[256,512]{1,0:T(8,128)(2,1)}, u32[]{:S(2)}) copy-start(bf16[256,512]{1,0:T(8,128)(2,1)} %copy-done.6) | copy-start | bytes 786436
  110.6 7.3 %copy-start.34 = (f32[256]{0:T(256)S(1)}, f32[256]{0:T(256)}, u32[]{:S(2)}) copy-start(f32[256]{0:T(256)} %copy-done.32) | copy-start | bytes 3076
  110.6 6.7 %collective-permute-start.18 = (f32[256]{0:T(256)S(1)}, f32[256]{0:T(256)S(1)}, u32[]{:S(2)}, u32[]{:S(2)}) collective-permute-start(f32[256]{0:T(256)S(1)} %add.378), channel_id=1, source_target_pairs={{0,2},{1,3},{2,0},{3,1},{4,6},{5,7},{6,4},{7,5},{8,10},{9,11},{10,... | collective-permute-start | bytes 3080 | tf_op jit(solution)/shard_map/ppermute | solution.py:271
  113.0 6.7 %copy-start.36 = (f32[256]{0:T(256)S(1)}, f32[256]{0:T(256)}, u32[]{:S(2)}) copy-start(f32[256]{0:T(256)} %get-tuple-element.108) | copy-start | bytes 3076
  113.0 6.7 %copy-start.38 = (f32[256]{0:T(256)S(1)}, f32[256]{0:T(256)}, u32[]{:S(2)}) copy-start(f32[256]{0:T(256)} %copy-done.37) | copy-start | bytes 3076
  113.0 6.7 %copy-start.41 = (f32[256]{0:T(256)S(1)}, f32[256]{0:T(256)}, u32[]{:S(2)}) copy-start(f32[256]{0:T(256)} %get-tuple-element.106) | copy-start | bytes 3076
  113.0 14.6 %collective-permute-start.21 = (bf16[128,1024]{0,1:T(8,128)(2,1)S(1)}, bf16[128,1024]{0,1:T(8,128)(2,1)S(1)}, u32[]{:S(2)}, u32[]{:S(2)}) collective-permute-start(bf16[128,1024]{0,1:T(8,128)(2,1)S(1)} %get-tuple-element.92), channel_id=1, source_target_pairs={{0,4},{1,9},{2,6},{3,11},{8,0},{9,17},{10,2},{11,19},{16,8},{17,25... | collective-permute-start | bytes 786440 | tf_op jit(solution)/shard_map/ppermute | solution.py:234
  117.4 16.4 %collective-permute-start.14 = (bf16[128,1024]{0,1:T(8,128)(2,1)}, bf16[128,1024]{0,1:T(8,128)(2,1)}, u32[]{:S(2)}, u32[]{:S(2)}) collective-permute-start(bf16[128,1024]{0,1:T(8,128)(2,1)} %get-tuple-element.93), channel_id=1, source_target_pairs={{0,8},{1,5},{2,10},{3,7},{8,16},{9,1},{10,18},{11,3},{16,24},{17,9... | collective-permute-start | bytes 786440 | tf_op jit(solution)/shard_map/ppermute | solution.py:234
  117.8 1.6 collective-permute-start.19
  123.3 14.8 %collective-permute-start.31 = (bf16[2,128,1024]{2,1,0:T(8,128)(2,1)S(1)}, bf16[2,128,1024]{2,1,0:T(8,128)(2,1)}, u32[]{:S(2)}, u32[]{:S(2)}) collective-permute-start(bf16[2,128,1024]{2,1,0:T(8,128)(2,1)S(1)} %add_convert_fusion.1), channel_id=1, source_target_pairs={{0,8},{1,5},{2,10},{3,7},{8,16},{9,1},{10,18},{11,3},{16,24},{17,9... | collective-permute-start | bytes 1572872 | tf_op jit(solution)/shard_map/ppermute | solution.py:234
  127.8 8.6 %collective-permute-start.22 = (bf16[128,1024]{0,1:T(8,128)(2,1)S(1)}, bf16[128,1024]{0,1:T(8,128)(2,1)S(1)}, u32[]{:S(2)}, u32[]{:S(2)}) collective-permute-start(bf16[128,1024]{0,1:T(8,128)(2,1)S(1)} %add_convert_fusion.9), channel_id=1, source_target_pairs={{0,4},{1,9},{2,6},{3,11},{8,0},{9,17},{10,2},{11,19},{16,8},{17,25... | collective-permute-start | bytes 786440 | tf_op jit(solution)/shard_map/ppermute | solution.py:234
  129.5 22.9 %all-to-all-start.2 = ((bf16[8,80,512]{2,1,0:T(8,128)(2,1)}), bf16[8,80,512]{2,1,0:T(8,128)(2,1)}, u32[]{:S(2)}, u32[]{:S(2)}) async-start(bf16[8,80,512]{2,1,0:T(8,128)(2,1)} %fusion.73), calls=%async_computation.2 | async-start | bytes 1310720 | tf_op jit(solution)/shard_map/all_to_all | solution.py:508
  138.1 9.1 %collective-permute-start.20 = (bf16[128,1024]{0,1:T(8,128)(2,1)}, bf16[128,1024]{0,1:T(8,128)(2,1)}, u32[]{:S(2)}, u32[]{:S(2)}) collective-permute-start(bf16[128,1024]{0,1:T(8,128)(2,1)} %get-tuple-element.91), channel_id=1, source_target_pairs={{0,8},{1,5},{2,10},{3,7},{8,16},{9,1},{10,18},{11,3},{16,24},{17,9... | collective-permute-start | bytes 786440 | tf_op jit(solution)/shard_map/ppermute | solution.py:234
  152.5 7.1 %collective-permute-start.27 = (bf16[128,1024]{0,1:T(8,128)(2,1)S(1)}, bf16[128,1024]{0,1:T(8,128)(2,1)S(1)}, u32[]{:S(2)}, u32[]{:S(2)}) collective-permute-start(bf16[128,1024]{0,1:T(8,128)(2,1)S(1)} %add_convert_fusion.10), channel_id=1, source_target_pairs={{0,8},{1,5},{2,10},{3,7},{8,16},{9,1},{10,18},{11,3},{16,24},{17,9... | collective-permute-start | bytes 786440 | tf_op jit(solution)/shard_map/ppermute | solution.py:234
  154.4 12.4 %collective-permute-start.25 = (bf16[8,64,256]{2,1,0:T(8,128)(2,1)S(1)}, bf16[8,64,256]{2,1,0:T(8,128)(2,1)S(1)}, u32[]{:S(2)}, u32[]{:S(2)}) collective-permute-start(bf16[8,64,256]{2,1,0:T(8,128)(2,1)S(1)} %get-tuple-element.96), channel_id=1, source_target_pairs={{0,2},{1,3},{2,0},{3,1},{4,6},{5,7},{6,4},{7,5},{8,10},{9,11},{10,... | collective-permute-start | bytes 786440 | tf_op jit(solution)/shard_map/ppermute | solution.py:271
  155.0 11.6 %collective-permute-start.23 = (bf16[8,64,256]{2,1,0:T(8,128)(2,1)S(1)}, bf16[8,64,256]{2,1,0:T(8,128)(2,1)S(1)}, u32[]{:S(2)}, u32[]{:S(2)}) collective-permute-start(bf16[8,64,256]{2,1,0:T(8,128)(2,1)S(1)} %get-tuple-element.97), channel_id=1, source_target_pairs={{0,2},{1,3},{2,0},{3,1},{4,6},{5,7},{6,4},{7,5},{8,10},{9,11},{10,... | collective-permute-start | bytes 786440 | tf_op jit(solution)/shard_map/ppermute | solution.py:271
  156.5 11.0 %collective-permute-start.29 = (bf16[128,1024]{0,1:T(8,128)(2,1)S(1)}, bf16[128,1024]{0,1:T(8,128)(2,1)S(1)}, u32[]{:S(2)}, u32[]{:S(2)}) collective-permute-start(bf16[128,1024]{0,1:T(8,128)(2,1)S(1)} %get-tuple-element.52), channel_id=1, source_target_pairs={{0,4},{1,9},{2,6},{3,11},{8,0},{9,17},{10,2},{11,19},{16,8},{17,25... | collective-permute-start | bytes 786440 | tf_op jit(solution)/shard_map/ppermute | solution.py:234
  159.7 7.8 %collective-permute-start.28 = (bf16[128,1024]{0,1:T(8,128)(2,1)S(1)}, bf16[128,1024]{0,1:T(8,128)(2,1)S(1)}, u32[]{:S(2)}, u32[]{:S(2)}) collective-permute-start(bf16[128,1024]{0,1:T(8,128)(2,1)S(1)} %add_convert_fusion.7), channel_id=1, source_target_pairs={{0,8},{1,5},{2,10},{3,7},{8,16},{9,1},{10,18},{11,3},{16,24},{17,9... | collective-permute-start | bytes 786440 | tf_op jit(solution)/shard_map/ppermute | solution.py:234
  166.7 2.5 %collective-permute-start.24 = (bf16[8,64,512]{2,1,0:T(8,128)(2,1)S(1)}, bf16[8,64,512]{2,1,0:T(8,128)(2,1)}, u32[]{:S(2)}, u32[]{:S(2)}) collective-permute-start(bf16[8,64,512]{2,1,0:T(8,128)(2,1)S(1)} %maximum_select_fusion.12), channel_id=1, source_target_pairs={{0,1},{1,0},{2,3},{3,2},{4,5},{5,4},{6,7},{7,6},{8,9},{9,8},{10,11... | collective-permute-start | bytes 1572872 | tf_op jit(solution)/shard_map/ppermute | solution.py:271
  167.0 8.4 %collective-permute-start.26 = (bf16[8,64,512]{2,1,0:T(8,128)(2,1)S(1)}, bf16[8,64,512]{2,1,0:T(8,128)(2,1)}, u32[]{:S(2)}, u32[]{:S(2)}) collective-permute-start(bf16[8,64,512]{2,1,0:T(8,128)(2,1)S(1)} %maximum_select_fusion.13), channel_id=1, source_target_pairs={{0,1},{1,0},{2,3},{3,2},{4,5},{5,4},{6,7},{7,6},{8,9},{9,8},{10,11... | collective-permute-start | bytes 1572872 | tf_op jit(solution)/shard_map/ppermute | solution.py:271
  (34 other events, 108.0 us)

commit v5 on v4

--- a/solution.py
+++ b/solution.py
@@ -296,8 +296,8 @@
     return (half.astype(jnp.float32) + moved.astype(jnp.float32)).astype(jnp.bfloat16)
 
 
-def tp_join(half, which):
-    return join_halves(half, tp_permute(half, 1), which).astype(jnp.float32)
+def tp_join(half, which, *others):
+    return join_halves(half, after(tp_permute(half, 1), *others), which).astype(jnp.float32)
 
 
 def to_owners(rows, share):
@@ -333,6 +333,7 @@
     side = lax.axis_index("tp") // 2
     share = routed_len // dev_count
     half_width = model_width // 2
+    quarter_width = half_width // 2
 
     padded_index = jnp.concatenate(
         [routed_index, jnp.full((seq_count, share), -1, jnp.int32)], axis=1
@@ -347,8 +348,8 @@
         (index_row >= jnp.sum((seg_row < t).astype(jnp.int32))).astype(jnp.int32)
         for t in range(1, 4)
     )
-    def pick(source):
-        own = lax.dynamic_slice_in_dim(source, core * half_width, half_width, 2)
+    def pick(source, first, width):
+        own = lax.dynamic_slice_in_dim(source, first, width, 2)
         return compact(table, own).astype(bf16)
 
     def exchange(own):
@@ -356,10 +357,16 @@
 
     def settle(slots):
         own = from_owners(slots, share)
+        if own.shape[1] < half_width:
+            own = join_halves(own, tp_permute(own, 2), side)
         return join_halves(own, tp_permute(own, 1), core)
 
     slots, seg_routed, picked_grads = lax.optimization_barrier(
-        (exchange(pick(tokens)), seg_routed, pick(out_grad))
+        (
+            exchange(pick(tokens, core * half_width, half_width)),
+            seg_routed,
+            pick(out_grad, core * half_width + side * quarter_width, quarter_width),
+        )
     )
     routed_rows = settle(slots)
 
@@ -436,11 +443,11 @@
     mlp_ring_0 = mlp_ring(None, 0)
     mlp_ring_1 = mlp_ring(mlp_ring_0, 1)
     pull_half, mlp_half = lax.optimization_barrier(
-        (tp_cross(pull_half, *mlp_ring_1, mlp_half), mlp_half)
+        (tp_cross(pull_half, mlp_half), mlp_half)
     )
     quarter = pick_half(attn_half, side).astype(f32) + pick_half(mlp_half, side).astype(f32)
     branch_part = quarter + tp_permute(pick_half(mlp_half, 1 - side), 2).astype(f32)
-    grad_mlp_input = tp_join(pull_half, core)
+    grad_mlp_input = tp_join(pull_half, core, *mlp_ring_1)
 
     weighted = grad_mlp_input * gain_second
     grad_residual = factor_second * weighted - residual * factor_second**3 * jnp.mean(
@@ -511,7 +518,7 @@
     for step in range(4, dev_count // 2 + 1):
         mlp_total = mlp_ring(mlp_total, step)
     for step in range(2, dev_count // 2 + 1):
-        if step == 3:
+        if step == 2:
             attn_total, got = lax.optimization_barrier((attn_total, got))
         attn_total = attn_ring(attn_total, step)
     grad_up, grad_down = mlp_total[0], mlp_total[1].T

time: 184 us -> 182 us (0.989)
  starting transfers between devices: 39.2 us -> 48.5 us
  matrix products: 39.5 us -> 32.3 us
  other arithmetic: 30.8 us -> 26.6 us
  waiting for transfers between devices: 60 us -> 62.7 us
    ppermute x14, starting transfers between devices: 12.5 us -> 21.8 us  [ring_permute(): return lax.ppermute(values, ('seq', 'tp'), pairs)]
    ppermute x14, waiting for transfers between devices: 20.5 us -> 27.6 us  [ring_permute(): return lax.ppermute(values, ('seq', 'tp'), pairs)]
    all_to_all x2, waiting for transfers between devices: 16.3 us -> 10.4 us  [exchange(): return lax.all_to_all(own, 'seq', 0, 0, tiled=True)]
    ppermute x19 -> x20, waiting for transfers between devices: 19 us -> 24.7 us  [tp_permute(): return lax.ppermute(values, 'tp', [(i, i ^ mask) for i in range(size)])]
    dot_general x2, matrix products: 12.3 us -> 7.87 us  [spread(): jnp.einsum('sqc,sqd->scd', table, routed_rows, preferred_element_type=jnp...]
    all_to_all x1, waiting for transfers between devices: 4.18 us -> 0.01 us  [on_device_whole(): got = lax.all_to_all(sent, 'seq', 0, 0, tiled=True)]
    convert_element_type x4 -> x3, other arithmetic: 7.49 us -> 6.11 us  [ring_step(): behind = (behind.astype(f32) + chunk(step - near).astype(f32)).astype(bf16)]
    ppermute x19 -> x20, starting transfers between devices: 10.9 us -> 11.4 us  [tp_permute(): return lax.ppermute(values, 'tp', [(i, i ^ mask) for i in range(size)])]
  transfers between devices with their start and end apart: 36 -> 37, of which waited for: 15 -> 18; matrix products, arithmetic and copies ran while one was open for 34% -> 29% of each run, Pallas kernels for 0% -> 0%
where the time goes in v5:
time: 182 us; the launch traced here: 181 us
  waiting for transfers between devices  62.7 us (34%)
  starting transfers between devices  48.5 us (27%)
  matrix products  32.3 us (18%)
  other arithmetic  26.6 us (15%)
  local copies, waits for them, and re-layouts  8.6 us (5%)
  between operations  1.9 us (1%)
    ppermute x14, waiting for transfers between devices, ring_permute(): return lax.ppermute(values, ('seq', 'tp'), pairs)  27.6 us
    ppermute x20, waiting for transfers between devices, tp_permute(): return lax.ppermute(values, 'tp', [(i, i ^ mask) for i in range(size)])  24.7 us
    ppermute x14, starting transfers between devices, ring_permute(): return lax.ppermute(values, ('seq', 'tp'), pairs)  21.8 us
    ppermute x20, starting transfers between devices, tp_permute(): return lax.ppermute(values, 'tp', [(i, i ^ mask) for i in range(size)])  11.4 us
    all_to_all x2, starting transfers between devices, exchange(): return lax.all_to_all(own, 'seq', 0, 0, tiled=True)  11.1 us
    all_to_all x2, waiting for transfers between devices, exchange(): return lax.all_to_all(own, 'seq', 0, 0, tiled=True)  10.4 us
    dot_general x2, matrix products, spread(): jnp.einsum('sqc,sqd->scd', table, routed_rows, preferred_element_type=jnp...  7.87 us
    convert_element_type x3, other arithmetic, ring_step(): behind = (behind.astype(f32) + chunk(step - near).astype(f32)).astype(bf16)  6.11 us
  transfers between devices with their start and end apart: 37, of which 18 were waited for; matrix products, arithmetic and copies ran while one was open for 29% of the time, Pallas kernels for 0%

profile of v5, /device:TPU:0, one launch (start us, length us, event | category | flops | bytes accessed | tf_op | source)
XLA Modules:
  0.0 180.7 jit_solution(16446560172746571480)
XLA Ops:
  1.6 2.9 %fusion.14 = bf16[8,64,512]{2,1,0:T(8,128)(2,1)} fusion(bf16[8,256,1024]{2,1,0:T(8,128)(2,1)} %param.11, s32[]{:T(128)S(6)} %select_n.402, s32[8,64]{1,0:T(8,128)S(1)} %fusion.118), kind=kOutput, calls=%fused_computation.54 | convolution fusion | flops 134610944 | bytes 2623492 | tf_op jit(solution)/shard_map/sqc,scd->sqd/dot_general | solution.py:28
  4.5 7.4 %all-to-all-start = ((bf16[8,64,512]{2,1,0:T(8,128)(2,1)}), bf16[8,64,512]{2,1,0:T(8,128)(2,1)S(1)}, u32[]{:S(2)}, u32[]{:S(2)}) async-start(bf16[8,64,512]{2,1,0:T(8,128)(2,1)} %fusion.14), calls=%async_computation | async-start | bytes 1048576 | tf_op jit(solution)/shard_map/all_to_all | solution.py:356
  11.9 1.5 fusion.113
  13.5 2.6 %fusion.121 = s32[1,256]{1,0:T(1,128)S(1)} fusion(s32[8,256]{1,0:T(8,128)} %param.13, s32[]{:T(128)S(6)} %select_n.403, s32[]{:T(128)} %get-tuple-element.85, s32[]{:T(128)} %get-tuple-element.84, s32[]{:T(128)} %get-tuple-element.83), kind=kLoop, calls=%fused_computation.247 | loop fusion | flops 2048 | bytes 2064 | tf_op jit(solution)/shard_map/add | solution.py:347
  16.1 2.3 %convolution_convert_fusion.4 = bf16[8,64,256]{2,1,0:T(8,128)(2,1)} fusion(bf16[8,256,1024]{2,1,0:T(8,128)(2,1)} %param.21, s32[]{:T(128)S(6)} %select_n.404, s32[8,64]{1,0:T(8,128)S(1)} %fusion.118), kind=kOutput, calls=%fused_computation.60 | convolution fusion | flops 67371008 | bytes 1312772 | tf_op jit(solution)/shard_map/sqc,scd->sqd/dot_general | solution.py:28
  18.4 8.0 %all-to-all-done = bf16[8,64,512]{2,1,0:T(8,128)(2,1)S(1)} async-done(((bf16[8,64,512]{2,1,0:T(8,128)(2,1)}), bf16[8,64,512]{2,1,0:T(8,128)(2,1)S(1)}, u32[]{:S(2)}, u32[]{:S(2)}) %all-to-all-start) | async-done | bytes 524320 | tf_op jit(solution)/shard_map/all_to_all | solution.py:356
  26.6 3.6 %all-to-all-start.1 = ((bf16[8,64,256]{2,1,0:T(8,128)(2,1)}), bf16[8,64,256]{2,1,0:T(8,128)(2,1)S(1)}, u32[]{:S(2)}, u32[]{:S(2)}) async-start(bf16[8,64,256]{2,1,0:T(8,128)(2,1)} %convolution_convert_fusion.4), calls=%async_computation.1 | async-start | bytes 524288 | tf_op jit(solution)/shard_map/all_to_all | solution.py:356
  31.2 2.2 %fusion.20 = bf16[3,256,256]{1,2,0:T(8,128)(2,1)S(1)} fusion(f32[1024]{0:T(1024)S(1)} %convert_element_type.390, f32[256]{0:T(256)S(1)} %get-tuple-element.111, bf16[1024,3,256]{2,0,1:T(8,128)(2,1)} %param.15, bf16[256,512]{1,0:T(8,128)(2,1)S(1)} %collective-permute-done, bf16[256,512]{1,0:T(8,128)(2,1)S(1)} %bitcast.103, pred[]{:T(512)S(6)} %eq.118), kind=kOutput, calls=%fused_computation.59 | convolution fusion | flops 406257664 | bytes 2495489 | tf_op jit(solution)/shard_map/rd,cdh->crh/dot_general | solution.py:386
  34.1 1.5 fusion.137
  35.6 1.8 %convolution_convert_fusion.9 = bf16[4,64,256]{2,1,0:T(8,128)(2,1)S(1)} fusion(bf16[256,4,64]{0,2,1:T(8,128)(2,1)} %bitcast.132, f32[4,256]{1,0:T(4,128)S(1)} %get-tuple-element.114, bf16[256,4,64]{0,2,1:T(8,128)(2,1)} %bitcast.137, bf16[256,4,64]{0,2,1:T(8,128)(2,1)} %bitcast.141, pred[256,256]{0,1:T(8,128)(4,1)} %copy-done.31), kind=kOutput, calls=%fused_computation.65 | convolution fusion | flops 68486400 | bytes 593920 | tf_op jit(solution)/shard_map/hqk,khe->qhe/dot_general | solution.py:399
  37.4 2.4 %all-to-all-done.1 = bf16[8,64,256]{2,1,0:T(8,128)(2,1)S(1)} async-done(((bf16[8,64,256]{2,1,0:T(8,128)(2,1)}), bf16[8,64,256]{2,1,0:T(8,128)(2,1)S(1)}, u32[]{:S(2)}, u32[]{:S(2)}) %all-to-all-start.1) | async-done | bytes 262176 | tf_op jit(solution)/shard_map/all_to_all | solution.py:356
  40.3 1.6 collective-permute-start.4
  42.0 1.5 collective-permute-start.2
  43.5 3.2 %collective-permute-done.4 = bf16[256,256]{1,0:T(8,128)(2,1)S(1)} collective-permute-done((bf16[256,256]{1,0:T(8,128)(2,1)S(1)}, bf16[256,256]{1,0:T(8,128)(2,1)S(1)}, u32[]{:S(2)}, u32[]{:S(2)}) %collective-permute-start.4) | collective-permute-done | bytes 131104 | tf_op jit(solution)/shard_map/ppermute | solution.py:271
  47.9 4.1 %collective-permute-done.2 = bf16[256,512]{1,0:T(8,128)(2,1)} collective-permute-done((bf16[256,512]{1,0:T(8,128)(2,1)S(1)}, bf16[256,512]{1,0:T(8,128)(2,1)}, u32[]{:S(2)}, u32[]{:S(2)}) %collective-permute-start.2) | collective-permute-done | bytes 262176 | tf_op jit(solution)/shard_map/ppermute | solution.py:271
  56.7 1.3 fusion.35
  61.5 1.3 convolution_convert_fusion
  62.8 1.6 collective-permute-start.7
  64.4 1.5 collective-permute-start.11
  66.7 4.8 %collective-permute-done.7 = bf16[256,512]{1,0:T(8,128)(2,1)S(1)} collective-permute-done((bf16[256,512]{1,0:T(8,128)(2,1)S(1)}, bf16[256,512]{1,0:T(8,128)(2,1)S(1)}, u32[]{:S(2)}, u32[]{:S(2)}) %collective-permute-start.7) | collective-permute-done | bytes 262176 | tf_op jit(solution)/shard_map/ppermute | solution.py:271
  71.6 1.5 collective-permute-start.12
  73.1 6.1 %collective-permute-done.11 = bf16[2,128,1024]{2,1,0:T(8,128)(2,1)S(1)} collective-permute-done((bf16[2,128,1024]{2,1,0:T(8,128)(2,1)S(1)}, bf16[2,128,1024]{2,1,0:T(8,128)(2,1)S(1)}, u32[]{:S(2)}, u32[]{:S(2)}) %collective-permute-start.11) | collective-permute-done | bytes 524320 | tf_op jit(solution)/shard_map/ppermute | solution.py:234
  79.2 1.4 add_convert_fusion.5
  85.9 2.0 %convolution_convert_fusion.7 = bf16[4,64,256]{2,1,0:T(8,128)(2,1)S(1)} fusion(bf16[256,4,64]{0,2,1:T(8,128)(2,1)S(1)} %bitcast.142, f32[4,256,256]{1,2,0:T(8,128)S(1)} %fusion.142, f32[4,256,256]{1,2,0:T(8,128)} %get-tuple-element.115, f32[4,256]{1,0:T(4,128)S(1)} %copy-done.46), kind=kOutput, calls=%fused_computation.63 | convolution fusion | flops 35456256 | bytes 2363392 | tf_op jit(solution)/shard_map/hqk,khe->qhe/dot_general | solution.py:468
  87.9 2.0 %convolution_convert_fusion.6 = bf16[4,64,256]{2,1,0:T(8,128)(2,1)S(1)} fusion(bf16[256,4,64]{0,2,1:T(8,128)(2,1)S(1)} %bitcast.138, f32[4,256,256]{1,2,0:T(8,128)S(1)} %fusion.142, f32[4,256,256]{1,2,0:T(8,128)} %get-tuple-element.115, f32[4,256]{1,0:T(4,128)S(1)} %copy-done.46), kind=kOutput, calls=%fused_computation.62 | convolution fusion | flops 35456256 | bytes 2363392 | tf_op jit(solution)/shard_map/hqk,qhe->khe/dot_general | solution.py:469
  89.9 1.6 convolution_convert_fusion.5
  91.6 3.2 %collective-permute-done.14 = bf16[2,128,1024]{2,1,0:T(8,128)(2,1)} collective-permute-done((bf16[2,128,1024]{2,1,0:T(8,128)(2,1)}, bf16[2,128,1024]{2,1,0:T(8,128)(2,1)}, u32[]{:S(2)}, u32[]{:S(2)}) %collective-permute-start.14) | collective-permute-done | bytes 524320 | tf_op jit(solution)/shard_map/ppermute | solution.py:234
  94.8 2.9 %add_convert_fusion.2 = (bf16[2,128,1024]{2,1,0:T(8,128)(2,1)}, bf16[2,128,1024]{2,1,0:T(8,128)(2,1)}) fusion(bf16[2,128,1024]{2,1,0:T(8,128)(2,1)} %collective-permute-done.14, bf16[2,1024,1024]{2,1,0:T(8,128)(2,1)} %copy-done.4, s32[]{:T(128)S(6)} %select_n.449, s32[]{:T(128)S(6)} %select_n.446, bf16[2,128,1024]{2,1,0:T(8,128)(2,1)} %collective-permute-done.13), kind=kLoop, calls=%fused_computation.110 | loop fusion | flops 2097152 | bytes 3145736 | tf_op jit(solution)/shard_map/convert_element_type | solution.py:265
  100.1 1.3 collective-permute-start.31
  102.9 1.6 collective-permute-start.17
  105.8 5.1 %collective-permute-done.17 = bf16[256,512]{1,0:T(8,128)(2,1)S(1)} collective-permute-done((bf16[256,512]{1,0:T(8,128)(2,1)S(1)}, bf16[256,512]{1,0:T(8,128)(2,1)S(1)}, u32[]{:S(2)}, u32[]{:S(2)}) %collective-permute-start.17) | collective-permute-done | bytes 262176 | tf_op jit(solution)/shard_map/ppermute | solution.py:271
  115.3 4.2 %all-to-all-start.2 = ((bf16[8,80,512]{2,1,0:T(8,128)(2,1)}), bf16[8,80,512]{2,1,0:T(8,128)(2,1)}, u32[]{:S(2)}, u32[]{:S(2)}) async-start(bf16[8,80,512]{2,1,0:T(8,128)(2,1)} %fusion.69), calls=%async_computation.2 | async-start | bytes 1310720 | tf_op jit(solution)/shard_map/all_to_all | solution.py:515
  119.5 1.4 add_convert_fusion.1
  120.9 1.9 %collective-permute-start.32 = (bf16[2,128,1024]{2,1,0:T(8,128)(2,1)S(1)}, bf16[2,128,1024]{2,1,0:T(8,128)(2,1)}, u32[]{:S(2)}, u32[]{:S(2)}) collective-permute-start(bf16[2,128,1024]{2,1,0:T(8,128)(2,1)S(1)} %add_convert_fusion.1), channel_id=1, source_target_pairs={{0,8},{1,5},{2,10},{3,7},{8,16},{9,1},{10,18},{11,3},{16,24},{17,9... | collective-permute-start | bytes 1572872 | tf_op jit(solution)/shard_map/ppermute | solution.py:234
  123.2 1.9 %collective-permute-start.15 = (bf16[128,1024]{0,1:T(8,128)(2,1)S(1)}, bf16[128,1024]{0,1:T(8,128)(2,1)}, u32[]{:S(2)}, u32[]{:S(2)}) collective-permute-start(bf16[128,1024]{0,1:T(8,128)(2,1)S(1)} %get-tuple-element.97), channel_id=1, source_target_pairs={{0,8},{1,5},{2,10},{3,7},{8,16},{9,1},{10,18},{11,3},{16,24},{17,9... | collective-permute-start | bytes 786440 | tf_op jit(solution)/shard_map/ppermute | solution.py:234
  125.1 14.2 %collective-permute-done.21 = bf16[128,1024]{0,1:T(8,128)(2,1)S(1)} collective-permute-done((bf16[128,1024]{0,1:T(8,128)(2,1)S(1)}, bf16[128,1024]{0,1:T(8,128)(2,1)S(1)}, u32[]{:S(2)}, u32[]{:S(2)}) %collective-permute-start.21) | collective-permute-done | bytes 262176 | tf_op jit(solution)/shard_map/ppermute | solution.py:234
  139.3 2.9 %collective-permute-done.15 = bf16[128,1024]{0,1:T(8,128)(2,1)} collective-permute-done((bf16[128,1024]{0,1:T(8,128)(2,1)S(1)}, bf16[128,1024]{0,1:T(8,128)(2,1)}, u32[]{:S(2)}, u32[]{:S(2)}) %collective-permute-start.15) | collective-permute-done | bytes 262176 | tf_op jit(solution)/shard_map/ppermute | solution.py:234
  142.2 1.8 %add_convert_fusion.10 = (bf16[128,1024]{0,1:T(8,128)(2,1)S(1)}, bf16[128,1024]{0,1:T(8,128)(2,1)}) fusion(bf16[128,1024]{0,1:T(8,128)(2,1)S(1)} %collective-permute-done.21, s32[]{:T(128)S(6)} %select_n.437, bf16[1024,256]{0,1:T(8,128)(2,1)S(1)} %convolution_convert_fusion.2, bf16[1024,768]{0,1:T(8,128)(2,1)S(1)} %convolution_convert_fusion.1, ...), kind=kLoop, calls=%fused_computation.166 | loop fusion | flops 1835008 | bytes 3145736 | tf_op jit(solution)/shard_map/convert_element_type | solution.py:265
  144.0 1.6 convert_add_fusion.2
  146.7 2.0 %copy.36 = f32[1024,128]{1,0:T(8,128)} copy(f32[1024,128]{0,1:T(8,128)} %get-tuple-element.98) | data formatting | bytes 1048576
  148.7 4.9 %collective-permute-start.26 = (bf16[128,1024]{0,1:T(8,128)(2,1)}, bf16[128,1024]{0,1:T(8,128)(2,1)S(1)}, u32[]{:S(2)}, u32[]{:S(2)}) collective-permute-start(bf16[128,1024]{0,1:T(8,128)(2,1)} %get-tuple-element.53), channel_id=1, source_target_pairs={{0,8},{1,5},{2,10},{3,7},{8,16},{9,1},{10,18},{11,3},{16,24},{17,9... | collective-permute-start | bytes 786440 | tf_op jit(solution)/shard_map/ppermute | solution.py:234
  154.7 1.5 collective-permute-start.24
  157.9 2.6 %collective-permute-start.27 = (bf16[128,1024]{0,1:T(8,128)(2,1)S(1)}, bf16[128,1024]{0,1:T(8,128)(2,1)S(1)}, u32[]{:S(2)}, u32[]{:S(2)}) collective-permute-start(bf16[128,1024]{0,1:T(8,128)(2,1)S(1)} %add_convert_fusion.9), channel_id=1, source_target_pairs={{0,8},{1,5},{2,10},{3,7},{8,16},{9,1},{10,18},{11,3},{16,24},{17,9... | collective-permute-start | bytes 786440 | tf_op jit(solution)/shard_map/ppermute | solution.py:234
  160.6 2.2 %collective-permute-done.24 = bf16[8,64,256]{2,1,0:T(8,128)(2,1)S(1)} collective-permute-done((bf16[8,64,256]{2,1,0:T(8,128)(2,1)S(1)}, bf16[8,64,256]{2,1,0:T(8,128)(2,1)S(1)}, u32[]{:S(2)}, u32[]{:S(2)}) %collective-permute-start.24) | collective-permute-done | bytes 262176 | tf_op jit(solution)/shard_map/ppermute | solution.py:271
  163.5 2.1 %collective-permute-done.22 = bf16[8,64,256]{2,1,0:T(8,128)(2,1)S(1)} collective-permute-done((bf16[8,64,256]{2,1,0:T(8,128)(2,1)S(1)}, bf16[8,64,256]{2,1,0:T(8,128)(2,1)S(1)}, u32[]{:S(2)}, u32[]{:S(2)}) %collective-permute-start.22) | collective-permute-done | bytes 262176 | tf_op jit(solution)/shard_map/ppermute | solution.py:271
  167.0 4.0 %collective-permute-start.28 = (bf16[128,1024]{0,1:T(8,128)(2,1)S(1)}, bf16[128,1024]{0,1:T(8,128)(2,1)S(1)}, u32[]{:S(2)}, u32[]{:S(2)}) collective-permute-start(bf16[128,1024]{0,1:T(8,128)(2,1)S(1)} %get-tuple-element.92), channel_id=1, source_target_pairs={{0,8},{1,5},{2,10},{3,7},{8,16},{9,1},{10,18},{11,3},{16,24},{17,9... | collective-permute-start | bytes 786440 | tf_op jit(solution)/shard_map/ppermute | solution.py:234
  171.0 4.8 %convert_add_fusion = f32[8,256,1024]{2,1,0:T(8,128)} fusion(bf16[8,256,1024]{2,1,0:T(8,128)(2,1)S(1)} %copy-done.8, bf16[8,64,512]{2,1,0:T(8,128)(2,1)S(1)} %collective-permute-done.25, bf16[8,64,512]{2,1,0:T(8,128)(2,1)S(1)} %maximum_select_fusion.13, pred[]{:T(512)S(6)} %eq.118, s32[8,64]{1,0:T(8,128)S(1)} %fusion.118), kind=kOutput, calls=%fused_computation.2 | convolution fusion | flops 277479424 | bytes 13633537 | tf_op jit(solution)/shard_map/sqc,sqd->scd/dot_general | solution.py:32
  175.9 3.1 %add_convert_fusion = bf16[8,256,1024]{2,1,0:T(8,128)(2,1)} fusion(bf16[8,256,1024]{2,1,0:T(8,128)(2,1)S(1)} %copy-done.7, bf16[8,64,512]{2,1,0:T(8,128)(2,1)S(1)} %collective-permute-done.23, bf16[8,64,512]{2,1,0:T(8,128)(2,1)S(1)} %maximum_select_fusion.12, pred[]{:T(512)S(6)} %eq.118, s32[8,64]{1,0:T(8,128)S(1)} %fusion.118), kind=kOutput, calls=%fused_computation.3 | convolution fusion | flops 279576576 | bytes 9439233 | tf_op jit(solution)/shard_map/sqc,sqd->scd/dot_general | solution.py:32
  (215 shorter events, 35.6 us)
Async XLA Ops:
  0.6 54.5 %copy-start = (bf16[1024,1024]{1,0:T(8,128)(2,1)S(1)}, bf16[1024,1024]{1,0:T(8,128)(2,1)}, u32[]{:S(2)}) copy-start(bf16[1024,1024]{1,0:T(8,128)(2,1)} %param.18) | copy-start | bytes 6291460
  4.5 22.1 %copy-start.43 = (bf16[1024]{0:T(1024)(128)(2,1)S(1)}, bf16[1024]{0:T(1024)(128)(2,1)}, u32[]{:S(2)}) copy-start(bf16[1024]{0:T(1024)(128)(2,1)} %param.14) | copy-start | bytes 6148
  4.5 21.9 %all-to-all-start = ((bf16[8,64,512]{2,1,0:T(8,128)(2,1)}), bf16[8,64,512]{2,1,0:T(8,128)(2,1)S(1)}, u32[]{:S(2)}, u32[]{:S(2)}) async-start(bf16[8,64,512]{2,1,0:T(8,128)(2,1)} %fusion.14), calls=%async_computation | async-start | bytes 1048576 | tf_op jit(solution)/shard_map/all_to_all | solution.py:356
  26.5 3.9 %collective-permute-start = (bf16[256,512]{1,0:T(8,128)(2,1)S(1)}, bf16[256,512]{1,0:T(8,128)(2,1)S(1)}, u32[]{:S(2)}, u32[]{:S(2)}) collective-permute-start(bf16[256,512]{1,0:T(8,128)(2,1)S(1)} %bitcast.101), channel_id=1, source_target_pairs={{0,1},{1,0},{2,3},{3,2},{4,5},{5,4},{6,7},{7,6},{8,9},{9,8},{10,11... | collective-permute-start | bytes 786440 | tf_op jit(solution)/shard_map/ppermute | solution.py:271
  26.6 13.2 %all-to-all-start.1 = ((bf16[8,64,256]{2,1,0:T(8,128)(2,1)}), bf16[8,64,256]{2,1,0:T(8,128)(2,1)S(1)}, u32[]{:S(2)}, u32[]{:S(2)}) async-start(bf16[8,64,256]{2,1,0:T(8,128)(2,1)} %convolution_convert_fusion.4), calls=%async_computation.1 | async-start | bytes 524288 | tf_op jit(solution)/shard_map/all_to_all | solution.py:356
  40.2 1.7 collective-permute-start.1
  40.3 6.4 %collective-permute-start.4 = (bf16[256,256]{1,0:T(8,128)(2,1)S(1)}, bf16[256,256]{1,0:T(8,128)(2,1)S(1)}, u32[]{:S(2)}, u32[]{:S(2)}) collective-permute-start(bf16[256,256]{1,0:T(8,128)(2,1)S(1)} %bitcast.128), channel_id=1, source_target_pairs={{0,2},{1,3},{2,0},{3,1},{4,6},{5,7},{6,4},{7,5},{8,10},{9,11},{10,... | collective-permute-start | bytes 393224 | tf_op jit(solution)/shard_map/ppermute | solution.py:271
  42.0 10.0 %collective-permute-start.2 = (bf16[256,512]{1,0:T(8,128)(2,1)S(1)}, bf16[256,512]{1,0:T(8,128)(2,1)}, u32[]{:S(2)}, u32[]{:S(2)}) collective-permute-start(bf16[256,512]{1,0:T(8,128)(2,1)S(1)} %fusion.80), channel_id=1, source_target_pairs={{0,2},{1,3},{2,0},{3,1},{4,6},{5,7},{6,4},{7,5},{8,10},{9,11},{10,... | collective-permute-start | bytes 786440 | tf_op jit(solution)/shard_map/ppermute | solution.py:271
  46.8 6.3 %collective-permute-start.5 = (bf16[256,512]{1,0:T(8,128)(2,1)S(1)}, bf16[256,512]{1,0:T(8,128)(2,1)S(1)}, u32[]{:S(2)}, u32[]{:S(2)}) collective-permute-start(bf16[256,512]{1,0:T(8,128)(2,1)S(1)} %maximum_select_fusion.14), channel_id=1, source_target_pairs={{0,1},{1,0},{2,3},{3,2},{4,5},{5,4},{6,7},{7,6},{8,9},{9,8},{10,11... | collective-permute-start | bytes 786440 | tf_op jit(solution)/shard_map/ppermute | solution.py:271
  53.1 1.6 collective-permute-start.3
  54.7 29.2 %copy-start.5 = (bf16[256,512]{1,0:T(8,128)(2,1)}, bf16[256,512]{1,0:T(8,128)(2,1)S(1)}, u32[]{:S(2)}) copy-start(bf16[256,512]{1,0:T(8,128)(2,1)S(1)} %collective-permute-done.3) | copy-start | bytes 786436
  55.1 28.8 %copy-start.32 = (f32[256]{0:T(256)}, f32[256]{0:T(256)S(1)}, u32[]{:S(2)}) copy-start(f32[256]{0:T(256)S(1)} %get-tuple-element.126) | copy-start | bytes 3076
  55.1 28.8 %copy-start.34 = (f32[256]{0:T(256)}, f32[256]{0:T(256)S(1)}, u32[]{:S(2)}) copy-start(f32[256]{0:T(256)S(1)} %get-tuple-element.113) | copy-start | bytes 3076
  55.1 28.8 %copy-start.36 = (f32[256]{0:T(256)}, f32[256]{0:T(256)S(1)}, u32[]{:S(2)}) copy-start(f32[256]{0:T(256)S(1)} %get-tuple-element.112) | copy-start | bytes 3076
  58.8 1.6 collective-permute-start.6
  61.3 5.2 %collective-permute-start.8 = (bf16[256,512]{1,0:T(8,128)(2,1)S(1)}, bf16[256,512]{1,0:T(8,128)(2,1)S(1)}, u32[]{:S(2)}, u32[]{:S(2)}) collective-permute-start(bf16[256,512]{1,0:T(8,128)(2,1)S(1)} %slice_select_fusion.8), channel_id=1, source_target_pairs={{0,1},{1,0},{2,3},{3,2},{4,5},{5,4},{6,7},{7,6},{8,9},{9,8},{10,11... | collective-permute-start | bytes 786440 | tf_op jit(solution)/shard_map/ppermute | solution.py:271
  62.8 16.4 %copy-start.4 = (bf16[2,1024,1024]{2,1,0:T(8,128)(2,1)}, bf16[2,1024,1024]{2,1,0:T(8,128)(2,1)S(1)}, u32[]{:S(2)}) copy-start(bf16[2,1024,1024]{2,1,0:T(8,128)(2,1)S(1)} %convolution_convert_fusion) | copy-start | bytes 12582916
  62.8 8.7 %collective-permute-start.7 = (bf16[256,512]{1,0:T(8,128)(2,1)S(1)}, bf16[256,512]{1,0:T(8,128)(2,1)S(1)}, u32[]{:S(2)}, u32[]{:S(2)}) collective-permute-start(bf16[256,512]{1,0:T(8,128)(2,1)S(1)} %fusion.78), channel_id=1, source_target_pairs={{0,2},{1,3},{2,0},{3,1},{4,6},{5,7},{6,4},{7,5},{8,10},{9,11},{10,... | collective-permute-start | bytes 786440 | tf_op jit(solution)/shard_map/ppermute | solution.py:271
  64.4 14.8 %collective-permute-start.11 = (bf16[2,128,1024]{2,1,0:T(8,128)(2,1)S(1)}, bf16[2,128,1024]{2,1,0:T(8,128)(2,1)S(1)}, u32[]{:S(2)}, u32[]{:S(2)}) collective-permute-start(bf16[2,128,1024]{2,1,0:T(8,128)(2,1)S(1)} %get-tuple-element.90), channel_id=1, source_target_pairs={{0,4},{1,9},{2,6},{3,11},{8,0},{9,17},{10,2},{11,19},{16,8},{17,25... | collective-permute-start | bytes 1572872 | tf_op jit(solution)/shard_map/ppermute | solution.py:234
  65.9 13.3 %collective-permute-start.10 = (bf16[2,128,1024]{2,1,0:T(8,128)(2,1)S(1)}, bf16[2,128,1024]{2,1,0:T(8,128)(2,1)S(1)}, u32[]{:S(2)}, u32[]{:S(2)}) collective-permute-start(bf16[2,128,1024]{2,1,0:T(8,128)(2,1)S(1)} %get-tuple-element.91), channel_id=1, source_target_pairs={{0,8},{1,5},{2,10},{3,7},{8,16},{9,1},{10,18},{11,3},{16,24},{17,9... | collective-permute-start | bytes 1572872 | tf_op jit(solution)/shard_map/ppermute | solution.py:234
  71.6 12.4 %copy-start.12 = (bf16[256,512]{1,0:T(8,128)(2,1)S(1)}, bf16[256,512]{1,0:T(8,128)(2,1)}, u32[]{:S(2)}) copy-start(bf16[256,512]{1,0:T(8,128)(2,1)} %copy-done.11) | copy-start | bytes 786436
  71.6 11.1 %collective-permute-start.12 = (bf16[256,256]{1,0:T(8,128)(2,1)S(1)}, bf16[256,256]{1,0:T(8,128)(2,1)S(1)}, u32[]{:S(2)}, u32[]{:S(2)}) collective-permute-start(bf16[256,256]{1,0:T(8,128)(2,1)S(1)} %broadcast_select_fusion), channel_id=1, source_target_pairs={{0,2},{1,3},{2,0},{3,1},{4,6},{5,7},{6,4},{7,5},{8,10},{9,11},{10,... | collective-permute-start | bytes 393224 | tf_op jit(solution)/shard_map/ppermute | solution.py:271
  73.1 10.3 %collective-permute-start.9 = (bf16[256,512]{1,0:T(8,128)(2,1)S(1)}, bf16[256,512]{1,0:T(8,128)(2,1)S(1)}, u32[]{:S(2)}, u32[]{:S(2)}) collective-permute-start(bf16[256,512]{1,0:T(8,128)(2,1)S(1)} %add_convert_fusion.13), channel_id=1, source_target_pairs={{0,1},{1,0},{2,3},{3,2},{4,5},{5,4},{6,7},{7,6},{8,9},{9,8},{10,11... | collective-permute-start | bytes 786440 | tf_op jit(solution)/shard_map/ppermute | solution.py:271
  80.6 14.2 %collective-permute-start.14 = (bf16[2,128,1024]{2,1,0:T(8,128)(2,1)}, bf16[2,128,1024]{2,1,0:T(8,128)(2,1)}, u32[]{:S(2)}, u32[]{:S(2)}) collective-permute-start(bf16[2,128,1024]{2,1,0:T(8,128)(2,1)} %get-tuple-element.88), channel_id=1, source_target_pairs={{0,4},{1,9},{2,6},{3,11},{8,0},{9,17},{10,2},{11,19},{16,8},{17,25... | collective-permute-start | bytes 1572872 | tf_op jit(solution)/shard_map/ppermute | solution.py:234
  81.6 13.2 %collective-permute-start.13 = (bf16[2,128,1024]{2,1,0:T(8,128)(2,1)}, bf16[2,128,1024]{2,1,0:T(8,128)(2,1)}, u32[]{:S(2)}, u32[]{:S(2)}) collective-permute-start(bf16[2,128,1024]{2,1,0:T(8,128)(2,1)} %get-tuple-element.89), channel_id=1, source_target_pairs={{0,8},{1,5},{2,10},{3,7},{8,16},{9,1},{10,18},{11,3},{16,24},{17,9... | collective-permute-start | bytes 1572872 | tf_op jit(solution)/shard_map/ppermute | solution.py:234
  87.9 9.8 %copy-start.27 = (bf16[4,64,256]{2,1,0:T(8,128)(2,1)}, bf16[4,64,256]{2,1,0:T(8,128)(2,1)S(1)}, u32[]{:S(2)}) copy-start(bf16[4,64,256]{2,1,0:T(8,128)(2,1)S(1)} %convolution_convert_fusion.7) | copy-start | bytes 393220
  98.9 3.8 %collective-permute-start.16 = (bf16[256,512]{1,0:T(8,128)(2,1)S(1)}, bf16[256,512]{1,0:T(8,128)(2,1)S(1)}, u32[]{:S(2)}, u32[]{:S(2)}) collective-permute-start(bf16[256,512]{1,0:T(8,128)(2,1)S(1)} %slice_select_fusion.7), channel_id=1, source_target_pairs={{0,1},{1,0},{2,3},{3,2},{4,5},{5,4},{6,7},{7,6},{8,9},{9,8},{10,11... | collective-permute-start | bytes 786440 | tf_op jit(solution)/shard_map/ppermute | solution.py:271
  99.7 2.5 %collective-permute-start.18 = (f32[256]{0:T(256)S(1)}, f32[256]{0:T(256)S(1)}, u32[]{:S(2)}, u32[]{:S(2)}) collective-permute-start(f32[256]{0:T(256)S(1)} %get-tuple-element.106), channel_id=1, source_target_pairs={{0,1},{1,0},{2,3},{3,2},{4,5},{5,4},{6,7},{7,6},{8,9},{9,8},{10,11... | collective-permute-start | bytes 3080 | tf_op jit(solution)/shard_map/ppermute | solution.py:271
  100.1 19.4 %collective-permute-start.31 = (bf16[2,128,1024]{2,1,0:T(8,128)(2,1)}, bf16[2,128,1024]{2,1,0:T(8,128)(2,1)}, u32[]{:S(2)}, u32[]{:S(2)}) collective-permute-start(bf16[2,128,1024]{2,1,0:T(8,128)(2,1)} %get-tuple-element.55), channel_id=1, source_target_pairs={{0,8},{1,5},{2,10},{3,7},{8,16},{9,1},{10,18},{11,3},{16,24},{17,9... | collective-permute-start | bytes 1572872 | tf_op jit(solution)/shard_map/ppermute | solution.py:234
  101.4 23.7 %collective-permute-start.33 = (bf16[2,128,1024]{2,1,0:T(8,128)(2,1)}, bf16[2,128,1024]{2,1,0:T(8,128)(2,1)}, u32[]{:S(2)}, u32[]{:S(2)}) collective-permute-start(bf16[2,128,1024]{2,1,0:T(8,128)(2,1)} %get-tuple-element.57), channel_id=1, source_target_pairs={{0,4},{1,9},{2,6},{3,11},{8,0},{9,17},{10,2},{11,19},{16,8},{17,25... | collective-permute-start | bytes 1572872 | tf_op jit(solution)/shard_map/ppermute | solution.py:234
  102.2 3.6 %collective-permute-start.19 = (f32[256]{0:T(256)S(1)}, f32[256]{0:T(256)S(1)}, u32[]{:S(2)}, u32[]{:S(2)}) collective-permute-start(f32[256]{0:T(256)S(1)} %add.385), channel_id=1, source_target_pairs={{0,2},{1,3},{2,0},{3,1},{4,6},{5,7},{6,4},{7,5},{8,10},{9,11},{10,... | collective-permute-start | bytes 3080 | tf_op jit(solution)/shard_map/ppermute | solution.py:271
  102.9 8.2 %copy-start.6 = (bf16[256,512]{1,0:T(8,128)(2,1)S(1)}, bf16[256,512]{1,0:T(8,128)(2,1)}, u32[]{:S(2)}) copy-start(bf16[256,512]{1,0:T(8,128)(2,1)} %copy-done.5) | copy-start | bytes 786436
  102.9 8.0 %collective-permute-start.17 = (bf16[256,512]{1,0:T(8,128)(2,1)S(1)}, bf16[256,512]{1,0:T(8,128)(2,1)S(1)}, u32[]{:S(2)}, u32[]{:S(2)}) collective-permute-start(bf16[256,512]{1,0:T(8,128)(2,1)S(1)} %fusion.73), channel_id=1, source_target_pairs={{0,2},{1,3},{2,0},{3,1},{4,6},{5,7},{6,4},{7,5},{8,10},{9,11},{10,... | collective-permute-start | bytes 786440 | tf_op jit(solution)/shard_map/ppermute | solution.py:271
  105.2 61.7 %copy-start.2 = (bf16[1024,768]{0,1:T(8,128)(2,1)}, bf16[1024,768]{0,1:T(8,128)(2,1)S(1)}, u32[]{:S(2)}) copy-start(bf16[1024,768]{0,1:T(8,128)(2,1)S(1)} %convolution_convert_fusion.1) | copy-start | bytes 4718596
  111.0 1.6 collective-permute-start.20
  115.3 33.4 %all-to-all-start.2 = ((bf16[8,80,512]{2,1,0:T(8,128)(2,1)}), bf16[8,80,512]{2,1,0:T(8,128)(2,1)}, u32[]{:S(2)}, u32[]{:S(2)}) async-start(bf16[8,80,512]{2,1,0:T(8,128)(2,1)} %fusion.69), calls=%async_computation.2 | async-start | bytes 1310720 | tf_op jit(solution)/shard_map/all_to_all | solution.py:515
  120.9 23.0 %collective-permute-start.32 = (bf16[2,128,1024]{2,1,0:T(8,128)(2,1)S(1)}, bf16[2,128,1024]{2,1,0:T(8,128)(2,1)}, u32[]{:S(2)}, u32[]{:S(2)}) collective-permute-start(bf16[2,128,1024]{2,1,0:T(8,128)(2,1)S(1)} %add_convert_fusion.1), channel_id=1, source_target_pairs={{0,8},{1,5},{2,10},{3,7},{8,16},{9,1},{10,18},{11,3},{16,24},{17,9... | collective-permute-start | bytes 1572872 | tf_op jit(solution)/shard_map/ppermute | solution.py:234
  123.0 16.3 %collective-permute-start.21 = (bf16[128,1024]{0,1:T(8,128)(2,1)S(1)}, bf16[128,1024]{0,1:T(8,128)(2,1)S(1)}, u32[]{:S(2)}, u32[]{:S(2)}) collective-permute-start(bf16[128,1024]{0,1:T(8,128)(2,1)S(1)} %get-tuple-element.96), channel_id=1, source_target_pairs={{0,4},{1,9},{2,6},{3,11},{8,0},{9,17},{10,2},{11,19},{16,8},{17,25... | collective-permute-start | bytes 786440 | tf_op jit(solution)/shard_map/ppermute | solution.py:234
  123.2 19.0 %collective-permute-start.15 = (bf16[128,1024]{0,1:T(8,128)(2,1)S(1)}, bf16[128,1024]{0,1:T(8,128)(2,1)}, u32[]{:S(2)}, u32[]{:S(2)}) collective-permute-start(bf16[128,1024]{0,1:T(8,128)(2,1)S(1)} %get-tuple-element.97), channel_id=1, source_target_pairs={{0,8},{1,5},{2,10},{3,7},{8,16},{9,1},{10,18},{11,3},{16,24},{17,9... | collective-permute-start | bytes 786440 | tf_op jit(solution)/shard_map/ppermute | solution.py:234
  148.7 9.1 %collective-permute-start.26 = (bf16[128,1024]{0,1:T(8,128)(2,1)}, bf16[128,1024]{0,1:T(8,128)(2,1)S(1)}, u32[]{:S(2)}, u32[]{:S(2)}) collective-permute-start(bf16[128,1024]{0,1:T(8,128)(2,1)} %get-tuple-element.53), channel_id=1, source_target_pairs={{0,8},{1,5},{2,10},{3,7},{8,16},{9,1},{10,18},{11,3},{16,24},{17,9... | collective-permute-start | bytes 786440 | tf_op jit(solution)/shard_map/ppermute | solution.py:234
  154.7 8.0 %collective-permute-start.24 = (bf16[8,64,256]{2,1,0:T(8,128)(2,1)S(1)}, bf16[8,64,256]{2,1,0:T(8,128)(2,1)S(1)}, u32[]{:S(2)}, u32[]{:S(2)}) collective-permute-start(bf16[8,64,256]{2,1,0:T(8,128)(2,1)S(1)} %get-tuple-element.100), channel_id=1, source_target_pairs={{0,2},{1,3},{2,0},{3,1},{4,6},{5,7},{6,4},{7,5},{8,10},{9,11},{10,... | collective-permute-start | bytes 786440 | tf_op jit(solution)/shard_map/ppermute | solution.py:271
  157.0 8.6 %collective-permute-start.22 = (bf16[8,64,256]{2,1,0:T(8,128)(2,1)S(1)}, bf16[8,64,256]{2,1,0:T(8,128)(2,1)S(1)}, u32[]{:S(2)}, u32[]{:S(2)}) collective-permute-start(bf16[8,64,256]{2,1,0:T(8,128)(2,1)S(1)} %get-tuple-element.101), channel_id=1, source_target_pairs={{0,2},{1,3},{2,0},{3,1},{4,6},{5,7},{6,4},{7,5},{8,10},{9,11},{10,... | collective-permute-start | bytes 786440 | tf_op jit(solution)/shard_map/ppermute | solution.py:271
  157.6 9.2 %collective-permute-start.29 = (bf16[128,1024]{0,1:T(8,128)(2,1)S(1)}, bf16[128,1024]{0,1:T(8,128)(2,1)S(1)}, u32[]{:S(2)}, u32[]{:S(2)}) collective-permute-start(bf16[128,1024]{0,1:T(8,128)(2,1)S(1)} %get-tuple-element.54), channel_id=1, source_target_pairs={{0,4},{1,9},{2,6},{3,11},{8,0},{9,17},{10,2},{11,19},{16,8},{17,25... | collective-permute-start | bytes 786440 | tf_op jit(solution)/shard_map/ppermute | solution.py:234
  157.9 8.9 %collective-permute-start.27 = (bf16[128,1024]{0,1:T(8,128)(2,1)S(1)}, bf16[128,1024]{0,1:T(8,128)(2,1)S(1)}, u32[]{:S(2)}, u32[]{:S(2)}) collective-permute-start(bf16[128,1024]{0,1:T(8,128)(2,1)S(1)} %add_convert_fusion.9), channel_id=1, source_target_pairs={{0,8},{1,5},{2,10},{3,7},{8,16},{9,1},{10,18},{11,3},{16,24},{17,9... | collective-permute-start | bytes 786440 | tf_op jit(solution)/shard_map/ppermute | solution.py:234
  162.9 8.1 %collective-permute-start.25 = (bf16[8,64,512]{2,1,0:T(8,128)(2,1)S(1)}, bf16[8,64,512]{2,1,0:T(8,128)(2,1)S(1)}, u32[]{:S(2)}, u32[]{:S(2)}) collective-permute-start(bf16[8,64,512]{2,1,0:T(8,128)(2,1)S(1)} %maximum_select_fusion.13), channel_id=1, source_target_pairs={{0,1},{1,0},{2,3},{3,2},{4,5},{5,4},{6,7},{7,6},{8,9},{9,8},{10,11... | collective-permute-start | bytes 1572872 | tf_op jit(solution)/shard_map/ppermute | solution.py:271
  165.7 10.2 %collective-permute-start.23 = (bf16[8,64,512]{2,1,0:T(8,128)(2,1)S(1)}, bf16[8,64,512]{2,1,0:T(8,128)(2,1)S(1)}, u32[]{:S(2)}, u32[]{:S(2)}) collective-permute-start(bf16[8,64,512]{2,1,0:T(8,128)(2,1)S(1)} %maximum_select_fusion.12), channel_id=1, source_target_pairs={{0,1},{1,0},{2,3},{3,2},{4,5},{5,4},{6,7},{7,6},{8,9},{9,8},{10,11... | collective-permute-start | bytes 1572872 | tf_op jit(solution)/shard_map/ppermute | solution.py:271
  167.0 11.9 %collective-permute-start.28 = (bf16[128,1024]{0,1:T(8,128)(2,1)S(1)}, bf16[128,1024]{0,1:T(8,128)(2,1)S(1)}, u32[]{:S(2)}, u32[]{:S(2)}) collective-permute-start(bf16[128,1024]{0,1:T(8,128)(2,1)S(1)} %get-tuple-element.92), channel_id=1, source_target_pairs={{0,8},{1,5},{2,10},{3,7},{8,16},{9,1},{10,18},{11,3},{16,24},{17,9... | collective-permute-start | bytes 786440 | tf_op jit(solution)/shard_map/ppermute | solution.py:234
  171.0 7.9 %collective-permute-start.30 = (bf16[128,1024]{0,1:T(8,128)(2,1)S(1)}, bf16[128,1024]{0,1:T(8,128)(2,1)S(1)}, u32[]{:S(2)}, u32[]{:S(2)}) collective-permute-start(bf16[128,1024]{0,1:T(8,128)(2,1)S(1)} %get-tuple-element.93), channel_id=1, source_target_pairs={{0,4},{1,9},{2,6},{3,11},{8,0},{9,17},{10,2},{11,19},{16,8},{17,25... | collective-permute-start | bytes 786440 | tf_op jit(solution)/shard_map/ppermute | solution.py:234
  (36 other events, 152.1 us)

commit v6 on v5

--- a/solution.py
+++ b/solution.py
@@ -1,6 +1,8 @@
 import jax
 import jax.numpy as jnp
 from jax import lax
+from jax.experimental import pallas as pl
+from jax.experimental.pallas import tpu as pltpu
 from jax.sharding import PartitionSpec as P
 
 HEAD_DIM = 64
@@ -246,7 +248,13 @@
     return lax.dynamic_slice_in_dim(whole, owner * width, width, axis)
 
 
-def ring_step(whole, axis, core, state, step, *others):
+def ring_send(state, step):
+    near = lax.axis_size("seq") // 2 - 1
+    ahead = ring_permute(state[0], 1)
+    return ahead, ring_permute(state[1], -1) if step <= near else state[1]
+
+
+def ring_add(whole, axis, core, moved, step):
     size = lax.axis_size("seq")
     far, near = size // 2, size // 2 - 1
     f32, bf16 = jnp.float32, jnp.bfloat16
@@ -256,14 +264,20 @@
 
     if step == 0:
         return chunk(far), chunk(-near)
-    ahead = after(ring_permute(state[0], 1), *others)
+    ahead, behind = moved
     if step == far:
-        return chunk(0).astype(f32) + ahead.astype(f32) + state[1].astype(f32)
-    behind = after(ring_permute(state[1], -1), *others)
+        return chunk(0).astype(f32) + ahead.astype(f32) + behind.astype(f32)
     ahead = (ahead.astype(f32) + chunk(far - step).astype(f32)).astype(bf16)
     if step < near:
         behind = (behind.astype(f32) + chunk(step - near).astype(f32)).astype(bf16)
     return ahead, behind
+
+
+def ring_step(whole, axis, core, state, step, *others):
+    moved = None if step == 0 else ring_send(state, step)
+    if others:
+        moved = lax.optimization_barrier(moved + others)[:2]
+    return ring_add(whole, axis, core, moved, step)
 
 
 def tp_permute(values, mask):
@@ -309,6 +323,101 @@
 def from_owners(slots, share):
     later = jnp.concatenate([jnp.zeros_like(slots[:1, share:]), slots[:-1, share:]], axis=0)
     return (slots[:, :share] + later).reshape(-1, slots.shape[-1])
+
+
+def times(left, right, left_axis, right_axis):
+    return lax.dot_general(
+        left,
+        right,
+        (((left_axis,), (right_axis,)), ((), ())),
+        preferred_element_type=jnp.float32,
+    )
+
+
+def head_lanes(lanes, part):
+    return lax.broadcasted_iota(jnp.int32, (1, lanes), 1) // HEAD_DIM == part
+
+
+def forward_kernel(qkv_ref, allowed_ref, probs_ref, mixed_ref):
+    width = mixed_ref.shape[1]
+    lanes, each = 2 * HEAD_DIM, 2
+    allowed = allowed_ref[...] != 0
+    for block in range(width // lanes):
+        queries, keys, values = (
+            qkv_ref[:, c * width + block * lanes : c * width + (block + 1) * lanes]
+            for c in range(3)
+        )
+        mixed = None
+        for part in range(each):
+            mine = head_lanes(lanes, part)
+            raw = times(jnp.where(mine, queries, jnp.zeros_like(queries)), keys, 1, 1)
+            logits = jnp.where(allowed, raw * HEAD_DIM ** (-0.5), -1e30)
+            powered = jnp.exp(logits - jnp.max(logits, axis=-1, keepdims=True))
+            probs = powered / jnp.sum(powered, axis=-1, keepdims=True)
+            probs_ref[block * each + part] = probs
+            product = times(probs.astype(jnp.bfloat16), values, 1, 0)
+            mixed = product if part == 0 else jnp.where(mine, product, mixed)
+        mixed_ref[:, block * lanes : (block + 1) * lanes] = mixed.astype(jnp.bfloat16)
+
+
+def backward_kernel(qkv_ref, probs_ref, grad_ref, out_ref):
+    width = grad_ref.shape[1]
+    lanes, each = 2 * HEAD_DIM, 2
+    for block in range(width // lanes):
+        queries, keys, values = (
+            qkv_ref[:, c * width + block * lanes : c * width + (block + 1) * lanes]
+            for c in range(3)
+        )
+        grads = grad_ref[:, block * lanes : (block + 1) * lanes]
+        totals = None
+        for part in range(each):
+            mine = head_lanes(lanes, part)
+            probs = probs_ref[block * each + part]
+            grad_probs = times(jnp.where(mine, grads, jnp.zeros_like(grads)), values, 1, 1)
+            inner_sum = jnp.sum(probs * grad_probs, axis=-1, keepdims=True)
+            grad_raw = probs * (grad_probs - inner_sum) * HEAD_DIM ** (-0.5)
+            grad_raw = grad_raw.astype(jnp.bfloat16)
+            products = (
+                times(grad_raw, keys, 1, 0),
+                times(grad_raw, queries, 0, 0),
+                times(probs.astype(jnp.bfloat16), grads, 0, 0),
+            )
+            if part == 0:
+                totals = products
+            else:
+                totals = tuple(jnp.where(mine, new, old) for new, old in zip(products, totals))
+        for c in range(3):
+            first = c * width + block * lanes
+            out_ref[:, first : first + lanes] = totals[c].astype(jnp.bfloat16)
+
+
+def kernel_cost(rows, width, count):
+    return pl.CostEstimate(
+        flops=2 * count * rows * rows * width,
+        bytes_accessed=4 * rows * rows * width // HEAD_DIM + 8 * rows * width,
+        transcendentals=rows * rows * width // HEAD_DIM,
+    )
+
+
+def attend(qkv, allowed):
+    rows, width = qkv.shape[0], qkv.shape[1] // 3
+    return pl.pallas_call(
+        forward_kernel,
+        out_shape=(
+            jax.ShapeDtypeStruct((width // HEAD_DIM, rows, rows), jnp.float32),
+            jax.ShapeDtypeStruct((rows, width), jnp.bfloat16),
+        ),
+        cost_estimate=kernel_cost(rows, width, 2),
+    )(qkv, allowed)
+
+
+def attend_back(qkv, probs, grads):
+    rows, width = grads.shape
+    return pl.pallas_call(
+        backward_kernel,
+        out_shape=jax.ShapeDtypeStruct(qkv.shape, jnp.bfloat16),
+        cost_estimate=kernel_cost(rows, width, 5),
+    )(qkv, probs, grads)
 
 
 def on_device_whole(
@@ -361,11 +470,12 @@
             own = join_halves(own, tp_permute(own, 2), side)
         return join_halves(own, tp_permute(own, 1), core)
 
-    slots, seg_routed, picked_grads = lax.optimization_barrier(
+    slots, seg_routed, picked_grads, weights = lax.optimization_barrier(
         (
             exchange(pick(tokens, core * half_width, half_width)),
             seg_routed,
             pick(out_grad, core * half_width + side * quarter_width, quarter_width),
+            w_qkv.reshape(model_width, -1),
         )
     )
     routed_rows = settle(slots)
@@ -373,7 +483,7 @@
     ranks = jnp.arange(routed_len, dtype=jnp.int32)
     allowed = jnp.logical_and(
         ranks[None, :] <= ranks[:, None], seg_routed[None, :] == seg_routed[:, None]
-    )[None]
+    )
 
     rows = routed_rows.astype(f32)
     gain_first = gain_attn.astype(f32)
@@ -382,22 +492,8 @@
     gating = jax.nn.sigmoid(jnp.sum(rows * router, axis=-1, keepdims=True))
     factor_first = lax.rsqrt(jnp.mean(rows * rows, axis=-1, keepdims=True) + 1e-05)
     attn_input = (rows * factor_first * gain_first).astype(bf16)
-    weights = jnp.transpose(w_qkv, (1, 0, 2))
-    qkv = jnp.einsum("rd,cdh->crh", attn_input, weights, preferred_element_type=f32).astype(bf16)
-    head_count = qkv.shape[2] // HEAD_DIM
-    scaling = HEAD_DIM ** (-0.5)
-
-    def heads(values):
-        return values.reshape(routed_len, head_count, HEAD_DIM)
-
-    queries, keys, values = heads(qkv[0]), heads(qkv[1]), heads(qkv[2])
-    raw = jnp.einsum("qhe,khe->hqk", queries, keys, preferred_element_type=f32)
-    logits = jnp.where(allowed, raw * scaling, -1e30)
-    powered = jnp.exp(logits - jnp.max(logits, axis=-1, keepdims=True))
-    probs = powered / jnp.sum(powered, axis=-1, keepdims=True)
-    probs_low = probs.astype(bf16)
-    mixed = jnp.einsum("hqk,khe->qhe", probs_low, values, preferred_element_type=f32)
-    mixed = mixed.reshape(routed_len, -1).astype(bf16)
+    qkv = jnp.dot(attn_input, weights, preferred_element_type=f32).astype(bf16)
+    probs, mixed = attend(qkv, allowed.astype(jnp.int32))
     mixed, grad_slots = lax.optimization_barrier((mixed, exchange(picked_grads)))
     attn_half = tp_start(jnp.dot(mixed, w_out, preferred_element_type=f32), core)
     grad_rows = settle(grad_slots).astype(f32)
@@ -458,44 +554,29 @@
     grad_mixed = lax.dot_general(
         grad_attn, w_out, (((1,), (1,)), ((), ())), preferred_element_type=f32
     ).astype(bf16)
-    grad_heads = heads(grad_mixed)
-    grad_probs = jnp.einsum("qhe,khe->hqk", grad_heads, values, preferred_element_type=f32)
-    inner_sum = jnp.sum(probs * grad_probs, axis=-1, keepdims=True)
-    grad_raw = (probs * (grad_probs - inner_sum) * scaling).astype(bf16)
-    def flat(products):
-        return products.reshape(routed_len, -1).astype(bf16)
-
-    grad_query = flat(jnp.einsum("hqk,khe->qhe", grad_raw, keys, preferred_element_type=f32))
-    grad_key = flat(jnp.einsum("hqk,qhe->khe", grad_raw, queries, preferred_element_type=f32))
-    grad_value = flat(jnp.einsum("hqk,qhe->khe", probs_low, grad_heads, preferred_element_type=f32))
+    grad_parts = attend_back(qkv, probs, grad_mixed)
     mlp_ring_2 = mlp_ring(mlp_ring_1, 2)
-    grad_query, grad_key, grad_value, branch_part, mlp_ring_2 = lax.optimization_barrier(
-        (grad_query, grad_key, grad_value, branch_part, mlp_ring_2)
-    )
-    grad_parts = (grad_query, grad_key, grad_value)
+    grad_parts, branch_part = lax.optimization_barrier((grad_parts, branch_part))
     update = (gating * branch_part).astype(bf16)
     score = jnp.sum(pick_half(pick_half(grad_rows, core), side) * branch_part, axis=-1)
     score = score + tp_permute(score, 1)
     score = score + tp_permute(score, 2)
-    down_part = sum(
-        lax.dot_general(
-            grad_parts[c], weights[c], (((1,), (1,)), ((), ())), preferred_element_type=f32
-        )
-        for c in range(3)
+    down_part = lax.dot_general(
+        grad_parts, weights, (((1,), (1,)), ((), ())), preferred_element_type=f32
     )
     input_half = tp_start(down_part, core)
 
-    grad_rows_flat = jnp.concatenate(grad_parts, axis=1)
     attn_pairs = jnp.concatenate(
-        [outer(attn_input, grad_rows_flat), outer(grad_attn, mixed)], axis=1
+        [outer(attn_input, grad_parts), outer(grad_attn, mixed)], axis=1
     )
 
     def attn_ring(total, step, *others):
         return ring_step(attn_pairs, 0, core, total, step, *others)
 
     attn_ring_0 = attn_ring(None, 0)
-
-    input_half, score = lax.optimization_barrier((tp_cross(input_half), score))
+    attn_sent = ring_send(attn_ring_0, 1)
+
+    input_half, score = lax.optimization_barrier((tp_cross(input_half, *mlp_ring_2, *attn_ring_0), score))
     grad_score = gating * (1.0 - gating) * score[:, None]
     grad_attn_input = tp_join(input_half, core)
     weighted = grad_attn_input * gain_first
@@ -512,9 +593,10 @@
     grads_part = pick_half(pick_half(grad_routed_in, core), side)
     pieces = to_owners(jnp.concatenate([update, grads_part], axis=1), share)
     sent = jnp.concatenate([pieces, small], axis=1)
+    sent, *attn_sent = lax.optimization_barrier((sent,) + attn_sent)
     got = lax.all_to_all(sent, "seq", 0, 0, tiled=True)
     mlp_total = mlp_ring(mlp_ring_2, 3, sent)
-    attn_total = attn_ring(attn_ring_0, 1, sent)
+    attn_total = ring_add(attn_pairs, 0, core, attn_sent, 1)
     for step in range(4, dev_count // 2 + 1):
         mlp_total = mlp_ring(mlp_total, step)
     for step in range(2, dev_count // 2 + 1):

time: 182 us -> 170 us (0.934)
  waiting for transfers between devices: 62.7 us -> 51.9 us
  Pallas kernels: 0 us -> 6.85 us
  matrix products: 32.3 us -> 25.9 us
  starting transfers between devices: 48.5 us -> 45.8 us
  local copies, waits for them, and re-layouts: 8.6 us -> 10.5 us
    ppermute x14, waiting for transfers between devices: 27.6 us -> 20.5 us  [ring_permute(): return lax.ppermute(values, ('seq', 'tp'), pairs)]
    pallas_call x0 -> x2, Pallas kernels: none -> 6.85 us  [the longest x1 3.77 us: attend_back(): pl.pallas_call(backward_kernel, out_shape=jax.ShapeDtypeStruct(qkv.shape,...]
    dot_general x9 -> x2, matrix products: 11.1 us -> 4.53 us  [the longest x1 2.87 us: on_device_whole(): qkv = jnp.dot(attn_input, weights, preferred_element_type=f32).astype(bf16)]
    unnamed x97 -> x54, local copies, waits for them, and re-layouts: 4.45 us -> 7.03 us
    all_to_all x2, waiting for transfers between devices: 10.4 us -> 7.98 us  [exchange(): return lax.all_to_all(own, 'seq', 0, 0, tiled=True)]
    ppermute x14, starting transfers between devices: 21.8 us -> 19.7 us  [ring_permute(): return lax.ppermute(values, ('seq', 'tp'), pairs)]
    convert_element_type x6 -> x7, other arithmetic: 7.76 us -> 8.62 us  [the longest x3 6.17 us: ring_add(): behind = (behind.astype(f32) + chunk(step - near).astype(f32)).astype(bf16)]
  transfers between devices with their start and end apart: 37 -> 37, of which waited for: 18 -> 17; matrix products, arithmetic and copies ran while one was open for 29% -> 30% of each run, Pallas kernels for 0% -> 4%
where the time goes in v6:
time: 170 us; the launch traced here: 169 us
  waiting for transfers between devices  51.9 us (31%)
  starting transfers between devices  45.8 us (27%)
  other arithmetic  26.1 us (15%)
  matrix products  25.9 us (15%)
  local copies, waits for them, and re-layouts  10.5 us (6%)
  Pallas kernels  6.85 us (4%)
    ppermute x20, waiting for transfers between devices, tp_permute(): return lax.ppermute(values, 'tp', [(i, i ^ mask) for i in range(size)])  23.5 us
    ppermute x14, waiting for transfers between devices, ring_permute(): return lax.ppermute(values, ('seq', 'tp'), pairs)  20.5 us
    ppermute x14, starting transfers between devices, ring_permute(): return lax.ppermute(values, ('seq', 'tp'), pairs)  19.7 us
    ppermute x20, starting transfers between devices, tp_permute(): return lax.ppermute(values, 'tp', [(i, i ^ mask) for i in range(size)])  10.9 us
    all_to_all x2, starting transfers between devices, exchange(): return lax.all_to_all(own, 'seq', 0, 0, tiled=True)  10.9 us
    all_to_all x2, waiting for transfers between devices, exchange(): return lax.all_to_all(own, 'seq', 0, 0, tiled=True)  7.98 us
    dot_general x2, matrix products, spread(): jnp.einsum('sqc,sqd->scd', table, routed_rows, preferred_element_type=jnp...  7.87 us
    unnamed x54, local copies, waits for them, and re-layouts  7.03 us
  transfers between devices with their start and end apart: 37, of which 17 were waited for; matrix products, arithmetic and copies ran while one was open for 30% of the time, Pallas kernels for 4%

profile of v6, /device:TPU:0, one launch (start us, length us, event | category | flops | bytes accessed | tf_op | source)
XLA Modules:
  0.0 168.8 jit_solution(15297283586048081942)
XLA Ops:
  1.6 2.9 %fusion.5 = bf16[8,64,512]{2,1,0:T(8,128)(2,1)} fusion(bf16[8,256,1024]{2,1,0:T(8,128)(2,1)} %param.11, s32[]{:T(128)S(6)} %select_n.398, s32[8,64]{1,0:T(8,128)S(1)} %fusion.94), kind=kOutput, calls=%fused_computation.42 | convolution fusion | flops 134610944 | bytes 2623492 | tf_op jit(solution)/shard_map/sqc,scd->sqd/dot_general | solution.py:30
  4.5 7.3 %all-to-all-start = ((bf16[8,64,512]{2,1,0:T(8,128)(2,1)}), bf16[8,64,512]{2,1,0:T(8,128)(2,1)S(1)}, u32[]{:S(2)}, u32[]{:S(2)}) async-start(bf16[8,64,512]{2,1,0:T(8,128)(2,1)} %fusion.5), calls=%async_computation | async-start | bytes 1048576 | tf_op jit(solution)/shard_map/all_to_all | solution.py:465
  11.8 2.6 %copy.23 = bf16[1024,3,256]{0,2,1:T(8,128)(2,1)} copy(bf16[1024,3,256]{2,0,1:T(8,128)(2,1)} %param.15) | data formatting | bytes 3145728 | tf_op args[4]
  14.4 1.5 fusion.89
  15.9 2.6 %fusion.97 = s32[1,256]{1,0:T(1,128)S(1)} fusion(s32[8,256]{1,0:T(8,128)} %param.13, s32[]{:T(128)S(6)} %select_n.399, s32[]{:T(128)} %get-tuple-element.87, s32[]{:T(128)} %get-tuple-element.86, s32[]{:T(128)} %get-tuple-element.85), kind=kLoop, calls=%fused_computation.213 | loop fusion | flops 2048 | bytes 2064 | tf_op jit(solution)/shard_map/add | solution.py:456
  18.6 2.3 %convolution_convert_fusion.4 = bf16[8,64,256]{2,1,0:T(8,128)(2,1)} fusion(bf16[8,256,1024]{2,1,0:T(8,128)(2,1)} %param.21, s32[]{:T(128)S(6)} %select_n.400, s32[8,64]{1,0:T(8,128)S(1)} %fusion.94), kind=kOutput, calls=%fused_computation.47 | convolution fusion | flops 67371008 | bytes 1312772 | tf_op jit(solution)/shard_map/sqc,scd->sqd/dot_general | solution.py:30
  20.9 5.4 %all-to-all-done = bf16[8,64,512]{2,1,0:T(8,128)(2,1)S(1)} async-done(((bf16[8,64,512]{2,1,0:T(8,128)(2,1)}), bf16[8,64,512]{2,1,0:T(8,128)(2,1)S(1)}, u32[]{:S(2)}, u32[]{:S(2)}) %all-to-all-start) | async-done | bytes 524320 | tf_op jit(solution)/shard_map/all_to_all | solution.py:465
  26.5 3.6 %all-to-all-start.1 = ((bf16[8,64,256]{2,1,0:T(8,128)(2,1)}), bf16[8,64,256]{2,1,0:T(8,128)(2,1)S(1)}, u32[]{:S(2)}, u32[]{:S(2)}) async-start(bf16[8,64,256]{2,1,0:T(8,128)(2,1)} %convolution_convert_fusion.4), calls=%async_computation.1 | async-start | bytes 524288 | tf_op jit(solution)/shard_map/all_to_all | solution.py:465
  31.2 2.9 %convolution_convert_fusion.3.qkv_ref = bf16[256,768]{1,0:T(8,128)(2,1)} fusion(bf16[1024,768]{0,1:T(8,128)(2,1)} %bitcast.71, f32[1024]{0:T(1024)S(1)} %convert_element_type.349, f32[256]{0:T(256)S(1)} %get-tuple-element.110, bf16[256,512]{1,0:T(8,128)(2,1)S(1)} %collective-permute-done, bf16[256,512]{1,0:T(8,128)(2,1)S(1)} %bitcast.58, pred[]{:T(512)S(6)} %eq.114), kind=kOutput, calls=%fused_computation.43 | convolution fusion | flops 406257664 | bytes 2495489 | tf_op jit(solution)/shard_map/dot_general | solution.py:495
  34.0 3.1 %shard_map.178 = (f32[4,256,256]{2,1,0:T(8,128)}, bf16[256,256]{1,0:T(8,128)(2,1)}) custom-call(bf16[256,768]{1,0:T(8,128)(2,1)} %convolution_convert_fusion.3.qkv_ref, s32[256,256]{1,0:T(8,128)} %fusion.85.allowed_ref), custom_call_target="tpu_custom_call" | custom-call | flops 67108864 | bytes 1572864 | tf_op jit(solution)/shard_map/pallas_call | solution.py:404
  37.1 2.5 %all-to-all-done.1 = bf16[8,64,256]{2,1,0:T(8,128)(2,1)S(1)} async-done(((bf16[8,64,256]{2,1,0:T(8,128)(2,1)}), bf16[8,64,256]{2,1,0:T(8,128)(2,1)S(1)}, u32[]{:S(2)}, u32[]{:S(2)}) %all-to-all-start.1) | async-done | bytes 262176 | tf_op jit(solution)/shard_map/all_to_all | solution.py:465
  39.7 1.2 fusion.103
  41.1 1.6 collective-permute-start.4
  42.8 1.5 collective-permute-start.2
  44.2 3.2 %collective-permute-done.4 = bf16[256,256]{1,0:T(8,128)(2,1)S(1)} collective-permute-done((bf16[256,256]{1,0:T(8,128)(2,1)S(1)}, bf16[256,256]{1,0:T(8,128)(2,1)S(1)}, u32[]{:S(2)}, u32[]{:S(2)}) %collective-permute-start.4) | collective-permute-done | bytes 131104 | tf_op jit(solution)/shard_map/ppermute | solution.py:285
  48.0 4.7 %collective-permute-done.2 = bf16[256,512]{1,0:T(8,128)(2,1)} collective-permute-done((bf16[256,512]{1,0:T(8,128)(2,1)S(1)}, bf16[256,512]{1,0:T(8,128)(2,1)}, u32[]{:S(2)}, u32[]{:S(2)}) %collective-permute-start.2) | collective-permute-done | bytes 262176 | tf_op jit(solution)/shard_map/ppermute | solution.py:285
  52.7 1.1 add_convert_fusion.14
  57.5 1.3 fusion.25
  62.3 1.3 convolution_convert_fusion
  63.6 1.5 collective-permute-start.7
  65.2 1.5 collective-permute-start.11
  67.4 4.8 %collective-permute-done.7 = bf16[256,512]{1,0:T(8,128)(2,1)S(1)} collective-permute-done((bf16[256,512]{1,0:T(8,128)(2,1)S(1)}, bf16[256,512]{1,0:T(8,128)(2,1)S(1)}, u32[]{:S(2)}, u32[]{:S(2)}) %collective-permute-start.7) | collective-permute-done | bytes 262176 | tf_op jit(solution)/shard_map/ppermute | solution.py:285
  72.3 1.6 collective-permute-start.12
  73.9 6.1 %collective-permute-done.11 = bf16[2,128,1024]{2,1,0:T(8,128)(2,1)S(1)} collective-permute-done((bf16[2,128,1024]{2,1,0:T(8,128)(2,1)S(1)}, bf16[2,128,1024]{2,1,0:T(8,128)(2,1)S(1)}, u32[]{:S(2)}, u32[]{:S(2)}) %collective-permute-start.11) | collective-permute-done | bytes 524320 | tf_op jit(solution)/shard_map/ppermute | solution.py:236
  80.0 1.4 add_convert_fusion.5
  87.4 3.8 %shard_map.179 = bf16[256,768]{1,0:T(8,128)(2,1)} custom-call(bf16[256,768]{1,0:T(8,128)(2,1)} %convolution_convert_fusion.3.qkv_ref, f32[4,256,256]{2,1,0:T(8,128)} %get-tuple-element.38.probs_ref, bf16[256,256]{1,0:T(8,128)(2,1)} %convolution_convert_fusion.5.grad_ref), custom_call_target="tpu_custom_call" | custom-call | flops 167772160 | bytes 1572864 | tf_op jit(solution)/shard_map/pallas_call | solution.py:416
  91.2 1.7 fusion.106
  96.6 1.9 %collective-permute-done.18 = f32[256]{0:T(256)S(1)} collective-permute-done((f32[256]{0:T(256)S(1)}, f32[256]{0:T(256)S(1)}, u32[]{:S(2)}, u32[]{:S(2)}) %collective-permute-start.18) | collective-permute-done | bytes 1056 | tf_op jit(solution)/shard_map/ppermute | solution.py:285
  99.6 2.9 %add_convert_fusion.2 = (bf16[2,128,1024]{2,1,0:T(8,128)(2,1)}, bf16[2,128,1024]{2,1,0:T(8,128)(2,1)}) fusion(bf16[2,128,1024]{2,1,0:T(8,128)(2,1)} %collective-permute-done.16, bf16[2,1024,1024]{2,1,0:T(8,128)(2,1)} %copy-done.4, s32[]{:T(128)S(6)} %select_n.446, s32[]{:T(128)S(6)} %select_n.443, bf16[2,128,1024]{2,1,0:T(8,128)(2,1)} %collective-permute-done.15), kind=kLoop, calls=%fused_computation.93 | loop fusion | flops 2097152 | bytes 3145736 | tf_op jit(solution)/shard_map/convert_element_type | solution.py:272
  102.5 1.7 collective-permute-start.32
  104.5 2.0 %collective-permute-done.14 = bf16[256,512]{1,0:T(8,128)(2,1)S(1)} collective-permute-done((bf16[256,512]{1,0:T(8,128)(2,1)S(1)}, bf16[256,512]{1,0:T(8,128)(2,1)S(1)}, u32[]{:S(2)}, u32[]{:S(2)}) %collective-permute-start.14) | collective-permute-done | bytes 262176 | tf_op jit(solution)/shard_map/ppermute | solution.py:285
  108.6 1.2 fusion.14
  110.9 4.2 %all-to-all-start.2 = ((bf16[8,80,512]{2,1,0:T(8,128)(2,1)}), bf16[8,80,512]{2,1,0:T(8,128)(2,1)}, u32[]{:S(2)}, u32[]{:S(2)}) async-start(bf16[8,80,512]{2,1,0:T(8,128)(2,1)} %fusion.55), calls=%async_computation.2 | async-start | bytes 1310720 | tf_op jit(solution)/shard_map/all_to_all | solution.py:597
  115.1 1.3 collective-permute-done.32
  116.4 1.4 add_convert_fusion.1
  118.5 1.9 %add_convert_fusion.10 = (bf16[128,1024]{0,1:T(8,128)(2,1)S(1)}, bf16[128,1024]{0,1:T(8,128)(2,1)}) fusion(bf16[128,1024]{0,1:T(8,128)(2,1)} %collective-permute-done.21, s32[]{:T(128)S(6)} %select_n.432, bf16[1024,256]{0,1:T(8,128)(2,1)S(1)} %convolution_convert_fusion.2, bf16[1024,768]{0,1:T(8,128)(2,1)S(1)} %convolution_convert_fusion.1, ...), kind=kLoop, calls=%fused_computation.141 | loop fusion | flops 1835008 | bytes 3145736 | tf_op jit(solution)/shard_map/convert_element_type | solution.py:272
  120.4 11.8 %collective-permute-done.33 = bf16[2,128,1024]{2,1,0:T(8,128)(2,1)} collective-permute-done((bf16[2,128,1024]{2,1,0:T(8,128)(2,1)S(1)}, bf16[2,128,1024]{2,1,0:T(8,128)(2,1)}, u32[]{:S(2)}, u32[]{:S(2)}) %collective-permute-start.33) | collective-permute-done | bytes 524320 | tf_op jit(solution)/shard_map/ppermute | solution.py:236
  132.1 1.6 convert_add_fusion.2
  133.8 1.1 slice_bitcast_fusion
  134.8 2.0 %copy.27 = f32[1024,128]{1,0:T(8,128)} copy(f32[1024,128]{0,1:T(8,128)} %get-tuple-element.100) | data formatting | bytes 1048576
  136.9 4.9 %collective-permute-start.26 = (bf16[128,1024]{0,1:T(8,128)(2,1)}, bf16[128,1024]{0,1:T(8,128)(2,1)S(1)}, u32[]{:S(2)}, u32[]{:S(2)}) collective-permute-start(bf16[128,1024]{0,1:T(8,128)(2,1)} %get-tuple-element.57), channel_id=1, source_target_pairs={{0,8},{1,5},{2,10},{3,7},{8,16},{9,1},{10,18},{11,3},{16,24},{17,9... | collective-permute-start | bytes 786440 | tf_op jit(solution)/shard_map/ppermute | solution.py:236
  144.2 1.5 collective-permute-start.22
  146.1 2.6 %collective-permute-start.27 = (bf16[128,1024]{0,1:T(8,128)(2,1)S(1)}, bf16[128,1024]{0,1:T(8,128)(2,1)S(1)}, u32[]{:S(2)}, u32[]{:S(2)}) collective-permute-start(bf16[128,1024]{0,1:T(8,128)(2,1)S(1)} %add_convert_fusion.9), channel_id=1, source_target_pairs={{0,8},{1,5},{2,10},{3,7},{8,16},{9,1},{10,18},{11,3},{16,24},{17,9... | collective-permute-start | bytes 786440 | tf_op jit(solution)/shard_map/ppermute | solution.py:236
  148.8 2.2 %collective-permute-done.24 = bf16[8,64,256]{2,1,0:T(8,128)(2,1)S(1)} collective-permute-done((bf16[8,64,256]{2,1,0:T(8,128)(2,1)S(1)}, bf16[8,64,256]{2,1,0:T(8,128)(2,1)S(1)}, u32[]{:S(2)}, u32[]{:S(2)}) %collective-permute-start.24) | collective-permute-done | bytes 262176 | tf_op jit(solution)/shard_map/ppermute | solution.py:285
  151.7 2.1 %collective-permute-done.22 = bf16[8,64,256]{2,1,0:T(8,128)(2,1)S(1)} collective-permute-done((bf16[8,64,256]{2,1,0:T(8,128)(2,1)S(1)}, bf16[8,64,256]{2,1,0:T(8,128)(2,1)S(1)}, u32[]{:S(2)}, u32[]{:S(2)}) %collective-permute-start.22) | collective-permute-done | bytes 262176 | tf_op jit(solution)/shard_map/ppermute | solution.py:285
  155.2 4.0 %collective-permute-start.28 = (bf16[128,1024]{0,1:T(8,128)(2,1)S(1)}, bf16[128,1024]{0,1:T(8,128)(2,1)S(1)}, u32[]{:S(2)}, u32[]{:S(2)}) collective-permute-start(bf16[128,1024]{0,1:T(8,128)(2,1)S(1)} %get-tuple-element.94), channel_id=1, source_target_pairs={{0,8},{1,5},{2,10},{3,7},{8,16},{9,1},{10,18},{11,3},{16,24},{17,9... | collective-permute-start | bytes 786440 | tf_op jit(solution)/shard_map/ppermute | solution.py:236
  159.2 4.8 %convert_add_fusion = f32[8,256,1024]{2,1,0:T(8,128)} fusion(bf16[8,256,1024]{2,1,0:T(8,128)(2,1)S(1)} %copy-done.8, bf16[8,64,512]{2,1,0:T(8,128)(2,1)S(1)} %collective-permute-done.25, bf16[8,64,512]{2,1,0:T(8,128)(2,1)S(1)} %maximum_select_fusion.13, pred[]{:T(512)S(6)} %eq.114, s32[8,64]{1,0:T(8,128)S(1)} %fusion.94), kind=kOutput, calls=%fused_computation | convolution fusion | flops 277479424 | bytes 13633537 | tf_op jit(solution)/shard_map/sqc,sqd->scd/dot_general | solution.py:34
  164.0 3.1 %add_convert_fusion = bf16[8,256,1024]{2,1,0:T(8,128)(2,1)} fusion(bf16[8,256,1024]{2,1,0:T(8,128)(2,1)S(1)} %copy-done.7, bf16[8,64,512]{2,1,0:T(8,128)(2,1)S(1)} %collective-permute-done.23, bf16[8,64,512]{2,1,0:T(8,128)(2,1)S(1)} %maximum_select_fusion.12, pred[]{:T(512)S(6)} %eq.114, s32[8,64]{1,0:T(8,128)S(1)} %fusion.94), kind=kOutput, calls=%fused_computation.1 | convolution fusion | flops 279576576 | bytes 9439233 | tf_op jit(solution)/shard_map/sqc,sqd->scd/dot_general | solution.py:34
  (166 shorter events, 31.9 us)
Async XLA Ops:
  0.6 55.2 %copy-start = (bf16[1024,1024]{1,0:T(8,128)(2,1)S(1)}, bf16[1024,1024]{1,0:T(8,128)(2,1)}, u32[]{:S(2)}) copy-start(bf16[1024,1024]{1,0:T(8,128)(2,1)} %param.18) | copy-start | bytes 6291460
  4.5 21.8 %all-to-all-start = ((bf16[8,64,512]{2,1,0:T(8,128)(2,1)}), bf16[8,64,512]{2,1,0:T(8,128)(2,1)S(1)}, u32[]{:S(2)}, u32[]{:S(2)}) async-start(bf16[8,64,512]{2,1,0:T(8,128)(2,1)} %fusion.5), calls=%async_computation | async-start | bytes 1048576 | tf_op jit(solution)/shard_map/all_to_all | solution.py:465
  11.8 14.6 %copy-start.22 = (bf16[1024]{0:T(1024)(128)(2,1)S(1)}, bf16[1024]{0:T(1024)(128)(2,1)}, u32[]{:S(2)}) copy-start(bf16[1024]{0:T(1024)(128)(2,1)} %param.14) | copy-start | bytes 6148
  26.4 4.6 %collective-permute-start = (bf16[256,512]{1,0:T(8,128)(2,1)S(1)}, bf16[256,512]{1,0:T(8,128)(2,1)S(1)}, u32[]{:S(2)}, u32[]{:S(2)}) collective-permute-start(bf16[256,512]{1,0:T(8,128)(2,1)S(1)} %bitcast.56), channel_id=1, source_target_pairs={{0,1},{1,0},{2,3},{3,2},{4,5},{5,4},{6,7},{7,6},{8,9},{9,8},{10,11... | collective-permute-start | bytes 786440 | tf_op jit(solution)/shard_map/ppermute | solution.py:285
  26.5 13.2 %all-to-all-start.1 = ((bf16[8,64,256]{2,1,0:T(8,128)(2,1)}), bf16[8,64,256]{2,1,0:T(8,128)(2,1)S(1)}, u32[]{:S(2)}, u32[]{:S(2)}) async-start(bf16[8,64,256]{2,1,0:T(8,128)(2,1)} %convolution_convert_fusion.4), calls=%async_computation.1 | async-start | bytes 524288 | tf_op jit(solution)/shard_map/all_to_all | solution.py:465
  31.1 8.5 %copy-start.14 = (bf16[256,1024]{1,0:T(8,128)(2,1)S(1)}, bf16[256,1024]{1,0:T(8,128)(2,1)}, u32[]{:S(2)}) copy-start(bf16[256,1024]{1,0:T(8,128)(2,1)} %param.16) | copy-start | bytes 1572868
  40.9 7.0 %copy-start.23 = (bf16[1024]{0:T(1024)(128)(2,1)S(1)}, bf16[1024]{0:T(1024)(128)(2,1)}, u32[]{:S(2)}) copy-start(bf16[1024]{0:T(1024)(128)(2,1)} %param.17) | copy-start | bytes 6148
  40.9 7.0 %copy-start.24 = (bf16[1024]{0:T(1024)(128)(2,1)S(1)}, bf16[1024]{0:T(1024)(128)(2,1)}, u32[]{:S(2)}) copy-start(bf16[1024]{0:T(1024)(128)(2,1)} %param.20) | copy-start | bytes 6148
  40.9 1.7 collective-permute-start.1
  41.1 6.4 %collective-permute-start.4 = (bf16[256,256]{1,0:T(8,128)(2,1)S(1)}, bf16[256,256]{1,0:T(8,128)(2,1)S(1)}, u32[]{:S(2)}, u32[]{:S(2)}) collective-permute-start(bf16[256,256]{1,0:T(8,128)(2,1)S(1)} %bitcast.80), channel_id=1, source_target_pairs={{0,2},{1,3},{2,0},{3,1},{4,6},{5,7},{6,4},{7,5},{8,10},{9,11},{10,... | collective-permute-start | bytes 393224 | tf_op jit(solution)/shard_map/ppermute | solution.py:285
  42.8 10.0 %collective-permute-start.2 = (bf16[256,512]{1,0:T(8,128)(2,1)S(1)}, bf16[256,512]{1,0:T(8,128)(2,1)}, u32[]{:S(2)}, u32[]{:S(2)}) collective-permute-start(bf16[256,512]{1,0:T(8,128)(2,1)S(1)} %fusion.65), channel_id=1, source_target_pairs={{0,2},{1,3},{2,0},{3,1},{4,6},{5,7},{6,4},{7,5},{8,10},{9,11},{10,... | collective-permute-start | bytes 786440 | tf_op jit(solution)/shard_map/ppermute | solution.py:285
  47.6 6.3 %collective-permute-start.5 = (bf16[256,512]{1,0:T(8,128)(2,1)S(1)}, bf16[256,512]{1,0:T(8,128)(2,1)S(1)}, u32[]{:S(2)}, u32[]{:S(2)}) collective-permute-start(bf16[256,512]{1,0:T(8,128)(2,1)S(1)} %maximum_select_fusion.14), channel_id=1, source_target_pairs={{0,1},{1,0},{2,3},{3,2},{4,5},{5,4},{6,7},{7,6},{8,9},{9,8},{10,11... | collective-permute-start | bytes 786440 | tf_op jit(solution)/shard_map/ppermute | solution.py:285
  53.8 1.6 collective-permute-start.3
  55.4 29.2 %copy-start.5 = (bf16[256,512]{1,0:T(8,128)(2,1)}, bf16[256,512]{1,0:T(8,128)(2,1)S(1)}, u32[]{:S(2)}) copy-start(bf16[256,512]{1,0:T(8,128)(2,1)S(1)} %collective-permute-done.3) | copy-start | bytes 786436
  59.5 1.6 collective-permute-start.6
  62.0 5.3 %collective-permute-start.8 = (bf16[256,512]{1,0:T(8,128)(2,1)S(1)}, bf16[256,512]{1,0:T(8,128)(2,1)S(1)}, u32[]{:S(2)}, u32[]{:S(2)}) collective-permute-start(bf16[256,512]{1,0:T(8,128)(2,1)S(1)} %slice_select_fusion.8), channel_id=1, source_target_pairs={{0,1},{1,0},{2,3},{3,2},{4,5},{5,4},{6,7},{7,6},{8,9},{9,8},{10,11... | collective-permute-start | bytes 786440 | tf_op jit(solution)/shard_map/ppermute | solution.py:285
  63.6 16.4 %copy-start.4 = (bf16[2,1024,1024]{2,1,0:T(8,128)(2,1)}, bf16[2,1024,1024]{2,1,0:T(8,128)(2,1)S(1)}, u32[]{:S(2)}) copy-start(bf16[2,1024,1024]{2,1,0:T(8,128)(2,1)S(1)} %convolution_convert_fusion) | copy-start | bytes 12582916
  63.6 8.6 %collective-permute-start.7 = (bf16[256,512]{1,0:T(8,128)(2,1)S(1)}, bf16[256,512]{1,0:T(8,128)(2,1)S(1)}, u32[]{:S(2)}, u32[]{:S(2)}) collective-permute-start(bf16[256,512]{1,0:T(8,128)(2,1)S(1)} %fusion.63), channel_id=1, source_target_pairs={{0,2},{1,3},{2,0},{3,1},{4,6},{5,7},{6,4},{7,5},{8,10},{9,11},{10,... | collective-permute-start | bytes 786440 | tf_op jit(solution)/shard_map/ppermute | solution.py:285
  65.2 14.8 %collective-permute-start.11 = (bf16[2,128,1024]{2,1,0:T(8,128)(2,1)S(1)}, bf16[2,128,1024]{2,1,0:T(8,128)(2,1)S(1)}, u32[]{:S(2)}, u32[]{:S(2)}) collective-permute-start(bf16[2,128,1024]{2,1,0:T(8,128)(2,1)S(1)} %get-tuple-element.92), channel_id=1, source_target_pairs={{0,4},{1,9},{2,6},{3,11},{8,0},{9,17},{10,2},{11,19},{16,8},{17,25... | collective-permute-start | bytes 1572872 | tf_op jit(solution)/shard_map/ppermute | solution.py:236
  66.7 13.3 %collective-permute-start.10 = (bf16[2,128,1024]{2,1,0:T(8,128)(2,1)S(1)}, bf16[2,128,1024]{2,1,0:T(8,128)(2,1)S(1)}, u32[]{:S(2)}, u32[]{:S(2)}) collective-permute-start(bf16[2,128,1024]{2,1,0:T(8,128)(2,1)S(1)} %get-tuple-element.93), channel_id=1, source_target_pairs={{0,8},{1,5},{2,10},{3,7},{8,16},{9,1},{10,18},{11,3},{16,24},{17,9... | collective-permute-start | bytes 1572872 | tf_op jit(solution)/shard_map/ppermute | solution.py:236
  72.3 11.1 %collective-permute-start.12 = (bf16[256,256]{1,0:T(8,128)(2,1)S(1)}, bf16[256,256]{1,0:T(8,128)(2,1)S(1)}, u32[]{:S(2)}, u32[]{:S(2)}) collective-permute-start(bf16[256,256]{1,0:T(8,128)(2,1)S(1)} %broadcast_select_fusion), channel_id=1, source_target_pairs={{0,2},{1,3},{2,0},{3,1},{4,6},{5,7},{6,4},{7,5},{8,10},{9,11},{10,... | collective-permute-start | bytes 393224 | tf_op jit(solution)/shard_map/ppermute | solution.py:285
  73.9 10.3 %collective-permute-start.9 = (bf16[256,512]{1,0:T(8,128)(2,1)S(1)}, bf16[256,512]{1,0:T(8,128)(2,1)S(1)}, u32[]{:S(2)}, u32[]{:S(2)}) collective-permute-start(bf16[256,512]{1,0:T(8,128)(2,1)S(1)} %add_convert_fusion.13), channel_id=1, source_target_pairs={{0,1},{1,0},{2,3},{3,2},{4,5},{5,4},{6,7},{7,6},{8,9},{9,8},{10,11... | collective-permute-start | bytes 786440 | tf_op jit(solution)/shard_map/ppermute | solution.py:285
  81.4 18.2 %collective-permute-start.16 = (bf16[2,128,1024]{2,1,0:T(8,128)(2,1)}, bf16[2,128,1024]{2,1,0:T(8,128)(2,1)}, u32[]{:S(2)}, u32[]{:S(2)}) collective-permute-start(bf16[2,128,1024]{2,1,0:T(8,128)(2,1)} %get-tuple-element.90), channel_id=1, source_target_pairs={{0,4},{1,9},{2,6},{3,11},{8,0},{9,17},{10,2},{11,19},{16,8},{17,25... | collective-permute-start | bytes 1572872 | tf_op jit(solution)/shard_map/ppermute | solution.py:236
  82.3 17.3 %collective-permute-start.15 = (bf16[2,128,1024]{2,1,0:T(8,128)(2,1)}, bf16[2,128,1024]{2,1,0:T(8,128)(2,1)}, u32[]{:S(2)}, u32[]{:S(2)}) collective-permute-start(bf16[2,128,1024]{2,1,0:T(8,128)(2,1)} %get-tuple-element.91), channel_id=1, source_target_pairs={{0,8},{1,5},{2,10},{3,7},{8,16},{9,1},{10,18},{11,3},{16,24},{17,9... | collective-permute-start | bytes 1572872 | tf_op jit(solution)/shard_map/ppermute | solution.py:236
  93.1 1.7 collective-permute-start.17
  93.2 5.6 %collective-permute-start.13 = (bf16[256,512]{1,0:T(8,128)(2,1)S(1)}, bf16[256,512]{1,0:T(8,128)(2,1)S(1)}, u32[]{:S(2)}, u32[]{:S(2)}) collective-permute-start(bf16[256,512]{1,0:T(8,128)(2,1)S(1)} %slice_select_fusion.7), channel_id=1, source_target_pairs={{0,1},{1,0},{2,3},{3,2},{4,5},{5,4},{6,7},{7,6},{8,9},{9,8},{10,11... | collective-permute-start | bytes 786440 | tf_op jit(solution)/shard_map/ppermute | solution.py:285
  94.5 60.5 %copy-start.2 = (bf16[1024,768]{0,1:T(8,128)(2,1)}, bf16[1024,768]{0,1:T(8,128)(2,1)S(1)}, u32[]{:S(2)}) copy-start(bf16[1024,768]{0,1:T(8,128)(2,1)S(1)} %convolution_convert_fusion.1) | copy-start | bytes 4718596
  94.8 3.6 %collective-permute-start.18 = (f32[256]{0:T(256)S(1)}, f32[256]{0:T(256)S(1)}, u32[]{:S(2)}, u32[]{:S(2)}) collective-permute-start(f32[256]{0:T(256)S(1)} %add.377), channel_id=1, source_target_pairs={{0,2},{1,3},{2,0},{3,1},{4,6},{5,7},{6,4},{7,5},{8,10},{9,11},{10,... | collective-permute-start | bytes 3080 | tf_op jit(solution)/shard_map/ppermute | solution.py:285
  95.6 15.3 %collective-permute-start.21 = (bf16[128,1024]{0,1:T(8,128)(2,1)S(1)}, bf16[128,1024]{0,1:T(8,128)(2,1)}, u32[]{:S(2)}, u32[]{:S(2)}) collective-permute-start(bf16[128,1024]{0,1:T(8,128)(2,1)S(1)} %get-tuple-element.98), channel_id=1, source_target_pairs={{0,4},{1,9},{2,6},{3,11},{8,0},{9,17},{10,2},{11,19},{16,8},{17,25... | collective-permute-start | bytes 786440 | tf_op jit(solution)/shard_map/ppermute | solution.py:236
  98.5 12.4 %collective-permute-start.20 = (bf16[128,1024]{0,1:T(8,128)(2,1)S(1)}, bf16[128,1024]{0,1:T(8,128)(2,1)}, u32[]{:S(2)}, u32[]{:S(2)}) collective-permute-start(bf16[128,1024]{0,1:T(8,128)(2,1)S(1)} %get-tuple-element.99), channel_id=1, source_target_pairs={{0,8},{1,5},{2,10},{3,7},{8,16},{9,1},{10,18},{11,3},{16,24},{17,9... | collective-permute-start | bytes 786440 | tf_op jit(solution)/shard_map/ppermute | solution.py:236
  99.0 7.7 %copy-start.6 = (bf16[256,512]{1,0:T(8,128)(2,1)S(1)}, bf16[256,512]{1,0:T(8,128)(2,1)}, u32[]{:S(2)}) copy-start(bf16[256,512]{1,0:T(8,128)(2,1)} %copy-done.5) | copy-start | bytes 786436
  99.0 7.7 %copy-start.13 = (bf16[256,512]{1,0:T(8,128)(2,1)S(1)}, bf16[256,512]{1,0:T(8,128)(2,1)}, u32[]{:S(2)}) copy-start(bf16[256,512]{1,0:T(8,128)(2,1)} %copy-done.12) | copy-start | bytes 786436
  99.0 7.5 %collective-permute-start.14 = (bf16[256,512]{1,0:T(8,128)(2,1)S(1)}, bf16[256,512]{1,0:T(8,128)(2,1)S(1)}, u32[]{:S(2)}, u32[]{:S(2)}) collective-permute-start(bf16[256,512]{1,0:T(8,128)(2,1)S(1)} %fusion.59), channel_id=1, source_target_pairs={{0,2},{1,3},{2,0},{3,1},{4,6},{5,7},{6,4},{7,5},{8,10},{9,11},{10,... | collective-permute-start | bytes 786440 | tf_op jit(solution)/shard_map/ppermute | solution.py:285
  102.5 13.9 %collective-permute-start.32 = (bf16[2,128,1024]{2,1,0:T(8,128)(2,1)}, bf16[2,128,1024]{2,1,0:T(8,128)(2,1)}, u32[]{:S(2)}, u32[]{:S(2)}) collective-permute-start(bf16[2,128,1024]{2,1,0:T(8,128)(2,1)} %get-tuple-element.88), channel_id=1, source_target_pairs={{0,4},{1,9},{2,6},{3,11},{8,0},{9,17},{10,2},{11,19},{16,8},{17,25... | collective-permute-start | bytes 1572872 | tf_op jit(solution)/shard_map/ppermute | solution.py:236
  104.2 12.2 %collective-permute-start.31 = (bf16[2,128,1024]{2,1,0:T(8,128)(2,1)}, bf16[2,128,1024]{2,1,0:T(8,128)(2,1)}, u32[]{:S(2)}, u32[]{:S(2)}) collective-permute-start(bf16[2,128,1024]{2,1,0:T(8,128)(2,1)} %get-tuple-element.89), channel_id=1, source_target_pairs={{0,8},{1,5},{2,10},{3,7},{8,16},{9,1},{10,18},{11,3},{16,24},{17,9... | collective-permute-start | bytes 1572872 | tf_op jit(solution)/shard_map/ppermute | solution.py:236
  106.6 1.6 collective-permute-start.19
  110.9 26.0 %all-to-all-start.2 = ((bf16[8,80,512]{2,1,0:T(8,128)(2,1)}), bf16[8,80,512]{2,1,0:T(8,128)(2,1)}, u32[]{:S(2)}, u32[]{:S(2)}) async-start(bf16[8,80,512]{2,1,0:T(8,128)(2,1)} %fusion.55), calls=%async_computation.2 | async-start | bytes 1310720 | tf_op jit(solution)/shard_map/all_to_all | solution.py:597
  117.8 14.3 %collective-permute-start.33 = (bf16[2,128,1024]{2,1,0:T(8,128)(2,1)S(1)}, bf16[2,128,1024]{2,1,0:T(8,128)(2,1)}, u32[]{:S(2)}, u32[]{:S(2)}) collective-permute-start(bf16[2,128,1024]{2,1,0:T(8,128)(2,1)S(1)} %add_convert_fusion.1), channel_id=1, source_target_pairs={{0,8},{1,5},{2,10},{3,7},{8,16},{9,1},{10,18},{11,3},{16,24},{17,9... | collective-permute-start | bytes 1572872 | tf_op jit(solution)/shard_map/ppermute | solution.py:236
  136.9 9.1 %collective-permute-start.26 = (bf16[128,1024]{0,1:T(8,128)(2,1)}, bf16[128,1024]{0,1:T(8,128)(2,1)S(1)}, u32[]{:S(2)}, u32[]{:S(2)}) collective-permute-start(bf16[128,1024]{0,1:T(8,128)(2,1)} %get-tuple-element.57), channel_id=1, source_target_pairs={{0,8},{1,5},{2,10},{3,7},{8,16},{9,1},{10,18},{11,3},{16,24},{17,9... | collective-permute-start | bytes 786440 | tf_op jit(solution)/shard_map/ppermute | solution.py:236
  142.9 8.0 %collective-permute-start.24 = (bf16[8,64,256]{2,1,0:T(8,128)(2,1)S(1)}, bf16[8,64,256]{2,1,0:T(8,128)(2,1)S(1)}, u32[]{:S(2)}, u32[]{:S(2)}) collective-permute-start(bf16[8,64,256]{2,1,0:T(8,128)(2,1)S(1)} %get-tuple-element.102), channel_id=1, source_target_pairs={{0,2},{1,3},{2,0},{3,1},{4,6},{5,7},{6,4},{7,5},{8,10},{9,11},{10,... | collective-permute-start | bytes 786440 | tf_op jit(solution)/shard_map/ppermute | solution.py:285
  144.2 9.5 %collective-permute-start.22 = (bf16[8,64,256]{2,1,0:T(8,128)(2,1)S(1)}, bf16[8,64,256]{2,1,0:T(8,128)(2,1)S(1)}, u32[]{:S(2)}, u32[]{:S(2)}) collective-permute-start(bf16[8,64,256]{2,1,0:T(8,128)(2,1)S(1)} %get-tuple-element.103), channel_id=1, source_target_pairs={{0,2},{1,3},{2,0},{3,1},{4,6},{5,7},{6,4},{7,5},{8,10},{9,11},{10,... | collective-permute-start | bytes 786440 | tf_op jit(solution)/shard_map/ppermute | solution.py:285
  145.8 9.2 %collective-permute-start.29 = (bf16[128,1024]{0,1:T(8,128)(2,1)S(1)}, bf16[128,1024]{0,1:T(8,128)(2,1)S(1)}, u32[]{:S(2)}, u32[]{:S(2)}) collective-permute-start(bf16[128,1024]{0,1:T(8,128)(2,1)S(1)} %get-tuple-element.58), channel_id=1, source_target_pairs={{0,4},{1,9},{2,6},{3,11},{8,0},{9,17},{10,2},{11,19},{16,8},{17,25... | collective-permute-start | bytes 786440 | tf_op jit(solution)/shard_map/ppermute | solution.py:236
  146.1 8.9 %collective-permute-start.27 = (bf16[128,1024]{0,1:T(8,128)(2,1)S(1)}, bf16[128,1024]{0,1:T(8,128)(2,1)S(1)}, u32[]{:S(2)}, u32[]{:S(2)}) collective-permute-start(bf16[128,1024]{0,1:T(8,128)(2,1)S(1)} %add_convert_fusion.9), channel_id=1, source_target_pairs={{0,8},{1,5},{2,10},{3,7},{8,16},{9,1},{10,18},{11,3},{16,24},{17,9... | collective-permute-start | bytes 786440 | tf_op jit(solution)/shard_map/ppermute | solution.py:236
  151.1 8.1 %collective-permute-start.25 = (bf16[8,64,512]{2,1,0:T(8,128)(2,1)S(1)}, bf16[8,64,512]{2,1,0:T(8,128)(2,1)S(1)}, u32[]{:S(2)}, u32[]{:S(2)}) collective-permute-start(bf16[8,64,512]{2,1,0:T(8,128)(2,1)S(1)} %maximum_select_fusion.13), channel_id=1, source_target_pairs={{0,1},{1,0},{2,3},{3,2},{4,5},{5,4},{6,7},{7,6},{8,9},{9,8},{10,11... | collective-permute-start | bytes 1572872 | tf_op jit(solution)/shard_map/ppermute | solution.py:285
  151.7 7.5 %copy-start.8 = (bf16[8,256,1024]{2,1,0:T(8,128)(2,1)S(1)}, bf16[8,256,1024]{2,1,0:T(8,128)(2,1)}, u32[]{:S(2)}) copy-start(bf16[8,256,1024]{2,1,0:T(8,128)(2,1)} %param.21) | copy-start | bytes 12582916
  153.9 10.2 %collective-permute-start.23 = (bf16[8,64,512]{2,1,0:T(8,128)(2,1)S(1)}, bf16[8,64,512]{2,1,0:T(8,128)(2,1)S(1)}, u32[]{:S(2)}, u32[]{:S(2)}) collective-permute-start(bf16[8,64,512]{2,1,0:T(8,128)(2,1)S(1)} %maximum_select_fusion.12), channel_id=1, source_target_pairs={{0,1},{1,0},{2,3},{3,2},{4,5},{5,4},{6,7},{7,6},{8,9},{9,8},{10,11... | collective-permute-start | bytes 1572872 | tf_op jit(solution)/shard_map/ppermute | solution.py:285
  155.2 11.9 %collective-permute-start.28 = (bf16[128,1024]{0,1:T(8,128)(2,1)S(1)}, bf16[128,1024]{0,1:T(8,128)(2,1)S(1)}, u32[]{:S(2)}, u32[]{:S(2)}) collective-permute-start(bf16[128,1024]{0,1:T(8,128)(2,1)S(1)} %get-tuple-element.94), channel_id=1, source_target_pairs={{0,8},{1,5},{2,10},{3,7},{8,16},{9,1},{10,18},{11,3},{16,24},{17,9... | collective-permute-start | bytes 786440 | tf_op jit(solution)/shard_map/ppermute | solution.py:236
  159.2 7.9 %collective-permute-start.30 = (bf16[128,1024]{0,1:T(8,128)(2,1)S(1)}, bf16[128,1024]{0,1:T(8,128)(2,1)S(1)}, u32[]{:S(2)}, u32[]{:S(2)}) collective-permute-start(bf16[128,1024]{0,1:T(8,128)(2,1)S(1)} %get-tuple-element.95), channel_id=1, source_target_pairs={{0,4},{1,9},{2,6},{3,11},{8,0},{9,17},{10,2},{11,19},{16,8},{17,25... | collective-permute-start | bytes 786440 | tf_op jit(solution)/shard_map/ppermute | solution.py:236
  (14 other events, 37.5 us)

commit v7 on v6

--- a/solution.py
+++ b/solution.py
@@ -491,7 +491,7 @@
     router = w_router.astype(f32)
     gating = jax.nn.sigmoid(jnp.sum(rows * router, axis=-1, keepdims=True))
     factor_first = lax.rsqrt(jnp.mean(rows * rows, axis=-1, keepdims=True) + 1e-05)
-    attn_input = (rows * factor_first * gain_first).astype(bf16)
+    attn_input = after((rows * factor_first * gain_first).astype(bf16))
     qkv = jnp.dot(attn_input, weights, preferred_element_type=f32).astype(bf16)
     probs, mixed = attend(qkv, allowed.astype(jnp.int32))
     mixed, grad_slots = lax.optimization_barrier((mixed, exchange(picked_grads)))

time: 170 us -> 170 us (level)
    unnamed x54 -> x58, local copies, waits for them, and re-layouts: 7.03 us -> 8.22 us
  transfers between devices with their start and end apart: 37 -> 37, of which waited for: 17 -> 18; matrix products, arithmetic and copies ran while one was open for 30% -> 29% of each run, Pallas kernels for 4% -> 4%
where the time goes in v7:
time: 170 us; the launch traced here: 169 us
  waiting for transfers between devices  50.9 us (30%)
  starting transfers between devices  46.3 us (27%)
  other arithmetic  26.3 us (15%)
  matrix products  25.7 us (15%)
  local copies, waits for them, and re-layouts  11.7 us (7%)
  Pallas kernels  6.85 us (4%)
    ppermute x20, waiting for transfers between devices, tp_permute(): return lax.ppermute(values, 'tp', [(i, i ^ mask) for i in range(size)])  23.4 us
    ppermute x14, waiting for transfers between devices, ring_permute(): return lax.ppermute(values, ('seq', 'tp'), pairs)  20.4 us
    ppermute x14, starting transfers between devices, ring_permute(): return lax.ppermute(values, ('seq', 'tp'), pairs)  20.3 us
    all_to_all x2, starting transfers between devices, exchange(): return lax.all_to_all(own, 'seq', 0, 0, tiled=True)  10.9 us
    ppermute x20, starting transfers between devices, tp_permute(): return lax.ppermute(values, 'tp', [(i, i ^ mask) for i in range(size)])  10.9 us
    unnamed x58, local copies, waits for them, and re-layouts  8.22 us
    dot_general x2, matrix products, spread(): jnp.einsum('sqc,sqd->scd', table, routed_rows, preferred_element_type=jnp...  7.87 us
    all_to_all x2, waiting for transfers between devices, exchange(): return lax.all_to_all(own, 'seq', 0, 0, tiled=True)  7.1 us
  transfers between devices with their start and end apart: 37, of which 18 were waited for; matrix products, arithmetic and copies ran while one was open for 29% of the time, Pallas kernels for 4%

profile of v7, /device:TPU:0, one launch (start us, length us, event | category | flops | bytes accessed | tf_op | source)
XLA Modules:
  0.0 169.5 jit_solution(11129091578045912397)
XLA Ops:
  1.6 2.9 %fusion.5 = bf16[8,64,512]{2,1,0:T(8,128)(2,1)} fusion(bf16[8,256,1024]{2,1,0:T(8,128)(2,1)} %param.11, s32[]{:T(128)S(6)} %select_n.398, s32[8,64]{1,0:T(8,128)S(1)} %fusion.92), kind=kOutput, calls=%fused_computation.42 | convolution fusion | flops 134610944 | bytes 2623492 | tf_op jit(solution)/shard_map/sqc,scd->sqd/dot_general | solution.py:30
  4.5 7.3 %all-to-all-start = ((bf16[8,64,512]{2,1,0:T(8,128)(2,1)}), bf16[8,64,512]{2,1,0:T(8,128)(2,1)S(1)}, u32[]{:S(2)}, u32[]{:S(2)}) async-start(bf16[8,64,512]{2,1,0:T(8,128)(2,1)} %fusion.5), calls=%async_computation | async-start | bytes 1048576 | tf_op jit(solution)/shard_map/all_to_all | solution.py:465
  11.8 2.6 %copy.23 = bf16[1024,3,256]{0,2,1:T(8,128)(2,1)} copy(bf16[1024,3,256]{2,0,1:T(8,128)(2,1)} %param.15) | data formatting | bytes 3145728 | tf_op args[4]
  14.4 1.5 fusion.87
  15.9 2.6 %fusion.95 = s32[1,256]{1,0:T(1,128)S(1)} fusion(s32[8,256]{1,0:T(8,128)} %param.13, s32[]{:T(128)S(6)} %select_n.399, s32[]{:T(128)} %get-tuple-element.87, s32[]{:T(128)} %get-tuple-element.86, s32[]{:T(128)} %get-tuple-element.85), kind=kLoop, calls=%fused_computation.213 | loop fusion | flops 2048 | bytes 2064 | tf_op jit(solution)/shard_map/add | solution.py:456
  18.6 2.3 %convolution_convert_fusion.4 = bf16[8,64,256]{2,1,0:T(8,128)(2,1)} fusion(bf16[8,256,1024]{2,1,0:T(8,128)(2,1)} %param.21, s32[]{:T(128)S(6)} %select_n.400, s32[8,64]{1,0:T(8,128)S(1)} %fusion.92), kind=kOutput, calls=%fused_computation.47 | convolution fusion | flops 67371008 | bytes 1312772 | tf_op jit(solution)/shard_map/sqc,scd->sqd/dot_general | solution.py:30
  20.9 5.4 %all-to-all-done = bf16[8,64,512]{2,1,0:T(8,128)(2,1)S(1)} async-done(((bf16[8,64,512]{2,1,0:T(8,128)(2,1)}), bf16[8,64,512]{2,1,0:T(8,128)(2,1)S(1)}, u32[]{:S(2)}, u32[]{:S(2)}) %all-to-all-start) | async-done | bytes 524320 | tf_op jit(solution)/shard_map/all_to_all | solution.py:465
  26.5 3.6 %all-to-all-start.1 = ((bf16[8,64,256]{2,1,0:T(8,128)(2,1)}), bf16[8,64,256]{2,1,0:T(8,128)(2,1)S(1)}, u32[]{:S(2)}, u32[]{:S(2)}) async-start(bf16[8,64,256]{2,1,0:T(8,128)(2,1)} %convolution_convert_fusion.4), calls=%async_computation.1 | async-start | bytes 524288 | tf_op jit(solution)/shard_map/all_to_all | solution.py:465
  32.1 2.8 %convolution_convert_fusion.3.qkv_ref = bf16[256,768]{1,0:T(8,128)(2,1)} fusion(bf16[256,1024]{1,0:T(8,128)(2,1)S(1)} %fusion.29, bf16[1024,768]{0,1:T(8,128)(2,1)} %bitcast.72), kind=kOutput, calls=%fused_computation.43 | convolution fusion | flops 402849792 | bytes 2490368 | tf_op jit(solution)/shard_map/dot_general | solution.py:495
  34.9 3.1 %shard_map.178 = (f32[4,256,256]{2,1,0:T(8,128)}, bf16[256,256]{1,0:T(8,128)(2,1)}) custom-call(bf16[256,768]{1,0:T(8,128)(2,1)} %convolution_convert_fusion.3.qkv_ref, s32[256,256]{1,0:T(8,128)} %fusion.85.allowed_ref), custom_call_target="tpu_custom_call" | custom-call | flops 67108864 | bytes 1572864 | tf_op jit(solution)/shard_map/pallas_call | solution.py:404
  38.0 1.7 all-to-all-done.1
  39.7 1.2 fusion.101
  41.1 1.6 collective-permute-start.4
  42.8 1.5 collective-permute-start.2
  44.2 3.2 %collective-permute-done.4 = bf16[256,256]{1,0:T(8,128)(2,1)S(1)} collective-permute-done((bf16[256,256]{1,0:T(8,128)(2,1)S(1)}, bf16[256,256]{1,0:T(8,128)(2,1)S(1)}, u32[]{:S(2)}, u32[]{:S(2)}) %collective-permute-start.4) | collective-permute-done | bytes 131104 | tf_op jit(solution)/shard_map/ppermute | solution.py:285
  48.0 4.7 %collective-permute-done.2 = bf16[256,512]{1,0:T(8,128)(2,1)} collective-permute-done((bf16[256,512]{1,0:T(8,128)(2,1)S(1)}, bf16[256,512]{1,0:T(8,128)(2,1)}, u32[]{:S(2)}, u32[]{:S(2)}) %collective-permute-start.2) | collective-permute-done | bytes 262176 | tf_op jit(solution)/shard_map/ppermute | solution.py:285
  52.7 1.1 add_convert_fusion.14
  57.5 1.3 fusion.25
  62.3 1.3 convolution_convert_fusion
  63.6 1.5 collective-permute-start.7
  65.2 1.5 collective-permute-start.11
  67.4 4.8 %collective-permute-done.7 = bf16[256,512]{1,0:T(8,128)(2,1)S(1)} collective-permute-done((bf16[256,512]{1,0:T(8,128)(2,1)S(1)}, bf16[256,512]{1,0:T(8,128)(2,1)S(1)}, u32[]{:S(2)}, u32[]{:S(2)}) %collective-permute-start.7) | collective-permute-done | bytes 262176 | tf_op jit(solution)/shard_map/ppermute | solution.py:285
  72.3 1.6 collective-permute-start.12
  73.9 6.1 %collective-permute-done.11 = bf16[2,128,1024]{2,1,0:T(8,128)(2,1)S(1)} collective-permute-done((bf16[2,128,1024]{2,1,0:T(8,128)(2,1)S(1)}, bf16[2,128,1024]{2,1,0:T(8,128)(2,1)S(1)}, u32[]{:S(2)}, u32[]{:S(2)}) %collective-permute-start.11) | collective-permute-done | bytes 524320 | tf_op jit(solution)/shard_map/ppermute | solution.py:236
  80.0 1.4 add_convert_fusion.5
  87.5 3.8 %shard_map.179 = bf16[256,768]{1,0:T(8,128)(2,1)} custom-call(bf16[256,768]{1,0:T(8,128)(2,1)} %convolution_convert_fusion.3.qkv_ref, f32[4,256,256]{2,1,0:T(8,128)} %get-tuple-element.38.probs_ref, bf16[256,256]{1,0:T(8,128)(2,1)} %convolution_convert_fusion.5.grad_ref), custom_call_target="tpu_custom_call" | custom-call | flops 167772160 | bytes 1572864 | tf_op jit(solution)/shard_map/pallas_call | solution.py:416
  91.3 1.6 fusion.104
  97.2 1.9 %collective-permute-done.18 = f32[256]{0:T(256)S(1)} collective-permute-done((f32[256]{0:T(256)S(1)}, f32[256]{0:T(256)S(1)}, u32[]{:S(2)}, u32[]{:S(2)}) %collective-permute-start.18) | collective-permute-done | bytes 1056 | tf_op jit(solution)/shard_map/ppermute | solution.py:285
  100.6 2.9 %add_convert_fusion.2 = (bf16[2,128,1024]{2,1,0:T(8,128)(2,1)}, bf16[2,128,1024]{2,1,0:T(8,128)(2,1)}) fusion(bf16[2,128,1024]{2,1,0:T(8,128)(2,1)} %collective-permute-done.16, bf16[2,1024,1024]{2,1,0:T(8,128)(2,1)} %copy-done.4, s32[]{:T(128)S(6)} %select_n.446, s32[]{:T(128)S(6)} %select_n.443, bf16[2,128,1024]{2,1,0:T(8,128)(2,1)} %collective-permute-done.15), kind=kLoop, calls=%fused_computation.93 | loop fusion | flops 2097152 | bytes 3145736 | tf_op jit(solution)/shard_map/convert_element_type | solution.py:272
  103.5 1.3 collective-permute-start.32
  105.5 1.7 collective-permute-done.14
  109.3 1.2 fusion.14
  111.6 4.2 %all-to-all-start.2 = ((bf16[8,80,512]{2,1,0:T(8,128)(2,1)}), bf16[8,80,512]{2,1,0:T(8,128)(2,1)}, u32[]{:S(2)}, u32[]{:S(2)}) async-start(bf16[8,80,512]{2,1,0:T(8,128)(2,1)} %fusion.55), calls=%async_computation.2 | async-start | bytes 1310720 | tf_op jit(solution)/shard_map/all_to_all | solution.py:597
  115.8 1.3 collective-permute-done.32
  117.1 1.4 add_convert_fusion.1
  119.3 1.9 %add_convert_fusion.10 = (bf16[128,1024]{0,1:T(8,128)(2,1)S(1)}, bf16[128,1024]{0,1:T(8,128)(2,1)}) fusion(bf16[128,1024]{0,1:T(8,128)(2,1)} %collective-permute-done.21, s32[]{:T(128)S(6)} %select_n.432, bf16[1024,256]{0,1:T(8,128)(2,1)S(1)} %convolution_convert_fusion.2, bf16[1024,768]{0,1:T(8,128)(2,1)S(1)} %convolution_convert_fusion.1, ...), kind=kLoop, calls=%fused_computation.141 | loop fusion | flops 1835008 | bytes 3145736 | tf_op jit(solution)/shard_map/convert_element_type | solution.py:272
  121.2 11.6 %collective-permute-done.33 = bf16[2,128,1024]{2,1,0:T(8,128)(2,1)} collective-permute-done((bf16[2,128,1024]{2,1,0:T(8,128)(2,1)S(1)}, bf16[2,128,1024]{2,1,0:T(8,128)(2,1)}, u32[]{:S(2)}, u32[]{:S(2)}) %collective-permute-start.33) | collective-permute-done | bytes 524320 | tf_op jit(solution)/shard_map/ppermute | solution.py:236
  132.8 1.6 convert_add_fusion.2
  134.4 1.1 slice_bitcast_fusion
  135.5 2.0 %copy.27 = f32[1024,128]{1,0:T(8,128)} copy(f32[1024,128]{0,1:T(8,128)} %get-tuple-element.100) | data formatting | bytes 1048576
  137.5 4.9 %collective-permute-start.26 = (bf16[128,1024]{0,1:T(8,128)(2,1)}, bf16[128,1024]{0,1:T(8,128)(2,1)S(1)}, u32[]{:S(2)}, u32[]{:S(2)}) collective-permute-start(bf16[128,1024]{0,1:T(8,128)(2,1)} %get-tuple-element.57), channel_id=1, source_target_pairs={{0,8},{1,5},{2,10},{3,7},{8,16},{9,1},{10,18},{11,3},{16,24},{17,9... | collective-permute-start | bytes 786440 | tf_op jit(solution)/shard_map/ppermute | solution.py:236
  144.9 1.5 collective-permute-start.22
  146.8 2.6 %collective-permute-start.27 = (bf16[128,1024]{0,1:T(8,128)(2,1)S(1)}, bf16[128,1024]{0,1:T(8,128)(2,1)S(1)}, u32[]{:S(2)}, u32[]{:S(2)}) collective-permute-start(bf16[128,1024]{0,1:T(8,128)(2,1)S(1)} %add_convert_fusion.9), channel_id=1, source_target_pairs={{0,8},{1,5},{2,10},{3,7},{8,16},{9,1},{10,18},{11,3},{16,24},{17,9... | collective-permute-start | bytes 786440 | tf_op jit(solution)/shard_map/ppermute | solution.py:236
  149.4 2.2 %collective-permute-done.24 = bf16[8,64,256]{2,1,0:T(8,128)(2,1)S(1)} collective-permute-done((bf16[8,64,256]{2,1,0:T(8,128)(2,1)S(1)}, bf16[8,64,256]{2,1,0:T(8,128)(2,1)S(1)}, u32[]{:S(2)}, u32[]{:S(2)}) %collective-permute-start.24) | collective-permute-done | bytes 262176 | tf_op jit(solution)/shard_map/ppermute | solution.py:285
  152.3 2.1 %collective-permute-done.22 = bf16[8,64,256]{2,1,0:T(8,128)(2,1)S(1)} collective-permute-done((bf16[8,64,256]{2,1,0:T(8,128)(2,1)S(1)}, bf16[8,64,256]{2,1,0:T(8,128)(2,1)S(1)}, u32[]{:S(2)}, u32[]{:S(2)}) %collective-permute-start.22) | collective-permute-done | bytes 262176 | tf_op jit(solution)/shard_map/ppermute | solution.py:285
  155.8 4.0 %collective-permute-start.28 = (bf16[128,1024]{0,1:T(8,128)(2,1)S(1)}, bf16[128,1024]{0,1:T(8,128)(2,1)S(1)}, u32[]{:S(2)}, u32[]{:S(2)}) collective-permute-start(bf16[128,1024]{0,1:T(8,128)(2,1)S(1)} %get-tuple-element.94), channel_id=1, source_target_pairs={{0,8},{1,5},{2,10},{3,7},{8,16},{9,1},{10,18},{11,3},{16,24},{17,9... | collective-permute-start | bytes 786440 | tf_op jit(solution)/shard_map/ppermute | solution.py:236
  159.9 4.8 %convert_add_fusion = f32[8,256,1024]{2,1,0:T(8,128)} fusion(bf16[8,256,1024]{2,1,0:T(8,128)(2,1)S(1)} %copy-done.8, bf16[8,64,512]{2,1,0:T(8,128)(2,1)S(1)} %collective-permute-done.25, bf16[8,64,512]{2,1,0:T(8,128)(2,1)S(1)} %maximum_select_fusion.13, pred[]{:T(512)S(6)} %eq.114, s32[8,64]{1,0:T(8,128)S(1)} %fusion.92), kind=kOutput, calls=%fused_computation | convolution fusion | flops 277479424 | bytes 13633537 | tf_op jit(solution)/shard_map/sqc,sqd->scd/dot_general | solution.py:34
  164.7 3.1 %add_convert_fusion = bf16[8,256,1024]{2,1,0:T(8,128)(2,1)} fusion(bf16[8,256,1024]{2,1,0:T(8,128)(2,1)S(1)} %copy-done.7, bf16[8,64,512]{2,1,0:T(8,128)(2,1)S(1)} %collective-permute-done.23, bf16[8,64,512]{2,1,0:T(8,128)(2,1)S(1)} %maximum_select_fusion.12, pred[]{:T(512)S(6)} %eq.114, s32[8,64]{1,0:T(8,128)S(1)} %fusion.92), kind=kOutput, calls=%fused_computation.1 | convolution fusion | flops 279576576 | bytes 9439233 | tf_op jit(solution)/shard_map/sqc,sqd->scd/dot_general | solution.py:34
  (171 shorter events, 34.4 us)
Async XLA Ops:
  0.6 55.2 %copy-start = (bf16[1024,1024]{1,0:T(8,128)(2,1)S(1)}, bf16[1024,1024]{1,0:T(8,128)(2,1)}, u32[]{:S(2)}) copy-start(bf16[1024,1024]{1,0:T(8,128)(2,1)} %param.18) | copy-start | bytes 6291460
  4.5 21.8 %all-to-all-start = ((bf16[8,64,512]{2,1,0:T(8,128)(2,1)}), bf16[8,64,512]{2,1,0:T(8,128)(2,1)S(1)}, u32[]{:S(2)}, u32[]{:S(2)}) async-start(bf16[8,64,512]{2,1,0:T(8,128)(2,1)} %fusion.5), calls=%async_computation | async-start | bytes 1048576 | tf_op jit(solution)/shard_map/all_to_all | solution.py:465
  11.8 14.6 %copy-start.24 = (bf16[1024]{0:T(1024)(128)(2,1)S(1)}, bf16[1024]{0:T(1024)(128)(2,1)}, u32[]{:S(2)}) copy-start(bf16[1024]{0:T(1024)(128)(2,1)} %param.14) | copy-start | bytes 6148
  26.4 4.6 %collective-permute-start = (bf16[256,512]{1,0:T(8,128)(2,1)S(1)}, bf16[256,512]{1,0:T(8,128)(2,1)S(1)}, u32[]{:S(2)}, u32[]{:S(2)}) collective-permute-start(bf16[256,512]{1,0:T(8,128)(2,1)S(1)} %bitcast.58), channel_id=1, source_target_pairs={{0,1},{1,0},{2,3},{3,2},{4,5},{5,4},{6,7},{7,6},{8,9},{9,8},{10,11... | collective-permute-start | bytes 786440 | tf_op jit(solution)/shard_map/ppermute | solution.py:285
  26.5 13.2 %all-to-all-start.1 = ((bf16[8,64,256]{2,1,0:T(8,128)(2,1)}), bf16[8,64,256]{2,1,0:T(8,128)(2,1)S(1)}, u32[]{:S(2)}, u32[]{:S(2)}) async-start(bf16[8,64,256]{2,1,0:T(8,128)(2,1)} %convolution_convert_fusion.4), calls=%async_computation.1 | async-start | bytes 524288 | tf_op jit(solution)/shard_map/all_to_all | solution.py:465
  31.1 8.5 %copy-start.15 = (bf16[256,1024]{1,0:T(8,128)(2,1)S(1)}, bf16[256,1024]{1,0:T(8,128)(2,1)}, u32[]{:S(2)}) copy-start(bf16[256,1024]{1,0:T(8,128)(2,1)} %param.16) | copy-start | bytes 1572868
  40.9 7.0 %copy-start.25 = (bf16[1024]{0:T(1024)(128)(2,1)S(1)}, bf16[1024]{0:T(1024)(128)(2,1)}, u32[]{:S(2)}) copy-start(bf16[1024]{0:T(1024)(128)(2,1)} %param.17) | copy-start | bytes 6148
  40.9 7.0 %copy-start.26 = (bf16[1024]{0:T(1024)(128)(2,1)S(1)}, bf16[1024]{0:T(1024)(128)(2,1)}, u32[]{:S(2)}) copy-start(bf16[1024]{0:T(1024)(128)(2,1)} %param.20) | copy-start | bytes 6148
  40.9 1.7 collective-permute-start.1
  41.1 6.4 %collective-permute-start.4 = (bf16[256,256]{1,0:T(8,128)(2,1)S(1)}, bf16[256,256]{1,0:T(8,128)(2,1)S(1)}, u32[]{:S(2)}, u32[]{:S(2)}) collective-permute-start(bf16[256,256]{1,0:T(8,128)(2,1)S(1)} %bitcast.81), channel_id=1, source_target_pairs={{0,2},{1,3},{2,0},{3,1},{4,6},{5,7},{6,4},{7,5},{8,10},{9,11},{10,... | collective-permute-start | bytes 393224 | tf_op jit(solution)/shard_map/ppermute | solution.py:285
  42.8 10.0 %collective-permute-start.2 = (bf16[256,512]{1,0:T(8,128)(2,1)S(1)}, bf16[256,512]{1,0:T(8,128)(2,1)}, u32[]{:S(2)}, u32[]{:S(2)}) collective-permute-start(bf16[256,512]{1,0:T(8,128)(2,1)S(1)} %fusion.65), channel_id=1, source_target_pairs={{0,2},{1,3},{2,0},{3,1},{4,6},{5,7},{6,4},{7,5},{8,10},{9,11},{10,... | collective-permute-start | bytes 786440 | tf_op jit(solution)/shard_map/ppermute | solution.py:285
  47.6 6.3 %collective-permute-start.5 = (bf16[256,512]{1,0:T(8,128)(2,1)S(1)}, bf16[256,512]{1,0:T(8,128)(2,1)S(1)}, u32[]{:S(2)}, u32[]{:S(2)}) collective-permute-start(bf16[256,512]{1,0:T(8,128)(2,1)S(1)} %maximum_select_fusion.14), channel_id=1, source_target_pairs={{0,1},{1,0},{2,3},{3,2},{4,5},{5,4},{6,7},{7,6},{8,9},{9,8},{10,11... | collective-permute-start | bytes 786440 | tf_op jit(solution)/shard_map/ppermute | solution.py:285
  53.8 1.6 collective-permute-start.3
  55.4 29.2 %copy-start.5 = (bf16[256,512]{1,0:T(8,128)(2,1)}, bf16[256,512]{1,0:T(8,128)(2,1)S(1)}, u32[]{:S(2)}) copy-start(bf16[256,512]{1,0:T(8,128)(2,1)S(1)} %collective-permute-done.3) | copy-start | bytes 786436
  59.5 1.6 collective-permute-start.6
  62.0 5.3 %collective-permute-start.8 = (bf16[256,512]{1,0:T(8,128)(2,1)S(1)}, bf16[256,512]{1,0:T(8,128)(2,1)S(1)}, u32[]{:S(2)}, u32[]{:S(2)}) collective-permute-start(bf16[256,512]{1,0:T(8,128)(2,1)S(1)} %slice_select_fusion.8), channel_id=1, source_target_pairs={{0,1},{1,0},{2,3},{3,2},{4,5},{5,4},{6,7},{7,6},{8,9},{9,8},{10,11... | collective-permute-start | bytes 786440 | tf_op jit(solution)/shard_map/ppermute | solution.py:285
  63.6 16.4 %copy-start.4 = (bf16[2,1024,1024]{2,1,0:T(8,128)(2,1)}, bf16[2,1024,1024]{2,1,0:T(8,128)(2,1)S(1)}, u32[]{:S(2)}) copy-start(bf16[2,1024,1024]{2,1,0:T(8,128)(2,1)S(1)} %convolution_convert_fusion) | copy-start | bytes 12582916
  63.6 8.6 %collective-permute-start.7 = (bf16[256,512]{1,0:T(8,128)(2,1)S(1)}, bf16[256,512]{1,0:T(8,128)(2,1)S(1)}, u32[]{:S(2)}, u32[]{:S(2)}) collective-permute-start(bf16[256,512]{1,0:T(8,128)(2,1)S(1)} %fusion.63), channel_id=1, source_target_pairs={{0,2},{1,3},{2,0},{3,1},{4,6},{5,7},{6,4},{7,5},{8,10},{9,11},{10,... | collective-permute-start | bytes 786440 | tf_op jit(solution)/shard_map/ppermute | solution.py:285
  65.2 14.8 %collective-permute-start.11 = (bf16[2,128,1024]{2,1,0:T(8,128)(2,1)S(1)}, bf16[2,128,1024]{2,1,0:T(8,128)(2,1)S(1)}, u32[]{:S(2)}, u32[]{:S(2)}) collective-permute-start(bf16[2,128,1024]{2,1,0:T(8,128)(2,1)S(1)} %get-tuple-element.92), channel_id=1, source_target_pairs={{0,4},{1,9},{2,6},{3,11},{8,0},{9,17},{10,2},{11,19},{16,8},{17,25... | collective-permute-start | bytes 1572872 | tf_op jit(solution)/shard_map/ppermute | solution.py:236
  66.7 13.3 %collective-permute-start.10 = (bf16[2,128,1024]{2,1,0:T(8,128)(2,1)S(1)}, bf16[2,128,1024]{2,1,0:T(8,128)(2,1)S(1)}, u32[]{:S(2)}, u32[]{:S(2)}) collective-permute-start(bf16[2,128,1024]{2,1,0:T(8,128)(2,1)S(1)} %get-tuple-element.93), channel_id=1, source_target_pairs={{0,8},{1,5},{2,10},{3,7},{8,16},{9,1},{10,18},{11,3},{16,24},{17,9... | collective-permute-start | bytes 1572872 | tf_op jit(solution)/shard_map/ppermute | solution.py:236
  72.3 11.1 %collective-permute-start.12 = (bf16[256,256]{1,0:T(8,128)(2,1)S(1)}, bf16[256,256]{1,0:T(8,128)(2,1)S(1)}, u32[]{:S(2)}, u32[]{:S(2)}) collective-permute-start(bf16[256,256]{1,0:T(8,128)(2,1)S(1)} %broadcast_select_fusion), channel_id=1, source_target_pairs={{0,2},{1,3},{2,0},{3,1},{4,6},{5,7},{6,4},{7,5},{8,10},{9,11},{10,... | collective-permute-start | bytes 393224 | tf_op jit(solution)/shard_map/ppermute | solution.py:285
  73.9 10.4 %collective-permute-start.9 = (bf16[256,512]{1,0:T(8,128)(2,1)S(1)}, bf16[256,512]{1,0:T(8,128)(2,1)S(1)}, u32[]{:S(2)}, u32[]{:S(2)}) collective-permute-start(bf16[256,512]{1,0:T(8,128)(2,1)S(1)} %add_convert_fusion.13), channel_id=1, source_target_pairs={{0,1},{1,0},{2,3},{3,2},{4,5},{5,4},{6,7},{7,6},{8,9},{9,8},{10,11... | collective-permute-start | bytes 786440 | tf_op jit(solution)/shard_map/ppermute | solution.py:285
  81.4 19.2 %collective-permute-start.16 = (bf16[2,128,1024]{2,1,0:T(8,128)(2,1)}, bf16[2,128,1024]{2,1,0:T(8,128)(2,1)}, u32[]{:S(2)}, u32[]{:S(2)}) collective-permute-start(bf16[2,128,1024]{2,1,0:T(8,128)(2,1)} %get-tuple-element.90), channel_id=1, source_target_pairs={{0,4},{1,9},{2,6},{3,11},{8,0},{9,17},{10,2},{11,19},{16,8},{17,25... | collective-permute-start | bytes 1572872 | tf_op jit(solution)/shard_map/ppermute | solution.py:236
  82.3 18.2 %collective-permute-start.15 = (bf16[2,128,1024]{2,1,0:T(8,128)(2,1)}, bf16[2,128,1024]{2,1,0:T(8,128)(2,1)}, u32[]{:S(2)}, u32[]{:S(2)}) collective-permute-start(bf16[2,128,1024]{2,1,0:T(8,128)(2,1)} %get-tuple-element.91), channel_id=1, source_target_pairs={{0,8},{1,5},{2,10},{3,7},{8,16},{9,1},{10,18},{11,3},{16,24},{17,9... | collective-permute-start | bytes 1572872 | tf_op jit(solution)/shard_map/ppermute | solution.py:236
  93.6 62.0 %copy-start.2 = (bf16[1024,768]{0,1:T(8,128)(2,1)}, bf16[1024,768]{0,1:T(8,128)(2,1)S(1)}, u32[]{:S(2)}) copy-start(bf16[1024,768]{0,1:T(8,128)(2,1)S(1)} %convolution_convert_fusion.1) | copy-start | bytes 4718596
  94.2 1.2 collective-permute-start.17
  94.3 5.5 %collective-permute-start.13 = (bf16[256,512]{1,0:T(8,128)(2,1)S(1)}, bf16[256,512]{1,0:T(8,128)(2,1)S(1)}, u32[]{:S(2)}, u32[]{:S(2)}) collective-permute-start(bf16[256,512]{1,0:T(8,128)(2,1)S(1)} %slice_select_fusion.7), channel_id=1, source_target_pairs={{0,1},{1,0},{2,3},{3,2},{4,5},{5,4},{6,7},{7,6},{8,9},{9,8},{10,11... | collective-permute-start | bytes 786440 | tf_op jit(solution)/shard_map/ppermute | solution.py:285
  95.5 3.6 %collective-permute-start.18 = (f32[256]{0:T(256)S(1)}, f32[256]{0:T(256)S(1)}, u32[]{:S(2)}, u32[]{:S(2)}) collective-permute-start(f32[256]{0:T(256)S(1)} %add.377), channel_id=1, source_target_pairs={{0,2},{1,3},{2,0},{3,1},{4,6},{5,7},{6,4},{7,5},{8,10},{9,11},{10,... | collective-permute-start | bytes 3080 | tf_op jit(solution)/shard_map/ppermute | solution.py:285
  96.1 15.4 %collective-permute-start.21 = (bf16[128,1024]{0,1:T(8,128)(2,1)S(1)}, bf16[128,1024]{0,1:T(8,128)(2,1)}, u32[]{:S(2)}, u32[]{:S(2)}) collective-permute-start(bf16[128,1024]{0,1:T(8,128)(2,1)S(1)} %get-tuple-element.98), channel_id=1, source_target_pairs={{0,4},{1,9},{2,6},{3,11},{8,0},{9,17},{10,2},{11,19},{16,8},{17,25... | collective-permute-start | bytes 786440 | tf_op jit(solution)/shard_map/ppermute | solution.py:236
  99.0 12.5 %collective-permute-start.20 = (bf16[128,1024]{0,1:T(8,128)(2,1)S(1)}, bf16[128,1024]{0,1:T(8,128)(2,1)}, u32[]{:S(2)}, u32[]{:S(2)}) collective-permute-start(bf16[128,1024]{0,1:T(8,128)(2,1)S(1)} %get-tuple-element.99), channel_id=1, source_target_pairs={{0,8},{1,5},{2,10},{3,7},{8,16},{9,1},{10,18},{11,3},{16,24},{17,9... | collective-permute-start | bytes 786440 | tf_op jit(solution)/shard_map/ppermute | solution.py:236
  100.0 7.4 %copy-start.6 = (bf16[256,512]{1,0:T(8,128)(2,1)S(1)}, bf16[256,512]{1,0:T(8,128)(2,1)}, u32[]{:S(2)}) copy-start(bf16[256,512]{1,0:T(8,128)(2,1)} %copy-done.5) | copy-start | bytes 786436
  100.0 7.4 %copy-start.13 = (bf16[256,512]{1,0:T(8,128)(2,1)S(1)}, bf16[256,512]{1,0:T(8,128)(2,1)}, u32[]{:S(2)}) copy-start(bf16[256,512]{1,0:T(8,128)(2,1)} %copy-done.12) | copy-start | bytes 786436
  100.0 7.2 %collective-permute-start.14 = (bf16[256,512]{1,0:T(8,128)(2,1)S(1)}, bf16[256,512]{1,0:T(8,128)(2,1)S(1)}, u32[]{:S(2)}, u32[]{:S(2)}) collective-permute-start(bf16[256,512]{1,0:T(8,128)(2,1)S(1)} %fusion.59), channel_id=1, source_target_pairs={{0,2},{1,3},{2,0},{3,1},{4,6},{5,7},{6,4},{7,5},{8,10},{9,11},{10,... | collective-permute-start | bytes 786440 | tf_op jit(solution)/shard_map/ppermute | solution.py:285
  103.5 13.6 %collective-permute-start.32 = (bf16[2,128,1024]{2,1,0:T(8,128)(2,1)}, bf16[2,128,1024]{2,1,0:T(8,128)(2,1)}, u32[]{:S(2)}, u32[]{:S(2)}) collective-permute-start(bf16[2,128,1024]{2,1,0:T(8,128)(2,1)} %get-tuple-element.88), channel_id=1, source_target_pairs={{0,4},{1,9},{2,6},{3,11},{8,0},{9,17},{10,2},{11,19},{16,8},{17,25... | collective-permute-start | bytes 1572872 | tf_op jit(solution)/shard_map/ppermute | solution.py:236
  104.8 12.3 %collective-permute-start.31 = (bf16[2,128,1024]{2,1,0:T(8,128)(2,1)}, bf16[2,128,1024]{2,1,0:T(8,128)(2,1)}, u32[]{:S(2)}, u32[]{:S(2)}) collective-permute-start(bf16[2,128,1024]{2,1,0:T(8,128)(2,1)} %get-tuple-element.89), channel_id=1, source_target_pairs={{0,8},{1,5},{2,10},{3,7},{8,16},{9,1},{10,18},{11,3},{16,24},{17,9... | collective-permute-start | bytes 1572872 | tf_op jit(solution)/shard_map/ppermute | solution.py:236
  107.3 1.6 collective-permute-start.19
  111.6 26.0 %all-to-all-start.2 = ((bf16[8,80,512]{2,1,0:T(8,128)(2,1)}), bf16[8,80,512]{2,1,0:T(8,128)(2,1)}, u32[]{:S(2)}, u32[]{:S(2)}) async-start(bf16[8,80,512]{2,1,0:T(8,128)(2,1)} %fusion.55), calls=%async_computation.2 | async-start | bytes 1310720 | tf_op jit(solution)/shard_map/all_to_all | solution.py:597
  118.5 14.3 %collective-permute-start.33 = (bf16[2,128,1024]{2,1,0:T(8,128)(2,1)S(1)}, bf16[2,128,1024]{2,1,0:T(8,128)(2,1)}, u32[]{:S(2)}, u32[]{:S(2)}) collective-permute-start(bf16[2,128,1024]{2,1,0:T(8,128)(2,1)S(1)} %add_convert_fusion.1), channel_id=1, source_target_pairs={{0,8},{1,5},{2,10},{3,7},{8,16},{9,1},{10,18},{11,3},{16,24},{17,9... | collective-permute-start | bytes 1572872 | tf_op jit(solution)/shard_map/ppermute | solution.py:236
  137.5 9.1 %collective-permute-start.26 = (bf16[128,1024]{0,1:T(8,128)(2,1)}, bf16[128,1024]{0,1:T(8,128)(2,1)S(1)}, u32[]{:S(2)}, u32[]{:S(2)}) collective-permute-start(bf16[128,1024]{0,1:T(8,128)(2,1)} %get-tuple-element.57), channel_id=1, source_target_pairs={{0,8},{1,5},{2,10},{3,7},{8,16},{9,1},{10,18},{11,3},{16,24},{17,9... | collective-permute-start | bytes 786440 | tf_op jit(solution)/shard_map/ppermute | solution.py:236
  143.6 8.0 %collective-permute-start.24 = (bf16[8,64,256]{2,1,0:T(8,128)(2,1)S(1)}, bf16[8,64,256]{2,1,0:T(8,128)(2,1)S(1)}, u32[]{:S(2)}, u32[]{:S(2)}) collective-permute-start(bf16[8,64,256]{2,1,0:T(8,128)(2,1)S(1)} %get-tuple-element.102), channel_id=1, source_target_pairs={{0,2},{1,3},{2,0},{3,1},{4,6},{5,7},{6,4},{7,5},{8,10},{9,11},{10,... | collective-permute-start | bytes 786440 | tf_op jit(solution)/shard_map/ppermute | solution.py:285
  144.9 9.5 %collective-permute-start.22 = (bf16[8,64,256]{2,1,0:T(8,128)(2,1)S(1)}, bf16[8,64,256]{2,1,0:T(8,128)(2,1)S(1)}, u32[]{:S(2)}, u32[]{:S(2)}) collective-permute-start(bf16[8,64,256]{2,1,0:T(8,128)(2,1)S(1)} %get-tuple-element.103), channel_id=1, source_target_pairs={{0,2},{1,3},{2,0},{3,1},{4,6},{5,7},{6,4},{7,5},{8,10},{9,11},{10,... | collective-permute-start | bytes 786440 | tf_op jit(solution)/shard_map/ppermute | solution.py:285
  146.4 9.2 %collective-permute-start.29 = (bf16[128,1024]{0,1:T(8,128)(2,1)S(1)}, bf16[128,1024]{0,1:T(8,128)(2,1)S(1)}, u32[]{:S(2)}, u32[]{:S(2)}) collective-permute-start(bf16[128,1024]{0,1:T(8,128)(2,1)S(1)} %get-tuple-element.58), channel_id=1, source_target_pairs={{0,4},{1,9},{2,6},{3,11},{8,0},{9,17},{10,2},{11,19},{16,8},{17,25... | collective-permute-start | bytes 786440 | tf_op jit(solution)/shard_map/ppermute | solution.py:236
  146.8 8.9 %collective-permute-start.27 = (bf16[128,1024]{0,1:T(8,128)(2,1)S(1)}, bf16[128,1024]{0,1:T(8,128)(2,1)S(1)}, u32[]{:S(2)}, u32[]{:S(2)}) collective-permute-start(bf16[128,1024]{0,1:T(8,128)(2,1)S(1)} %add_convert_fusion.9), channel_id=1, source_target_pairs={{0,8},{1,5},{2,10},{3,7},{8,16},{9,1},{10,18},{11,3},{16,24},{17,9... | collective-permute-start | bytes 786440 | tf_op jit(solution)/shard_map/ppermute | solution.py:236
  151.7 8.1 %collective-permute-start.25 = (bf16[8,64,512]{2,1,0:T(8,128)(2,1)S(1)}, bf16[8,64,512]{2,1,0:T(8,128)(2,1)S(1)}, u32[]{:S(2)}, u32[]{:S(2)}) collective-permute-start(bf16[8,64,512]{2,1,0:T(8,128)(2,1)S(1)} %maximum_select_fusion.13), channel_id=1, source_target_pairs={{0,1},{1,0},{2,3},{3,2},{4,5},{5,4},{6,7},{7,6},{8,9},{9,8},{10,11... | collective-permute-start | bytes 1572872 | tf_op jit(solution)/shard_map/ppermute | solution.py:285
  152.3 7.5 %copy-start.8 = (bf16[8,256,1024]{2,1,0:T(8,128)(2,1)S(1)}, bf16[8,256,1024]{2,1,0:T(8,128)(2,1)}, u32[]{:S(2)}) copy-start(bf16[8,256,1024]{2,1,0:T(8,128)(2,1)} %param.21) | copy-start | bytes 12582916
  154.5 10.2 %collective-permute-start.23 = (bf16[8,64,512]{2,1,0:T(8,128)(2,1)S(1)}, bf16[8,64,512]{2,1,0:T(8,128)(2,1)S(1)}, u32[]{:S(2)}, u32[]{:S(2)}) collective-permute-start(bf16[8,64,512]{2,1,0:T(8,128)(2,1)S(1)} %maximum_select_fusion.12), channel_id=1, source_target_pairs={{0,1},{1,0},{2,3},{3,2},{4,5},{5,4},{6,7},{7,6},{8,9},{9,8},{10,11... | collective-permute-start | bytes 1572872 | tf_op jit(solution)/shard_map/ppermute | solution.py:285
  155.8 11.9 %collective-permute-start.28 = (bf16[128,1024]{0,1:T(8,128)(2,1)S(1)}, bf16[128,1024]{0,1:T(8,128)(2,1)S(1)}, u32[]{:S(2)}, u32[]{:S(2)}) collective-permute-start(bf16[128,1024]{0,1:T(8,128)(2,1)S(1)} %get-tuple-element.94), channel_id=1, source_target_pairs={{0,8},{1,5},{2,10},{3,7},{8,16},{9,1},{10,18},{11,3},{16,24},{17,9... | collective-permute-start | bytes 786440 | tf_op jit(solution)/shard_map/ppermute | solution.py:236
  159.8 7.9 %collective-permute-start.30 = (bf16[128,1024]{0,1:T(8,128)(2,1)S(1)}, bf16[128,1024]{0,1:T(8,128)(2,1)S(1)}, u32[]{:S(2)}, u32[]{:S(2)}) collective-permute-start(bf16[128,1024]{0,1:T(8,128)(2,1)S(1)} %get-tuple-element.95), channel_id=1, source_target_pairs={{0,4},{1,9},{2,6},{3,11},{8,0},{9,17},{10,2},{11,19},{16,8},{17,25... | collective-permute-start | bytes 786440 | tf_op jit(solution)/shard_map/ppermute | solution.py:236
  (16 other events, 38.8 us)
